TPU v7x, 128 devices: a whole 4x4x4 slice. The times are simulated.
128 devices in a mesh: rows: 16 (over x, z), cols: 8 (over y, core).
Axes of the slice: x: 4, y: 4, z: 4, core: 2. Of those that a mesh axis runs over, the one named last changes fastest.
Arguments:
- offsets: float32 [65536, 2, 256], P(('rows', 'cols')), may hold values from 0 to 16
- lens_weight: float32 [65536, 256], P(('rows', 'cols')), may hold values from 0.25 to 4
- counts: int32 [65536], P(('rows', 'cols')), may hold values from 1 to 256, as said below
- owners: int32 [65536], P(('rows', 'cols')), may hold values from 0 to 127, as said below
- brick_slot: int32 [65536], P(('rows', 'cols')), may hold values from 0 to 511
Outputs:
- leaders_fine: float32 [2048, 2048], P('rows', 'cols')
- leaders_second: float32 [1024, 1024], P('rows', 'cols')
- leaders_third: float32 [512, 512], P('rows', 'cols')
- leaders_coarse: float32 [256, 256], P('rows', 'cols')
- approx_coarse: float32 [256, 256], P('rows', 'cols')
Inputs may be any that keep to these rules, and one draw needn't show every extreme that they name: `owners`: the bricks of one device name any device at most 8 times; one device, drawn from the seed, is named exactly 8 times by the bricks of every device. `counts`: each device holds a brick with exactly 256 particles.
All inputs are finite; a program needn't handle non-finite values.
Results may differ from a plain program's by a relative error of at most 0.0026.
Values sent between devices are 32-bit elements; how exact they have to be, the bound alone decides.
No kernel may reach another device: no remote copies, remote signals or barrier semaphores. Data moves between devices by JAX's collectives and lax.ppermute only.
A program may use at most 64 MiB of HBM per device.

v0:
```python
import jax
import jax.numpy as jnp
from jax import lax
from jax.sharding import PartitionSpec as P

R_DEV = 256
C_DEV = 512
LEVELS = 4


taps_low = (
    0.33267055295008263,
    0.8068915093110925,
    0.4598775021184915,
    -0.13501102001025458,
    -0.08544127388202666,
    0.03522629188570953,
)
taps_high = tuple(((-1.0) ** index * taps_low[5 - index] for index in range(6)))


def from_behind(x, axis, by):
    size = lax.axis_size(axis)
    return lax.ppermute(x, axis, [(i, (i + by) % size) for i in range(size)])


def extended_2(block, sides, width):
    for axis, dim in sides:
        count = lax.axis_size(axis)
        forward = [(i, i + 1) for i in range(count - 1)]
        forward.append((count - 1, 0))
        backward = [(target, source) for source, target in forward]
        low = lax.ppermute(
            lax.slice_in_dim(block, block.shape[dim] - width, None, axis=dim), axis, forward
        )
        high = lax.ppermute(lax.slice_in_dim(block, 0, width, axis=dim), axis, backward)
        block = jnp.concatenate([low, block, high], axis=dim)
    return block


def deposit_block(offsets, weights, counts):
    slot_count = offsets.shape[-1]
    occupied = jnp.arange(slot_count, dtype=jnp.int32)[None, :] < counts[:, None]
    scaled = jnp.where(occupied, weights, 0.0)
    centres = jnp.arange(17, dtype=jnp.float32)
    row_hat = jnp.maximum(0.0, 1.0 - jnp.abs(offsets[:, 0, None, :] - centres[None, :, None]))
    col_hat = jnp.maximum(0.0, 1.0 - jnp.abs(offsets[:, 1, None, :] - centres[None, :, None]))
    row_part = (row_hat * scaled[:, None, :]).astype(jnp.bfloat16)
    col_part = col_hat.astype(jnp.bfloat16)
    deposit = jnp.einsum("gip,gjp->gij", row_part, col_part, preferred_element_type=jnp.float32)
    flat = deposit.reshape(deposit.shape[0], 289)
    return jnp.pad(flat, ((0, 0), (0, 95)))


def deposit_groups(offsets, weights, counts, per_group):
    brick_total = offsets.shape[0]
    blocks = brick_total // per_group

    def one_group(members):
        return deposit_block(members[0], members[1], members[2])

    grouped = lax.map(
        one_group,
        (
            offsets.reshape((blocks, per_group) + offsets.shape[1:]),
            weights.reshape((blocks, per_group) + weights.shape[1:]),
            counts.reshape(blocks, per_group),
        ),
    )
    return grouped.reshape(brick_total, 384)


def deposit_arrived(items):
    offsets, weights, brick_meta = items
    devices = offsets.shape[0]
    width = offsets.shape[1]
    flat = deposit_groups(
        offsets.reshape((devices * width,) + offsets.shape[2:]),
        weights.reshape((devices * width,) + weights.shape[2:]),
        brick_meta[:, :, 1].reshape(devices * width),
        8 * width,
    )
    return (flat.reshape(devices, width, 384), brick_meta[:, :, 0])


def route_bricks(first, second, third, finish):
    result = finish(
        (
            lax.all_to_all(first, ("rows", "cols"), split_axis=0, concat_axis=0, tiled=True),
            lax.all_to_all(second, ("rows", "cols"), split_axis=0, concat_axis=0, tiled=True),
            lax.all_to_all(third, ("rows", "cols"), split_axis=0, concat_axis=0, tiled=True),
        )
    )
    return result


def slot_sources(position, devices, capacity):
    brick_total = position.shape[0]
    slot_ids = jnp.arange(devices * capacity, dtype=jnp.int32)
    matched = slot_ids[:, None] == position[None, :]
    numbered = jnp.arange(brick_total, dtype=jnp.int32)[None, :] + 1
    found = jnp.sum(jnp.where(matched, numbered, 0), axis=1)
    return jnp.where(found > 0, found - 1, brick_total)


def pack_slots(values, sources, devices, capacity):
    picked = jnp.take(values, sources, axis=0, mode="fill", fill_value=0)
    return picked.reshape((devices, capacity) + values.shape[1:])


def fold_open(values):
    spilled = values[:, 16]
    carried = jnp.concatenate([jnp.zeros_like(spilled[:1]), spilled[:-1]], axis=0)
    interior = values[:, :16].at[:, 0].add(carried)
    return (interior.reshape((values.shape[0] * 16,) + values.shape[2:]), spilled[-1])


def filter_table(length):
    half = length // 2
    inner = jnp.arange(length + 4, dtype=jnp.int32)[:, None]
    outer = jnp.arange(length, dtype=jnp.int32)[None, :]
    lag = inner - 2 * (outer % half)
    upper = outer >= half
    table = jnp.zeros((length + 4, length), jnp.float32)
    for tap_index in range(6):
        tap_value = jnp.where(upper, taps_high[tap_index], taps_low[tap_index])
        table = table + jnp.where(lag == tap_index, tap_value, 0.0)
    return table


def pool_pairs(values):
    rows_n, cols_n = values.shape
    return jnp.max(values.reshape(rows_n // 2, 2, cols_n // 2, 2), axis=(1, 3))


def neighbourhood_max(framed):
    rows_n = framed.shape[0] - 2
    cols_n = framed.shape[1] - 2
    largest = framed[1:-1, 1:-1]
    for shift_row in range(3):
        for shift_col in range(3):
            largest = jnp.maximum(
                largest, framed[shift_row : shift_row + rows_n, shift_col : shift_col + cols_n]
            )
    return largest


def on_device(offsets, lens_weight, counts, owners, brick_slot):
    devices = lax.axis_size(("rows", "cols"))
    capacity = max(2, 2 * offsets.shape[0] // devices)
    matches = (owners[:, None] == jnp.arange(devices, dtype=jnp.int32)[None, :]).astype(jnp.int32)
    ranking = jnp.sum(jnp.cumsum(matches, axis=0) * matches, axis=1) - 1
    position = owners * capacity + ranking
    sources = slot_sources(position, devices, capacity)
    brick_meta = jnp.stack([brick_slot, counts], axis=1)
    arrived, landing = route_bricks(
        pack_slots(offsets, sources, devices, capacity),
        pack_slots(lens_weight, sources, devices, capacity),
        pack_slots(brick_meta, sources, devices, capacity),
        deposit_arrived,
    )
    row_bricks = R_DEV // 16
    col_bricks = C_DEV // 16
    tile_slots = jnp.arange(row_bricks * col_bricks, dtype=jnp.int32)
    placing = (tile_slots[:, None] == landing.reshape(-1)[None, :]).astype(jnp.float32)
    brick_grid = jnp.dot(placing, arrived.reshape(-1, 384), precision=lax.Precision.HIGHEST)
    brick_grid = brick_grid[:, :289].reshape(row_bricks, col_bricks, 17, 17)
    across, col_spill = fold_open(brick_grid.transpose(1, 3, 0, 2))
    density, row_spill = fold_open(across.transpose(1, 2, 0))
    col_vec, corner = fold_open(col_spill)
    col_in, corner_in = from_behind((col_vec, corner), "cols", 1)
    density = density.at[:, 0].add(col_in)
    row_spill = row_spill.at[0].add(corner_in)
    row_in = from_behind(row_spill, "rows", 1)
    current = density.at[0].add(row_in)
    previous = None
    leader_maps = []
    for level_index in range(LEVELS):
        rows_n, cols_n = current.shape
        edge_cols = from_behind(jnp.swapaxes(current[:, :4], 0, 1), "cols", -1)
        widened = jnp.concatenate([current, jnp.swapaxes(edge_cols, 0, 1)], axis=1)
        col_done = jnp.dot(widened, filter_table(cols_n), precision=lax.Precision.HIGHEST)
        edge_rows = from_behind(col_done[:4], "rows", -1)
        extended = jnp.concatenate([col_done, edge_rows], axis=0)
        both_done = jnp.dot(filter_table(rows_n).T, extended, precision=lax.Precision.HIGHEST)
        half_rows = rows_n // 2
        half_cols = cols_n // 2
        current = both_done[:half_rows, :half_cols]
        detail_a = both_done[:half_rows, half_cols:]
        detail_b = both_done[half_rows:, :half_cols]
        detail_c = both_done[half_rows:, half_cols:]
        peak_now = jnp.maximum(jnp.maximum(jnp.abs(detail_a), jnp.abs(detail_b)), jnp.abs(detail_c))
        if previous is not None:
            peak_now = jnp.maximum(peak_now, pool_pairs(previous))
        previous = peak_now
        framed = extended_2(peak_now, (("rows", 0), ("cols", 1)), 1)
        leader_maps.append(neighbourhood_max(framed))
    return (leader_maps[0], leader_maps[1], leader_maps[2], leader_maps[3], current)


def solution(mesh):
    placed = (
        P(("rows", "cols"), None, None),
        P(("rows", "cols"), None),
        P(("rows", "cols")),
        P(("rows", "cols")),
        P(("rows", "cols")),
    )
    return jax.shard_map(
        on_device,
        mesh=mesh,
        in_specs=placed,
        out_specs=(
            P("rows", "cols"),
            P("rows", "cols"),
            P("rows", "cols"),
            P("rows", "cols"),
            P("rows", "cols"),
        ),
        check_vma=False,
    )
```

profile of v0, /device:TPU:0, one launch (start us, length us, event | category | flops | bytes accessed | tf_op | source)
XLA Modules:
  0.0 265.9 jit_solution(10804522798650307548)
XLA Ops:
  3.4 2.8 %gather_fusion = s32[1024,2]{1,0:T(8,128)S(1)} fusion(s32[512,2]{1,0:T(8,128)S(1)} %copy.98, s32[1024]{0:T(1024)S(1)} %broadcast_clamp_fusion), kind=kCustom, calls=%fused_computation | custom fusion | bytes 20480 | tf_op jit(solution)/shard_map/jit(_take)/gather | solution.py:107
  7.9 11.1 %all-to-all-start = ((s32[128,8,2]{1,2,0:T(2,128)}), s32[128,8,2]{1,2,0:T(2,128)S(1)}, u32[]{:S(2)}, u32[]{:S(2)}) async-start(s32[128,8,2]{1,2,0:T(2,128)} %broadcast_select_fusion), calls=%async_computation | async-start | bytes 262144 | tf_op jit(solution)/shard_map/all_to_all | solution.py:91
  19.0 4.1 %gather_fusion.1 = f32[1024,2,256]{2,1,0:T(2,128)S(1)} fusion(f32[512,2,256]{2,1,0:T(2,128)S(1)} %copy-done, s32[1024]{0:T(1024)S(1)} %broadcast_clamp_fusion), kind=kCustom, calls=%fused_computation.1 | custom fusion | bytes 4198400 | tf_op jit(solution)/shard_map/jit(_take)/gather | solution.py:107
  23.4 1.6 copy.101
  25.1 3.3 %all-to-all-done = s32[128,8,2]{1,2,0:T(2,128)S(1)} async-done(((s32[128,8,2]{1,2,0:T(2,128)}), s32[128,8,2]{1,2,0:T(2,128)S(1)}, u32[]{:S(2)}, u32[]{:S(2)}) %all-to-all-start) | async-done | bytes 8224 | tf_op jit(solution)/shard_map/all_to_all | solution.py:91
  28.4 7.0 %all-to-all-start.1 = ((f32[128,8,2,256]{3,1,2,0:T(8,128)}), f32[128,8,2,256]{3,1,2,0:T(8,128)}, u32[]{:S(2)}, u32[]{:S(2)}) async-start(f32[128,8,2,256]{3,1,2,0:T(8,128)} %copy.101), calls=%async_computation.1 | async-start | bytes 4194304 | tf_op jit(solution)/shard_map/all_to_all | solution.py:89
  35.4 3.5 %gather_fusion.2 = f32[1024,256]{1,0:T(8,128)S(1)} fusion(f32[512,256]{1,0:T(8,128)S(1)} %copy-done.1, s32[1024]{0:T(1024)S(1)} %broadcast_clamp_fusion), kind=kCustom, calls=%fused_computation.2 | custom fusion | bytes 2101248 | tf_op jit(solution)/shard_map/jit(_take)/gather | solution.py:107
  44.0 1.2 bitcast_select_fusion.2
  45.2 20.2 %all-to-all-done.1 = f32[128,8,2,256]{3,1,2,0:T(8,128)} async-done(((f32[128,8,2,256]{3,1,2,0:T(8,128)}), f32[128,8,2,256]{3,1,2,0:T(8,128)}, u32[]{:S(2)}, u32[]{:S(2)}) %all-to-all-start.1) | async-done | bytes 2097184 | tf_op jit(solution)/shard_map/all_to_all | solution.py:89
  65.4 4.6 %all-to-all-start.2 = ((f32[128,8,256]{2,1,0:T(8,128)}), f32[128,8,256]{2,1,0:T(8,128)S(1)}, u32[]{:S(2)}, u32[]{:S(2)}) async-start(f32[128,8,256]{2,1,0:T(8,128)} %bitcast_select_fusion.2), calls=%async_computation.2 | async-start | bytes 2097152 | tf_op jit(solution)/shard_map/all_to_all | solution.py:90
  77.2 3.1 %copy.102 = f32[128,8,2,256]{3,1,0,2:T(8,128)} copy(f32[128,8,2,256]{3,1,2,0:T(8,128)} %all-to-all-done.1) | data formatting | bytes 4194304 | tf_op jit(solution)/shard_map/all_to_all | solution.py:89
  80.3 8.9 %all-to-all-done.2 = f32[128,8,256]{2,1,0:T(8,128)S(1)} async-done(((f32[128,8,256]{2,1,0:T(8,128)}), f32[128,8,256]{2,1,0:T(8,128)S(1)}, u32[]{:S(2)}, u32[]{:S(2)}) %all-to-all-start.2) | async-done | bytes 1048608 | tf_op jit(solution)/shard_map/all_to_all | solution.py:90
  89.2 45.5 %while.18 = (s32[]{:T(128)}, f32[16,64,384]{2,1,0:T(8,128)}, f32[16,64,2,256]{3,1,0,2:T(8,128)}, s32[16,64]{1,0:T(8,128)S(1)}, f32[16,64,256]{2,1,0:T(8,128)S(1)}, /*index=5*/s32[]{:T(128)}) while((s32[]{:T(128)}, f32[16,64,384]{2,1,0:T(8,128)}, f32[16,64,2,256]{3,1,0,2:T(8,128)}, s32[16,64]{1,0:T(8,128)S(1)}, f32[16,64,256]{2,1,0:T(8,128)S(1)}, ...), condition=%wide.region_5.6_spmd, body=%wide.region_4.5_spmd.sunk | while | flops 12566530 | bytes 1788253 | solution.py:62
  89.3 0.9 dynamic-slice_bitcast_fusion.2
  134.7 3.9 %fusion.9 = f32[512,289]{0,1:T(8,128)} fusion(f32[1024,384]{1,0:T(8,128)} %bitcast.108, s32[1024]{0:T(1024)S(1)} %eq.261), kind=kOutput, calls=%fused_computation.26 | convolution fusion | flops 1818755072 | bytes 2168832 | tf_op jit(solution)/shard_map/dot_general | solution.py:166
  138.6 1.7 reshape.520
  140.2 4.3 %copy.105 = f32[16,32,17,17]{0,2,3,1:T(8,128)} copy(f32[16,32,17,17]{1,0,3,2:T(8,128)S(1)} %reshape.520) | data formatting | bytes 1183744 | tf_op jit(solution)/shard_map/reshape | solution.py:167
  146.4 1.8 slice_bitcast_fusion.2
  148.2 6.2 %slice.550 = f32[32,16,16,17]{2,3,1,0:T(8,128)} slice(f32[32,17,16,17]{2,3,1,0:T(8,128)} %bitcast.98), slice={[0:32], [0:16], [0:16], [0:17]} | slice | bytes 1114112 | tf_op jit(solution)/shard_map/slice | solution.py:114
  154.6 1.8 bitcast_dynamic-update-slice_fusion
  156.4 4.4 %copy.114 = f32[512,16,17]{0,1,2:T(8,128)S(1)} copy(f32[512,16,17]{1,2,0:T(8,128)} %bitcast.99) | data formatting | bytes 1114112 | tf_op jit(solution)/shard_map/reshape | solution.py:115
  163.3 3.5 %collective-permute-done.1 = f32[]{:T(128)} collective-permute-done((f32[]{:T(128)}, f32[]{:T(128)}, u32[]{:S(2)}, u32[]{:S(2)}) %collective-permute-start.1) | collective-permute-done | bytes 36 | tf_op jit(solution)/shard_map/ppermute | solution.py:24
  166.8 1.3 constant_dynamic-update-slice_fusion.1
  170.5 4.6 %collective-permute-done.2 = f32[512]{0:T(512)S(1)} collective-permute-done((f32[512]{0:T(512)S(1)}, f32[512]{0:T(512)S(1)}, u32[]{:S(2)}, u32[]{:S(2)}) %collective-permute-start.2) | collective-permute-done | bytes 2080 | tf_op jit(solution)/shard_map/ppermute | solution.py:24
  175.2 2.5 collective-permute-done.3
  177.9 2.1 fusion.11
  180.1 3.6 %collective-permute-done.4 = f32[4,512]{1,0:T(4,128)S(1)} collective-permute-done((f32[4,512]{1,0:T(4,128)S(1)}, f32[4,512]{1,0:T(4,128)S(1)}, u32[]{:S(2)}, u32[]{:S(2)}) %collective-permute-start.4) | collective-permute-done | bytes 8224 | tf_op jit(solution)/shard_map/ppermute | solution.py:24
  183.8 1.2 fusion.39
  185.1 5.3 %collective-permute-start.6 = (f32[1,256]{1,0:T(1,128)S(1)}, f32[1,256]{1,0:T(1,128)S(1)}, u32[]{:S(2)}, u32[]{:S(2)}) collective-permute-start(f32[1,256]{1,0:T(1,128)S(1)} %get-tuple-element.196), channel_id=1, source_target_pairs={{8,0},{16,8},{24,16},{32,24},{40,32},{48,40},{56,48},{64,56},{72,6... | collective-permute-start | bytes 3080 | tf_op jit(solution)/shard_map/ppermute | solution.py:36
  190.4 9.8 %reshape.531 = f32[64,2,128,2]{3,2,1,0:T(8,128)} reshape(f32[128,256]{1,0:T(8,128)S(1)} %get-tuple-element.188) | data formatting | bytes 262144 | tf_op jit(solution)/shard_map/reshape | solution.py:133
  200.2 1.4 collective-permute-start.9
  201.6 4.5 %reduce_max.27 = f32[64,128]{1,0:T(8,128)S(1)} reduce(f32[64,2,128,2]{3,2,1,0:T(8,128)} %reshape.531, f32[]{:T(128)} %constant.389.clone.1), dimensions={1,3}, to_apply=%region_8.9 | reduce | flops 24576 | bytes 163844 | tf_op jit(solution)/shard_map/reduce_max | solution.py:133
  206.3 2.9 %collective-permute-start.8 = (f32[130,1]{1,0:T(8,128)S(1)}, f32[130,1]{1,0:T(8,128)S(1)}, u32[]{:S(2)}, u32[]{:S(2)}) collective-permute-start(f32[130,1]{1,0:T(8,128)S(1)} %get-tuple-element.190), channel_id=1, source_target_pairs={{1,0},{2,1},{3,2},{4,3},{5,4},{6,5},{7,6},{0,7},{9,8},{10,9},{11,1... | collective-permute-start | bytes 1568 | tf_op jit(solution)/shard_map/ppermute | solution.py:36
  210.2 1.1 collective-permute-done.7
  211.4 2.1 collective-permute-done.10
  214.1 5.3 %collective-permute-start.12 = (f32[1,128]{1,0:T(1,128)S(1)}, f32[1,128]{1,0:T(1,128)S(1)}, u32[]{:S(2)}, u32[]{:S(2)}) collective-permute-start(f32[1,128]{1,0:T(1,128)S(1)} %get-tuple-element.204), channel_id=1, source_target_pairs={{8,0},{16,8},{24,16},{32,24},{40,32},{48,40},{56,48},{64,56},{72,6... | collective-permute-start | bytes 1544 | tf_op jit(solution)/shard_map/ppermute | solution.py:36
  221.0 3.0 %collective-permute-start.14 = (f32[66,1]{1,0:T(8,128)S(1)}, f32[66,1]{1,0:T(8,128)S(1)}, u32[]{:S(2)}, u32[]{:S(2)}) collective-permute-start(f32[66,1]{1,0:T(8,128)S(1)} %get-tuple-element.198), channel_id=1, source_target_pairs={{1,0},{2,1},{3,2},{4,3},{5,4},{6,5},{7,6},{0,7},{9,8},{10,9},{11,1... | collective-permute-start | bytes 800 | tf_op jit(solution)/shard_map/ppermute | solution.py:36
  224.0 2.1 reshape.532
  226.7 1.1 collective-permute-done.15
  228.0 5.4 %collective-permute-start.16 = (f32[4,128]{1,0:T(4,128)S(1)}, f32[4,128]{1,0:T(4,128)S(1)}, u32[]{:S(2)}, u32[]{:S(2)}) collective-permute-start(f32[4,128]{1,0:T(4,128)S(1)} %slice.598), channel_id=1, source_target_pairs={{0,120},{8,0},{16,8},{24,16},{32,24},{40,32},{48,40},{56,48},{64,5... | collective-permute-start | bytes 6152 | tf_op jit(solution)/shard_map/ppermute | solution.py:24
  235.5 5.7 %collective-permute-start.18 = (f32[1,64]{1,0:T(1,128)S(1)}, f32[1,64]{1,0:T(1,128)S(1)}, u32[]{:S(2)}, u32[]{:S(2)}) collective-permute-start(f32[1,64]{1,0:T(1,128)S(1)} %get-tuple-element.212), channel_id=1, source_target_pairs={{8,0},{16,8},{24,16},{32,24},{40,32},{48,40},{56,48},{64,56},{72,6... | collective-permute-start | bytes 776 | tf_op jit(solution)/shard_map/ppermute | solution.py:36
  241.7 1.5 collective-permute-start.21
  243.5 3.0 %collective-permute-start.20 = (f32[34,1]{1,0:T(8,128)S(1)}, f32[34,1]{1,0:T(8,128)S(1)}, u32[]{:S(2)}, u32[]{:S(2)}) collective-permute-start(f32[34,1]{1,0:T(8,128)S(1)} %get-tuple-element.206), channel_id=1, source_target_pairs={{1,0},{2,1},{3,2},{4,3},{5,4},{6,5},{7,6},{0,7},{9,8},{10,9},{11,1... | collective-permute-start | bytes 416 | tf_op jit(solution)/shard_map/ppermute | solution.py:36
  246.7 4.7 %collective-permute-start.22 = (f32[4,64]{1,0:T(4,128)S(1)}, f32[4,64]{1,0:T(4,128)S(1)}, u32[]{:S(2)}, u32[]{:S(2)}) collective-permute-start(f32[4,64]{1,0:T(4,128)S(1)} %slice.614), channel_id=1, source_target_pairs={{0,120},{8,0},{16,8},{24,16},{32,24},{40,32},{48,40},{56,48},{64,5... | collective-permute-start | bytes 3080 | tf_op jit(solution)/shard_map/ppermute | solution.py:24
  251.4 1.2 collective-permute-done.22
  253.5 5.6 %collective-permute-start.24 = (f32[1,32]{1,0:T(1,128)S(1)}, f32[1,32]{1,0:T(1,128)S(1)}, u32[]{:S(2)}, u32[]{:S(2)}) collective-permute-start(f32[1,32]{1,0:T(1,128)S(1)} %get-tuple-element.218), channel_id=1, source_target_pairs={{8,0},{16,8},{24,16},{32,24},{40,32},{48,40},{56,48},{64,56},{72,6... | collective-permute-start | bytes 392 | tf_op jit(solution)/shard_map/ppermute | solution.py:36
  260.7 3.0 %collective-permute-start.26 = (f32[18,1]{1,0:T(8,128)S(1)}, f32[18,1]{1,0:T(8,128)S(1)}, u32[]{:S(2)}, u32[]{:S(2)}) collective-permute-start(f32[18,1]{1,0:T(8,128)S(1)} %get-tuple-element.214), channel_id=1, source_target_pairs={{1,0},{2,1},{3,2},{4,3},{5,4},{6,5},{7,6},{0,7},{9,8},{10,9},{11,1... | collective-permute-start | bytes 224 | tf_op jit(solution)/shard_map/ppermute | solution.py:36
  263.7 1.4 collective-permute-done.25
  (384 shorter events, 78.3 us)
Async XLA Ops:
  0.6 18.4 %copy-start = (f32[512,2,256]{2,1,0:T(2,128)S(1)}, f32[512,2,256]{2,1,0:T(2,128)}, u32[]{:S(2)}) copy-start(f32[512,2,256]{2,1,0:T(2,128)} %param.19) | copy-start | bytes 3145732
  7.9 20.6 %all-to-all-start = ((s32[128,8,2]{1,2,0:T(2,128)}), s32[128,8,2]{1,2,0:T(2,128)S(1)}, u32[]{:S(2)}, u32[]{:S(2)}) async-start(s32[128,8,2]{1,2,0:T(2,128)} %broadcast_select_fusion), calls=%async_computation | async-start | bytes 262144 | tf_op jit(solution)/shard_map/all_to_all | solution.py:91
  25.1 10.3 %copy-start.1 = (f32[512,256]{1,0:T(8,128)S(1)}, f32[512,256]{1,0:T(8,128)}, u32[]{:S(2)}) copy-start(f32[512,256]{1,0:T(8,128)} %param.20) | copy-start | bytes 1572868
  28.4 37.0 %all-to-all-start.1 = ((f32[128,8,2,256]{3,1,2,0:T(8,128)}), f32[128,8,2,256]{3,1,2,0:T(8,128)}, u32[]{:S(2)}, u32[]{:S(2)}) async-start(f32[128,8,2,256]{3,1,2,0:T(8,128)} %copy.101), calls=%async_computation.1 | async-start | bytes 4194304 | tf_op jit(solution)/shard_map/all_to_all | solution.py:89
  65.4 23.8 %all-to-all-start.2 = ((f32[128,8,256]{2,1,0:T(8,128)}), f32[128,8,256]{2,1,0:T(8,128)S(1)}, u32[]{:S(2)}, u32[]{:S(2)}) async-start(f32[128,8,256]{2,1,0:T(8,128)} %bitcast_select_fusion.2), calls=%async_computation.2 | async-start | bytes 2097152 | tf_op jit(solution)/shard_map/all_to_all | solution.py:90
  161.4 16.3 %copy-start.5 = (s32[512]{0:T(512)S(1)}, s32[512]{0:T(512)}, u32[]{:S(2)}) copy-start(s32[512]{0:T(512)} %fusion.164) | copy-start | bytes 6148
  161.4 16.3 %copy-start.6 = (f32[512]{0:T(512)S(1)}, f32[512]{0:T(512)}, u32[]{:S(2)}) copy-start(f32[512]{0:T(512)} %get-tuple-element.225) | copy-start | bytes 6148
  161.5 16.3 %copy-start.7 = (f32[512]{0:T(512)S(1)}, f32[512]{0:T(512)}, u32[]{:S(2)}) copy-start(f32[512]{0:T(512)} %get-tuple-element.226) | copy-start | bytes 6148
  161.5 16.3 %copy-start.8 = (f32[512]{0:T(512)S(1)}, f32[512]{0:T(512)}, u32[]{:S(2)}) copy-start(f32[512]{0:T(512)} %get-tuple-element.223) | copy-start | bytes 6148
  161.5 16.3 %copy-start.9 = (f32[512]{0:T(512)S(1)}, f32[512]{0:T(512)}, u32[]{:S(2)}) copy-start(f32[512]{0:T(512)} %get-tuple-element.224) | copy-start | bytes 6148
  161.5 16.3 %copy-start.10 = (f32[512]{0:T(512)S(1)}, f32[512]{0:T(512)}, u32[]{:S(2)}) copy-start(f32[512]{0:T(512)} %get-tuple-element.221) | copy-start | bytes 6148
  161.5 16.3 %copy-start.11 = (f32[512]{0:T(512)S(1)}, f32[512]{0:T(512)}, u32[]{:S(2)}) copy-start(f32[512]{0:T(512)} %get-tuple-element.222) | copy-start | bytes 6148
  162.5 4.3 %collective-permute-start.1 = (f32[]{:T(128)}, f32[]{:T(128)}, u32[]{:S(2)}, u32[]{:S(2)}) collective-permute-start(f32[]{:T(128)} %bitcast.36), channel_id=1, source_target_pairs={{0,1},{1,2},{2,3},{3,4},{4,5},{5,6},{6,7},{7,0},{8,9},{9,10},{10,1... | collective-permute-start | bytes 20 | tf_op jit(solution)/shard_map/ppermute | solution.py:24
  162.5 6.5 %collective-permute-start = (f32[256]{0:T(256)S(1)}, f32[256]{0:T(256)S(1)}, u32[]{:S(2)}, u32[]{:S(2)}) collective-permute-start(f32[256]{0:T(256)S(1)} %reshape.526), channel_id=1, source_target_pairs={{0,1},{1,2},{2,3},{3,4},{4,5},{5,6},{6,7},{7,0},{8,9},{9,10},{10,1... | collective-permute-start | bytes 3080 | tf_op jit(solution)/shard_map/ppermute | solution.py:24
  168.2 7.0 %collective-permute-start.2 = (f32[512]{0:T(512)S(1)}, f32[512]{0:T(512)S(1)}, u32[]{:S(2)}, u32[]{:S(2)}) collective-permute-start(f32[512]{0:T(512)S(1)} %constant_dynamic-update-slice_fusion.1), channel_id=1, source_target_pairs={{0,8},{8,16},{16,24},{24,32},{32,40},{40,48},{48,56},{56,64},{64,7... | collective-permute-start | bytes 6152 | tf_op jit(solution)/shard_map/ppermute | solution.py:24
  175.2 2.5 collective-permute-start.3
  180.0 3.7 %collective-permute-start.4 = (f32[4,512]{1,0:T(4,128)S(1)}, f32[4,512]{1,0:T(4,128)S(1)}, u32[]{:S(2)}, u32[]{:S(2)}) collective-permute-start(f32[4,512]{1,0:T(4,128)S(1)} %slice.566), channel_id=1, source_target_pairs={{0,120},{8,0},{16,8},{24,16},{32,24},{40,32},{48,40},{56,48},{64,5... | collective-permute-start | bytes 24584 | tf_op jit(solution)/shard_map/ppermute | solution.py:24
  185.0 21.2 %collective-permute-start.5 = (f32[1,256]{1,0:T(1,128)S(1)}, f32[1,256]{1,0:T(1,128)S(1)}, u32[]{:S(2)}, u32[]{:S(2)}) collective-permute-start(f32[1,256]{1,0:T(1,128)S(1)} %get-tuple-element.195), channel_id=1, source_target_pairs={{0,8},{8,16},{16,24},{24,32},{32,40},{40,48},{48,56},{56,64},{64,7... | collective-permute-start | bytes 3080 | tf_op jit(solution)/shard_map/ppermute | solution.py:33
  185.1 21.1 %collective-permute-start.6 = (f32[1,256]{1,0:T(1,128)S(1)}, f32[1,256]{1,0:T(1,128)S(1)}, u32[]{:S(2)}, u32[]{:S(2)}) collective-permute-start(f32[1,256]{1,0:T(1,128)S(1)} %get-tuple-element.196), channel_id=1, source_target_pairs={{8,0},{16,8},{24,16},{32,24},{40,32},{48,40},{56,48},{64,56},{72,6... | collective-permute-start | bytes 3080 | tf_op jit(solution)/shard_map/ppermute | solution.py:36
  200.2 9.1 %collective-permute-start.9 = (f32[4,128]{0,1:T(8,128)S(1)}, f32[4,128]{0,1:T(8,128)S(1)}, u32[]{:S(2)}, u32[]{:S(2)}) collective-permute-start(f32[4,128]{0,1:T(8,128)S(1)} %slice_bitcast_fusion.4), channel_id=1, source_target_pairs={{0,7},{1,0},{2,1},{3,2},{4,3},{5,4},{6,5},{7,6},{8,15},{9,8},{10,9... | collective-permute-start | bytes 6152 | tf_op jit(solution)/shard_map/ppermute | solution.py:24
  206.3 5.0 %collective-permute-start.7 = (f32[130,1]{1,0:T(8,128)S(1)}, f32[130,1]{1,0:T(8,128)S(1)}, u32[]{:S(2)}, u32[]{:S(2)}) collective-permute-start(f32[130,1]{1,0:T(8,128)S(1)} %get-tuple-element.189), channel_id=1, source_target_pairs={{0,1},{1,2},{2,3},{3,4},{4,5},{5,6},{6,7},{7,0},{8,9},{9,10},{10,1... | collective-permute-start | bytes 1568 | tf_op jit(solution)/shard_map/ppermute | solution.py:33
  206.3 4.9 %collective-permute-start.8 = (f32[130,1]{1,0:T(8,128)S(1)}, f32[130,1]{1,0:T(8,128)S(1)}, u32[]{:S(2)}, u32[]{:S(2)}) collective-permute-start(f32[130,1]{1,0:T(8,128)S(1)} %get-tuple-element.190), channel_id=1, source_target_pairs={{1,0},{2,1},{3,2},{4,3},{5,4},{6,5},{7,6},{0,7},{9,8},{10,9},{11,1... | collective-permute-start | bytes 1568 | tf_op jit(solution)/shard_map/ppermute | solution.py:36
  209.8 3.7 %collective-permute-start.10 = (f32[4,256]{1,0:T(4,128)S(1)}, f32[4,256]{1,0:T(4,128)S(1)}, u32[]{:S(2)}, u32[]{:S(2)}) collective-permute-start(f32[4,256]{1,0:T(4,128)S(1)} %slice.582), channel_id=1, source_target_pairs={{0,120},{8,0},{16,8},{24,16},{32,24},{40,32},{48,40},{56,48},{64,5... | collective-permute-start | bytes 12296 | tf_op jit(solution)/shard_map/ppermute | solution.py:24
  214.0 6.9 %collective-permute-start.11 = (f32[1,128]{1,0:T(1,128)S(1)}, f32[1,128]{1,0:T(1,128)S(1)}, u32[]{:S(2)}, u32[]{:S(2)}) collective-permute-start(f32[1,128]{1,0:T(1,128)S(1)} %get-tuple-element.203), channel_id=1, source_target_pairs={{0,8},{8,16},{16,24},{24,32},{32,40},{40,48},{48,56},{56,64},{64,7... | collective-permute-start | bytes 1544 | tf_op jit(solution)/shard_map/ppermute | solution.py:33
  214.1 6.8 %collective-permute-start.12 = (f32[1,128]{1,0:T(1,128)S(1)}, f32[1,128]{1,0:T(1,128)S(1)}, u32[]{:S(2)}, u32[]{:S(2)}) collective-permute-start(f32[1,128]{1,0:T(1,128)S(1)} %get-tuple-element.204), channel_id=1, source_target_pairs={{8,0},{16,8},{24,16},{32,24},{40,32},{48,40},{56,48},{64,56},{72,6... | collective-permute-start | bytes 1544 | tf_op jit(solution)/shard_map/ppermute | solution.py:36
  221.0 5.6 %collective-permute-start.13 = (f32[66,1]{1,0:T(8,128)S(1)}, f32[66,1]{1,0:T(8,128)S(1)}, u32[]{:S(2)}, u32[]{:S(2)}) collective-permute-start(f32[66,1]{1,0:T(8,128)S(1)} %get-tuple-element.197), channel_id=1, source_target_pairs={{0,1},{1,2},{2,3},{3,4},{4,5},{5,6},{6,7},{7,0},{8,9},{9,10},{10,1... | collective-permute-start | bytes 800 | tf_op jit(solution)/shard_map/ppermute | solution.py:33
  221.0 5.6 %collective-permute-start.14 = (f32[66,1]{1,0:T(8,128)S(1)}, f32[66,1]{1,0:T(8,128)S(1)}, u32[]{:S(2)}, u32[]{:S(2)}) collective-permute-start(f32[66,1]{1,0:T(8,128)S(1)} %get-tuple-element.198), channel_id=1, source_target_pairs={{1,0},{2,1},{3,2},{4,3},{5,4},{6,5},{7,6},{0,7},{9,8},{10,9},{11,1... | collective-permute-start | bytes 800 | tf_op jit(solution)/shard_map/ppermute | solution.py:36
  226.1 8.7 %copy-start.28 = (f32[64]{0:T(128)S(1)}, f32[64]{0:T(128)}, u32[]{:S(2)}) copy-start(f32[64]{0:T(128)} %get-tuple-element.243) | copy-start | bytes 772
  226.1 8.7 %copy-start.29 = (f32[64]{0:T(128)S(1)}, f32[64]{0:T(128)}, u32[]{:S(2)}) copy-start(f32[64]{0:T(128)} %get-tuple-element.244) | copy-start | bytes 772
  226.1 8.7 %copy-start.30 = (f32[64]{0:T(128)S(1)}, f32[64]{0:T(128)}, u32[]{:S(2)}) copy-start(f32[64]{0:T(128)} %get-tuple-element.241) | copy-start | bytes 772
  226.2 1.6 collective-permute-start.15
  226.5 26.1 %copy-start.22 = (f32[32]{0:T(128)S(1)}, f32[32]{0:T(128)}, u32[]{:S(2)}) copy-start(f32[32]{0:T(128)} %get-tuple-element.249) | copy-start | bytes 388
  226.6 26.1 %copy-start.23 = (f32[32]{0:T(128)S(1)}, f32[32]{0:T(128)}, u32[]{:S(2)}) copy-start(f32[32]{0:T(128)} %get-tuple-element.250) | copy-start | bytes 388
  226.6 26.1 %copy-start.24 = (f32[32]{0:T(128)S(1)}, f32[32]{0:T(128)}, u32[]{:S(2)}) copy-start(f32[32]{0:T(128)} %get-tuple-element.247) | copy-start | bytes 388
  226.6 26.1 %copy-start.25 = (f32[32]{0:T(128)S(1)}, f32[32]{0:T(128)}, u32[]{:S(2)}) copy-start(f32[32]{0:T(128)} %get-tuple-element.248) | copy-start | bytes 388
  226.6 26.1 %copy-start.26 = (f32[32]{0:T(128)S(1)}, f32[32]{0:T(128)}, u32[]{:S(2)}) copy-start(f32[32]{0:T(128)} %get-tuple-element.245) | copy-start | bytes 388
  226.6 26.1 %copy-start.27 = (f32[32]{0:T(128)S(1)}, f32[32]{0:T(128)}, u32[]{:S(2)}) copy-start(f32[32]{0:T(128)} %get-tuple-element.246) | copy-start | bytes 388
  228.0 6.7 %collective-permute-start.16 = (f32[4,128]{1,0:T(4,128)S(1)}, f32[4,128]{1,0:T(4,128)S(1)}, u32[]{:S(2)}, u32[]{:S(2)}) collective-permute-start(f32[4,128]{1,0:T(4,128)S(1)} %slice.598), channel_id=1, source_target_pairs={{0,120},{8,0},{16,8},{24,16},{32,24},{40,32},{48,40},{56,48},{64,5... | collective-permute-start | bytes 6152 | tf_op jit(solution)/shard_map/ppermute | solution.py:24
  235.2 8.2 %collective-permute-start.17 = (f32[1,64]{1,0:T(1,128)S(1)}, f32[1,64]{1,0:T(1,128)S(1)}, u32[]{:S(2)}, u32[]{:S(2)}) collective-permute-start(f32[1,64]{1,0:T(1,128)S(1)} %get-tuple-element.211), channel_id=1, source_target_pairs={{0,8},{8,16},{16,24},{24,32},{32,40},{40,48},{48,56},{56,64},{64,7... | collective-permute-start | bytes 776 | tf_op jit(solution)/shard_map/ppermute | solution.py:33
  235.5 7.9 %collective-permute-start.18 = (f32[1,64]{1,0:T(1,128)S(1)}, f32[1,64]{1,0:T(1,128)S(1)}, u32[]{:S(2)}, u32[]{:S(2)}) collective-permute-start(f32[1,64]{1,0:T(1,128)S(1)} %get-tuple-element.212), channel_id=1, source_target_pairs={{8,0},{16,8},{24,16},{32,24},{40,32},{48,40},{56,48},{64,56},{72,6... | collective-permute-start | bytes 776 | tf_op jit(solution)/shard_map/ppermute | solution.py:36
  241.7 4.8 %collective-permute-start.21 = (f32[4,32]{0,1:T(8,128)S(1)}, f32[4,32]{0,1:T(8,128)S(1)}, u32[]{:S(2)}, u32[]{:S(2)}) collective-permute-start(f32[4,32]{0,1:T(8,128)S(1)} %slice_bitcast_fusion.7), channel_id=1, source_target_pairs={{0,7},{1,0},{2,1},{3,2},{4,3},{5,4},{6,5},{7,6},{8,15},{9,8},{10,9... | collective-permute-start | bytes 1544 | tf_op jit(solution)/shard_map/ppermute | solution.py:24
  243.5 7.9 %collective-permute-start.19 = (f32[34,1]{1,0:T(8,128)S(1)}, f32[34,1]{1,0:T(8,128)S(1)}, u32[]{:S(2)}, u32[]{:S(2)}) collective-permute-start(f32[34,1]{1,0:T(8,128)S(1)} %get-tuple-element.205), channel_id=1, source_target_pairs={{0,1},{1,2},{2,3},{3,4},{4,5},{5,6},{6,7},{7,0},{8,9},{9,10},{10,1... | collective-permute-start | bytes 416 | tf_op jit(solution)/shard_map/ppermute | solution.py:33
  243.5 7.9 %collective-permute-start.20 = (f32[34,1]{1,0:T(8,128)S(1)}, f32[34,1]{1,0:T(8,128)S(1)}, u32[]{:S(2)}, u32[]{:S(2)}) collective-permute-start(f32[34,1]{1,0:T(8,128)S(1)} %get-tuple-element.206), channel_id=1, source_target_pairs={{1,0},{2,1},{3,2},{4,3},{5,4},{6,5},{7,6},{0,7},{9,8},{10,9},{11,1... | collective-permute-start | bytes 416 | tf_op jit(solution)/shard_map/ppermute | solution.py:36
  246.7 6.0 %collective-permute-start.22 = (f32[4,64]{1,0:T(4,128)S(1)}, f32[4,64]{1,0:T(4,128)S(1)}, u32[]{:S(2)}, u32[]{:S(2)}) collective-permute-start(f32[4,64]{1,0:T(4,128)S(1)} %slice.614), channel_id=1, source_target_pairs={{0,120},{8,0},{16,8},{24,16},{32,24},{40,32},{48,40},{56,48},{64,5... | collective-permute-start | bytes 3080 | tf_op jit(solution)/shard_map/ppermute | solution.py:24
  253.5 7.1 %collective-permute-start.23 = (f32[1,32]{1,0:T(1,128)S(1)}, f32[1,32]{1,0:T(1,128)S(1)}, u32[]{:S(2)}, u32[]{:S(2)}) collective-permute-start(f32[1,32]{1,0:T(1,128)S(1)} %get-tuple-element.217), channel_id=1, source_target_pairs={{0,8},{8,16},{16,24},{24,32},{32,40},{40,48},{48,56},{56,64},{64,7... | collective-permute-start | bytes 392 | tf_op jit(solution)/shard_map/ppermute | solution.py:33
  253.5 7.1 %collective-permute-start.24 = (f32[1,32]{1,0:T(1,128)S(1)}, f32[1,32]{1,0:T(1,128)S(1)}, u32[]{:S(2)}, u32[]{:S(2)}) collective-permute-start(f32[1,32]{1,0:T(1,128)S(1)} %get-tuple-element.218), channel_id=1, source_target_pairs={{8,0},{16,8},{24,16},{32,24},{40,32},{48,40},{56,48},{64,56},{72,6... | collective-permute-start | bytes 392 | tf_op jit(solution)/shard_map/ppermute | solution.py:36
  260.7 4.3 %collective-permute-start.25 = (f32[18,1]{1,0:T(8,128)S(1)}, f32[18,1]{1,0:T(8,128)S(1)}, u32[]{:S(2)}, u32[]{:S(2)}) collective-permute-start(f32[18,1]{1,0:T(8,128)S(1)} %get-tuple-element.213), channel_id=1, source_target_pairs={{0,1},{1,2},{2,3},{3,4},{4,5},{5,6},{6,7},{7,0},{8,9},{9,10},{10,1... | collective-permute-start | bytes 224 | tf_op jit(solution)/shard_map/ppermute | solution.py:33
  260.7 4.4 %collective-permute-start.26 = (f32[18,1]{1,0:T(8,128)S(1)}, f32[18,1]{1,0:T(8,128)S(1)}, u32[]{:S(2)}, u32[]{:S(2)}) collective-permute-start(f32[18,1]{1,0:T(8,128)S(1)} %get-tuple-element.214), channel_id=1, source_target_pairs={{1,0},{2,1},{3,2},{4,3},{5,4},{6,5},{7,6},{0,7},{9,8},{10,9},{11,1... | collective-permute-start | bytes 224 | tf_op jit(solution)/shard_map/ppermute | solution.py:36
  (24 other events, 144.9 us)
where the time goes:
time: 267 us; the launch traced here: 266 us
  local copies, waits for them, and re-layouts  85.3 us (32%)
  starting transfers between devices  71.7 us (27%)
  waiting for transfers between devices  55.7 us (21%)
  other arithmetic  30.4 us (11%)
  matrix products  20.4 us (8%)
    ppermute x8, starting transfers between devices, extended_2(): lax.ppermute(lax.slice_in_dim(block, 0, width, axis=dim), axis, backward)  33.8 us
    all_to_all x1, waiting for transfers between devices, route_bricks(): lax.all_to_all(first, ('rows', 'cols'), split_axis=0, concat_axis=0, tile...  20.2 us
    ppermute x11, waiting for transfers between devices, from_behind(): return lax.ppermute(x, axis, [(i, (i + by) % size) for i in range(size)])  19.3 us
    ppermute x11, starting transfers between devices, from_behind(): return lax.ppermute(x, axis, [(i, (i + by) % size) for i in range(size)])  14.8 us
    squeeze x16, local copies, waits for them, and re-layouts, deposit_groups(): lax.map(one_group, (offsets.reshape((blocks, per_group) + offsets.shape[1...  14.7 us
    reshape x3, local copies, waits for them, and re-layouts, pool_pairs(): return jnp.max(values.reshape(rows_n // 2, 2, cols_n // 2, 2), axis=(1, 3))  12.4 us
    dynamic_update_slice x32, local copies, waits for them, and re-layouts, deposit_groups(): lax.map(one_group, (offsets.reshape((blocks, per_group) + offsets.shape[1...  12.3 us
    dot_general x16, matrix products, deposit_block(): jnp.einsum('gip,gjp->gij', row_part, col_part, preferred_element_type=jnp...  11.3 us
  transfers between devices with their start and end apart: 30, of which 15 were waited for; matrix products, arithmetic and copies ran while one was open for 19% of the time, Pallas kernels for 0%

commit v1 on v0

v1 whole, which is shorter than its diff:
```python
import functools

import jax
import jax.numpy as jnp
import numpy as np
from jax import lax
from jax.experimental import pallas as pl
from jax.experimental.pallas import tpu as pltpu
from jax.sharding import PartitionSpec as P

R_DEV = 256
C_DEV = 512
PMAX = 256
CAP = 8
N_DEST = 128
BRICKS = 512
SLOTS = N_DEST * CAP

TILE_ROWS = 272
UP_ROWS = 80
DOWN_ROWS = 24
DOWN_FROM = 240
ROW_ROOM = (192, 96, 48, 24)
COL_ROOM = (384, 256, 128, 128)

taps_low = (
    0.33267055295008263,
    0.8068915093110925,
    0.4598775021184915,
    -0.13501102001025458,
    -0.08544127388202666,
    0.03522629188570953,
)
taps_high = tuple(((-1.0) ** index * taps_low[5 - index] for index in range(6)))

f32 = jnp.float32
bf16 = jnp.bfloat16


def spans(size):
    out = []
    for level in range(1, 5):
        n = size >> level
        before = 8 >> (level - 1)
        after = (36, 16, 6, 1)[level - 1]
        out.append((-before, n + after, -before, n + before))
    return out


def level_table(sources, room, span):
    low_from, low_to, high_from, high_to = span
    table = np.zeros((len(sources), 2 * room), np.float64)
    for position, index in enumerate(sources):
        if index is None:
            continue
        for half, (lo, hi, taps) in enumerate(
            ((low_from, low_to, taps_low), (high_from, high_to, taps_high))
        ):
            for tap in range(6):
                if (index - tap) % 2 == 0:
                    k = (index - tap) // 2
                    if lo <= k < hi:
                        table[position, half * room + (k % room)] += taps[tap]
    return table


def room_sources(room, low_from, low_to):
    out = [None] * room
    for k in range(low_from, low_to):
        out[k % room] = k
    return out


def split(table):
    table = np.asarray(table, np.float32)
    high = table.astype(jnp.bfloat16)
    low = (table - high.astype(np.float32)).astype(jnp.bfloat16)
    return np.stack([high, low])


@functools.lru_cache(maxsize=1)
def tables():
    col_spans = spans(C_DEV)
    row_spans = spans(R_DEV)
    col_src = list(range(C_DEV))
    col_src += [C_DEV + j if j < 76 else None for j in range(128)]
    col_src += [0, C_DEV] + [None] * 110 + [j - 16 for j in range(16)]
    row_src = [i if i < 257 else None for i in range(TILE_ROWS)]
    row_src += [R_DEV + i if i < 76 else None for i in range(UP_ROWS)]
    row_src += [i - 16 if i < 17 else None for i in range(DOWN_ROWS)]
    cols, rows = [], []
    for level in range(4):
        cols.append(level_table(col_src, COL_ROOM[level], col_spans[level]))
        rows.append(level_table(row_src, ROW_ROOM[level], row_spans[level]).T)
        col_src = room_sources(COL_ROOM[level], col_spans[level][0], col_spans[level][1])
        row_src = room_sources(ROW_ROOM[level], row_spans[level][0], row_spans[level][1])
    picks = []
    for level in range(3):
        _, _, high_from, high_to = col_spans[level + 1]
        pick = np.zeros((COL_ROOM[level], COL_ROOM[level + 1]), np.float64)
        for k in range(high_from, high_to):
            pick[(2 * k) % COL_ROOM[level], k % COL_ROOM[level + 1]] = 1.0
        picks.append(pick.astype(jnp.bfloat16))
    return [split(t) for t in cols], [split(t) for t in rows], picks


def hi_lo(x):
    high = x.astype(bf16)
    low = (x - high.astype(f32)).astype(bf16)
    return high, low


def mm(a, b):
    return jnp.dot(a, b, preferred_element_type=f32)


def mm_nt(a, b):
    return lax.dot_general(a, b, (((1,), (1,)), ((), ())), preferred_element_type=f32)


def iota(shape, dim):
    return lax.broadcasted_iota(jnp.int32, shape, dim)


GROUPS_PER_STEP = 4


def deposit_kernel(off_ref, w_ref, counts_ref, owners_ref, slot_ref, out_ref, cnt_ref, patch_ref, edge_ref):
    owners = owners_ref[...]
    dest = (iota((N_DEST, BRICKS), 0) == owners).astype(f32)
    before = (iota((BRICKS, BRICKS), 0) < iota((BRICKS, BRICKS), 1)).astype(bf16)
    ranks = jnp.sum(mm(dest.astype(bf16), before) * dest, axis=0, keepdims=True)
    position = owners * CAP + ranks.astype(jnp.int32)

    slot = slot_ref[...]
    grid_row = slot // 32
    grid_col = slot % 32
    coarse = (grid_col % 8) * 4 + grid_col // 8
    row_id = iota((256, BRICKS), 0)
    spread = jnp.where(
        row_id < 128,
        counts_ref[...],
        jnp.where(row_id == 168, coarse, jnp.where(row_id == 169, grid_row, 0)),
    )
    eye = (iota((BRICKS, BRICKS), 0) == iota((BRICKS, BRICKS), 1)).astype(bf16)
    cnt_ref[...] = mm_nt(eye, spread.astype(f32).astype(bf16))

    lane = iota((8, 128), 1)
    sub = iota((8, 128), 0)
    particle = iota((8, PMAX), 1).astype(f32)
    cell = iota((16, PMAX), 0).astype(f32)

    def hat(x, at):
        return jnp.maximum(0.0, 1.0 - jnp.abs(x - at))

    def one_group(start):
        rows_at = off_ref[pl.ds(start, 8), 0:PMAX]
        cols_at = off_ref[pl.ds(start, 8), PMAX : 2 * PMAX]
        count = cnt_ref[pl.ds(start, 8), 0:128]
        count = jnp.concatenate([count, count], axis=1)
        weight = jnp.where(particle < count, w_ref[pl.ds(start, 8), :], 0.0)
        left = jnp.concatenate([hat(rows_at, float(i)) * weight for i in range(17)], axis=0).astype(bf16)
        right = [hat(cols_at[(8 - g) % 8 : (8 - g) % 8 + 1, :], cell) for g in range(8)]
        last = hat(cols_at, 16.0)
        right = jnp.concatenate(right + [last] * 16, axis=0).astype(bf16)
        full = mm_nt(left, right)
        halves = []
        for half in range(2):
            acc = None
            for pair in range(4):
                at = (half * 8 + pair * 2) * 8
                even = pltpu.roll(full[at : at + 8, 0:128], 0, 1, stride=16, stride_axis=0)
                odd = pltpu.roll(full[at + 8 : at + 16, 0:128], 16, 1, stride=16, stride_axis=0)
                both = jnp.where(lane // 16 == 0, even, odd)
                acc = both if pair == 0 else jnp.where(lane // 32 == pair, pltpu.roll(both, 32 * pair, 1), acc)
            halves.append(acc)
        bottom = pltpu.roll(full[128:136, 0:128], 0, 1, stride=16, stride_axis=0)
        corner = jnp.sum(jnp.where(lane == sub, full[128:136, 128:256], 0.0), axis=1, keepdims=True)
        third = jnp.where(lane < 16, bottom, jnp.where(lane == 32, corner, 0.0))
        edge = jnp.zeros((8, 128), f32)
        for i in range(16):
            edge = jnp.where(lane == 8 * i + sub, full[8 * i : 8 * i + 8, 128:256], edge)
        patch_ref[pl.ds(start, 8), 0:128] = halves[0]
        patch_ref[pl.ds(start, 8), 128:256] = halves[1]
        patch_ref[pl.ds(start, 8), 256:384] = third + cnt_ref[pl.ds(start, 8), 128:256]
        edge_ref[pl.ds(start, 8), :] = edge

    def step(index, carry):
        for sub_group in range(GROUPS_PER_STEP):
            one_group(pl.multiple_of((index * GROUPS_PER_STEP + sub_group) * 8, 8))
        return carry

    lax.fori_loop(0, BRICKS // 8 // GROUPS_PER_STEP, step, 0)

    gather = (iota((128, 128), 1) == iota((128, 128), 0) // 8 + 16).astype(bf16)
    edge_high, edge_low = hi_lo(edge_ref[...])
    patch_ref[:, 256:384] = patch_ref[:, 256:384] + (mm(edge_high, gather) + mm(edge_low, gather))

    high, low = hi_lo(patch_ref[...])
    for chunk in range(4):
        rows = SLOTS // 4
        pick = (iota((rows, BRICKS), 0) + chunk * rows == position).astype(bf16)
        out_ref[chunk * rows : (chunk + 1) * rows, :] = mm(pick, high) + mm(pick, low)


def deposit_and_pack(offsets, weights, counts, owners, slots):
    return pl.pallas_call(
        deposit_kernel,
        out_shape=jax.ShapeDtypeStruct((SLOTS, 384), f32),
        scratch_shapes=[
            pltpu.VMEM((BRICKS, 256), f32),
            pltpu.VMEM((BRICKS, 384), f32),
            pltpu.VMEM((BRICKS, 128), f32),
        ],
        compiler_params=pltpu.CompilerParams(vmem_limit_bytes=40 << 20),
        name="deposit",
    )(
        offsets.reshape(BRICKS, 2 * PMAX),
        weights,
        counts.reshape(1, BRICKS),
        owners.reshape(1, BRICKS),
        slots.reshape(1, BRICKS),
    )


def place_kernel(x_ref, raw_ref, left_ref, right_ref, grid_ref):
    lane8 = iota((8, 128), 1)
    weigh = jnp.where(lane8 == 40, 16.0, jnp.where(lane8 == 41, 1.0, 0.0)).astype(bf16)
    slot = mm_nt(weigh, x_ref[:, 256:384].astype(bf16))[0:1, :].astype(jnp.int32)
    high, low = hi_lo(x_ref[...])
    for chunk in range(4):
        pick = (iota((128, SLOTS), 0) + chunk * 128 == slot).astype(bf16)
        grid_ref[chunk * 128 : (chunk + 1) * 128, :] = mm(pick, high) + mm(pick, low)

    group = lane8 // 16
    masks = {d: (group // d) % 2 == 0 for d in (1, 2, 4)}

    def swap_groups(tiles):
        for d in (1, 2, 4):
            new = list(tiles)
            for a in range(8):
                if (a // d) % 2 == 0:
                    one, two = tiles[a], tiles[a + d]
                    new[a] = jnp.where(masks[d], one, pltpu.roll(two, 16 * d, 1))
                    new[a + d] = jnp.where(masks[d], pltpu.roll(one, 128 - 16 * d, 1), two)
            tiles = new
        return tiles

    def tiles_of(third, across, half):
        at = across * 16 + half * 8
        return swap_groups(
            [grid_ref[low_col * 64 + at : low_col * 64 + at + 8, third * 128 : (third + 1) * 128] for low_col in range(8)]
        )

    first_lane = lane8 == 0
    group_start = lane8 % 16 == 0
    for across in range(4):
        raw_ref[across * TILE_ROWS + 256 : (across + 1) * TILE_ROWS, :] = jnp.zeros((TILE_ROWS - 256, 128), f32)
    right_ref[256:TILE_ROWS, :] = jnp.zeros((TILE_ROWS - 256, 128), f32)
    left_ref[256:TILE_ROWS, :] = jnp.zeros((TILE_ROWS - 256, 128), f32)

    previous = None
    for across in range(4):
        rows = [[None, None] for _ in range(17)]
        turned = [[None, None] for _ in range(17)]
        for half in range(2):
            upper = tiles_of(0, across, half)
            lower = tiles_of(1, across, half)
            edges = tiles_of(2, across, half)
            for i in range(8):
                rows[i][half] = upper[i]
                rows[8 + i][half] = lower[i]
            rows[16][half] = edges[0]
            for i in range(16):
                turned[i][half] = pltpu.roll(edges[1], 16 - i, 1)
            turned[16][half] = pltpu.roll(edges[2], 16, 1)
            for i in range(17):
                before = jnp.zeros((8, 128), f32) if previous is None else previous[i][half]
                spill = jnp.where(first_lane, before, jnp.where(group_start, turned[i][half], 0.0))
                rows[i][half] = rows[i][half] + spill
        previous = turned
        def finish(parts, i, ref, top):
            if i == 0:
                down_low = pltpu.roll(parts[16][0], 1, 0)
                down_high = pltpu.roll(parts[16][1], 1, 0)
                sub = iota((8, 128), 0)
                low = parts[0][0] + jnp.where(sub == 0, 0.0, down_low)
                high_part = parts[0][1] + jnp.where(sub == 0, down_low, down_high)
                both = (low, high_part)
                ref[top + 256 : top + 257, :] = parts[16][1][7:8, :]
            else:
                both = (parts[i][0], parts[i][1])
            ref[pl.ds(top + i, 8, stride=16), :] = both[0]
            ref[pl.ds(top + 128 + i, 8, stride=16), :] = both[1]

        for i in range(16):
            finish(rows, i, raw_ref, across * TILE_ROWS)
        if across == 0:
            for i in range(16):
                finish(rows, i, left_ref, 0)
        if across == 3:
            with_spill = [
                [jnp.where(first_lane, turned[i][half], rows[i][half]) for half in range(2)] for i in range(17)
            ]
            for i in range(16):
                finish(with_spill, i, right_ref, 0)


def place_and_fold(arrived):
    return pl.pallas_call(
        place_kernel,
        out_shape=(
            jax.ShapeDtypeStruct((4 * TILE_ROWS, 128), f32),
            jax.ShapeDtypeStruct((TILE_ROWS, 128), f32),
            jax.ShapeDtypeStruct((TILE_ROWS, 128), f32),
        ),
        scratch_shapes=[pltpu.VMEM((BRICKS, 384), f32)],
        compiler_params=pltpu.CompilerParams(vmem_limit_bytes=40 << 20),
        name="place",
    )(arrived)


def mm3(data, table_ref):
    high, low = hi_lo(data)
    return mm(high, table_ref[0]) + (mm(low, table_ref[0]) + mm(high, table_ref[1]))


def mm3_left(table_ref, data):
    high, low = hi_lo(data)
    return mm(table_ref[0], high) + (mm(table_ref[0], low) + mm(table_ref[1], high))


def columns_kernel(raw_ref, to_right_ref, from_right_ref, from_left_ref, table_ref, out_ref, up_ref, down_ref):
    lane = iota((TILE_ROWS, 128), 1)
    from_left = jnp.where(lane == 1, pltpu.roll(to_right_ref[...], 1, 1), from_left_ref[...])
    data = jnp.concatenate(
        [raw_ref[across * TILE_ROWS : (across + 1) * TILE_ROWS, :] for across in range(4)]
        + [from_right_ref[...], from_left],
        axis=1,
    )
    out_ref[...] = mm3(data, table_ref)
    up_ref[...] = out_ref[0:UP_ROWS, :]
    down_ref[...] = out_ref[DOWN_FROM : DOWN_FROM + DOWN_ROWS, :]


def first_columns(raw, to_right, from_right, from_left, table):
    width = 2 * COL_ROOM[0]
    return pl.pallas_call(
        columns_kernel,
        out_shape=(
            jax.ShapeDtypeStruct((TILE_ROWS, width), f32),
            jax.ShapeDtypeStruct((UP_ROWS, width), f32),
            jax.ShapeDtypeStruct((DOWN_ROWS, width), f32),
        ),
        compiler_params=pltpu.CompilerParams(vmem_limit_bytes=40 << 20),
        name="columns",
    )(raw, to_right, from_right, from_left, table)


def levels_kernel(own_ref, below_ref, above_ref, *refs):
    col_refs = (None,) + refs[0:3]
    row_refs = refs[3:7]
    pick_refs = refs[7:10]
    leader_refs = refs[10:14]
    approx_ref = refs[14]
    peak_ref = refs[15]
    current = jnp.concatenate([own_ref[...], below_ref[...], above_ref[...]], axis=0)
    peak = None
    for level in range(4):
        room_r = ROW_ROOM[level]
        room_c = COL_ROOM[level]
        if level:
            current = mm3(current, col_refs[level])
        both = mm3_left(row_refs[level], current)
        current = both[:room_r, :room_c]
        detail_a = both[:room_r, room_c:]
        detail_b = both[room_r:, :room_c]
        detail_c = both[room_r:, room_c:]
        now = jnp.maximum(jnp.maximum(jnp.abs(detail_a), jnp.abs(detail_b)), jnp.abs(detail_c))
        if peak is not None:
            now = jnp.maximum(now, peak)
        wide = jnp.maximum(now, jnp.maximum(pltpu.roll(now, 1, 1), pltpu.roll(now, room_c - 1, 1)))
        wide = jnp.maximum(wide, jnp.maximum(pltpu.roll(wide, 1, 0), pltpu.roll(wide, room_r - 1, 0)))
        n_r = R_DEV >> (level + 1)
        n_c = C_DEV >> (level + 1)
        leader_refs[level][...] = wide[:n_r, :n_c]
        if level < 3:
            pairs = jnp.maximum(now, pltpu.roll(now, room_c - 1, 1))
            pooled = []
            for across in range(room_c // 128):
                top = across * ROW_ROOM[0]
                peak_ref[top : top + room_r, :] = pairs[:, across * 128 : (across + 1) * 128]
                pooled.append(
                    jnp.maximum(
                        peak_ref[pl.ds(top, room_r // 2, stride=2), :],
                        peak_ref[pl.ds(top + 1, room_r // 2, stride=2), :],
                    )
                )
            high, low = hi_lo(jnp.concatenate(pooled, axis=1) if len(pooled) > 1 else pooled[0])
            pick = pick_refs[level][...]
            peak = mm(high, pick) + mm(low, pick)
    approx_ref[...] = current[: R_DEV >> 4, : C_DEV >> 4]


def all_levels(own, below, above, cols, rows, picks):
    shapes = [(R_DEV >> level, C_DEV >> level) for level in (1, 2, 3, 4, 4)]
    return pl.pallas_call(
        levels_kernel,
        out_shape=tuple(jax.ShapeDtypeStruct(shape, f32) for shape in shapes),
        scratch_shapes=[pltpu.VMEM((3 * ROW_ROOM[0], 128), f32)],
        compiler_params=pltpu.CompilerParams(vmem_limit_bytes=48 << 20),
        name="levels",
    )(own, below, above, *cols[1:], *rows, *picks)


def shifted(x, axis, by):
    size = lax.axis_size(axis)
    return lax.ppermute(x, axis, [(i, (i + by) % size) for i in range(size)])


def on_device(offsets, lens_weight, counts, owners, brick_slot):
    cols, rows, picks = tables()
    cols = [jnp.asarray(t) for t in cols]
    rows = [jnp.asarray(t) for t in rows]
    picks = [jnp.asarray(t) for t in picks]
    packed = deposit_and_pack(offsets, lens_weight, counts, owners, brick_slot)
    arrived = lax.all_to_all(
        packed.reshape(N_DEST, CAP, 384), ("rows", "cols"), split_axis=0, concat_axis=0, tiled=True
    )
    raw, to_left, to_right = place_and_fold(arrived.reshape(SLOTS, 384))
    from_right = shifted(to_left, "cols", -1)
    from_left = shifted(to_right, "cols", 1)
    own, to_up, to_down = first_columns(raw, to_right, from_right, from_left, cols[0])
    below = shifted(to_up, "rows", -1)
    above = shifted(to_down, "rows", 1)
    return all_levels(own, below, above, cols, rows, picks)


def solution(mesh):
    placed = (
        P(("rows", "cols"), None, None),
        P(("rows", "cols"), None),
        P(("rows", "cols")),
        P(("rows", "cols")),
        P(("rows", "cols")),
    )
    return jax.shard_map(
        on_device,
        mesh=mesh,
        in_specs=placed,
        out_specs=(P("rows", "cols"),) * 5,
        check_vma=False,
    )
```

time: 267 us -> 70.3 us (0.26)
  local copies, waits for them, and re-layouts: 85.3 us -> 1.44 us
  starting transfers between devices: 71.7 us -> 2.61 us
  waiting for transfers between devices: 55.7 us -> 12.2 us
  blocking collectives: 0 us -> 35.7 us
  other arithmetic: 30.4 us -> 0 us
  matrix products: 20.4 us -> 0 us
  Pallas kernels: 0 us -> 17.3 us
    ppermute x27 -> x4, starting transfers between devices: 49 us -> 2.61 us  [shifted(): return lax.ppermute(x, axis, [(i, (i + by) % size) for i in range(size)])]
    all_to_all x0 -> x1, blocking collectives: none -> 35.7 us  [on_device(): lax.all_to_all(packed.reshape(N_DEST, CAP, 384), ('rows', 'cols'), split_...]
    all_to_all x3 -> x0, waiting for transfers between devices: 32.4 us -> none  [the longest x1 20.2 us: route_bricks(): lax.all_to_all(first, ('rows', 'cols'), split_axis=0, concat_axis=0, tile...]
    reshape x39 -> x0, local copies, waits for them, and re-layouts: 27.7 us -> none  [the longest x3 12.4 us: pool_pairs(): return jnp.max(values.reshape(rows_n // 2, 2, cols_n // 2, 2), axis=(1, 3))]
    all_to_all x3 -> x0, starting transfers between devices: 22.7 us -> none  [the longest x1 11.1 us: route_bricks(): lax.all_to_all(third, ('rows', 'cols'), split_axis=0, concat_axis=0, tile...]
    dot_general x25 -> x0, matrix products: 20.4 us -> none  [the longest x16 11.3 us: deposit_block(): jnp.einsum('gip,gjp->gij', row_part, col_part, preferred_element_type=jnp...]
    pallas_call x0 -> x4, Pallas kernels: none -> 17.3 us  [the longest x1 9.77 us: deposit_and_pack(): pl.pallas_call(deposit_kernel, out_shape=jax.ShapeDtypeStruct((SLOTS, 384...]
    squeeze x17 -> x0, local copies, waits for them, and re-layouts: 15.4 us -> none  [the longest x16 14.7 us: deposit_groups(): lax.map(one_group, (offsets.reshape((blocks, per_group) + offsets.shape[1...]
  transfers between devices with their start and end apart: 30 -> 4, of which waited for: 15 -> 3; matrix products, arithmetic and copies ran while one was open for 19% -> 0% of each run, Pallas kernels for 0% -> 0%
where the time goes in v1:
time: 70.3 us; the launch traced here: 70.1 us
  blocking collectives  35.7 us (51%)
  Pallas kernels  17.3 us (25%)
  waiting for transfers between devices  12.2 us (17%)
  starting transfers between devices  2.61 us (4%)
  local copies, waits for them, and re-layouts  1.44 us (2%)
  between operations  0.87 us (1%)
    all_to_all x1, blocking collectives, on_device(): lax.all_to_all(packed.reshape(N_DEST, CAP, 384), ('rows', 'cols'), split_...  35.7 us
    ppermute x4, waiting for transfers between devices, shifted(): return lax.ppermute(x, axis, [(i, (i + by) % size) for i in range(size)])  12.2 us
    pallas_call x1, Pallas kernels, deposit_and_pack(): pl.pallas_call(deposit_kernel, out_shape=jax.ShapeDtypeStruct((SLOTS, 384...  9.77 us
    pallas_call x1, Pallas kernels, all_levels(): pl.pallas_call(levels_kernel, out_shape=tuple((jax.ShapeDtypeStruct(shape...  4.33 us
    ppermute x4, starting transfers between devices, shifted(): return lax.ppermute(x, axis, [(i, (i + by) % size) for i in range(size)])  2.61 us
    pallas_call x1, Pallas kernels, place_and_fold(): pl.pallas_call(place_kernel, out_shape=(jax.ShapeDtypeStruct((4 * TILE_RO...  2 us
    unnamed x31, local copies, waits for them, and re-layouts  1.44 us
  transfers between devices with their start and end apart: 4, of which 3 were waited for; matrix products, arithmetic and copies ran while one was open for 0% of the time, Pallas kernels for 0%

profile of v1, /device:TPU:0, one launch (start us, length us, event | category | flops | bytes accessed | tf_op | source)
XLA Modules:
  0.0 70.1 jit_solution(463127665631885117)
XLA Ops:
  0.6 0.0 copy-start.14
  0.6 0.0 copy-start.13
  0.7 0.0 copy-start.12
  0.7 0.0 copy-start.3
  0.7 1.4 %copy.21 = f32[64,8,2,256]{3,1,2,0:T(8,128)S(1)} copy(f32[64,8,2,256]{3,2,1,0:T(2,128)} %bitcast.13) | data formatting | bytes 2097152
  2.0 0.0 copy-done.14
  2.0 0.0 copy-done.13
  2.0 0.0 copy-done.12
  2.1 0.0 copy-done.3
  2.1 9.8 %deposit.1 = f32[1024,384]{1,0:T(8,128)S(1)} custom-call(f32[512,512]{1,0:T(8,128)S(1)} %bitcast.9, f32[512,256]{1,0:T(8,128)S(1)} %copy-done.3, s32[1,512]{1,0:T(1,128)S(1)} %bitcast.10, s32[1,512]{1,0:T(1,128)S(1)} %bitcast.11, s32[1,512]{1,0:T(1,128)S(1)} %bitcast.12), custom_call_target="tpu_custom_call" | custom-call | tf_op jit(solution)/shard_map/deposit/pallas_call | solution.py:207
  11.8 0.0 copy-start
  11.9 35.7 %all_to_all.5 = f32[128,8,384]{2,1,0:T(8,128)S(1)} all-to-all(f32[128,8,384]{2,1,0:T(8,128)S(1)} %bitcast.8), channel_id=1, replica_groups=mesh['rows'=16,'cols'=8] {'rows','cols'}, dimensions={0} | all-to-all | bytes 3145728 | tf_op jit(solution)/shard_map/all_to_all | solution.py:427
  47.6 2.0 %place.1 = (f32[1088,128]{1,0:T(8,128)S(1)}, f32[272,128]{1,0:T(8,128)S(1)}, f32[272,128]{1,0:T(8,128)S(1)}) custom-call(f32[1024,384]{1,0:T(8,128)S(1)} %bitcast.7), custom_call_target="tpu_custom_call" | custom-call | tf_op jit(solution)/shard_map/place/pallas_call | solution.py:310
  49.6 0.0 collective-permute-start
  49.6 0.5 collective-permute-start.1
  50.1 2.1 %collective-permute-done.from_right_ref = f32[272,128]{1,0:T(8,128)S(1)} collective-permute-done((f32[272,128]{1,0:T(8,128)S(1)}, f32[272,128]{1,0:T(8,128)S(1)}, u32[]{:S(2)}, u32[]{:S(2)}) %collective-permute-start) | collective-permute-done | bytes 139296 | tf_op jit(solution)/shard_map/ppermute | solution.py:418
  52.2 3.1 %collective-permute-done.1.from_left_ref = f32[272,128]{1,0:T(8,128)S(1)} collective-permute-done((f32[272,128]{1,0:T(8,128)S(1)}, f32[272,128]{1,0:T(8,128)S(1)}, u32[]{:S(2)}, u32[]{:S(2)}) %collective-permute-start.1) | collective-permute-done | bytes 139296 | tf_op jit(solution)/shard_map/ppermute | solution.py:418
  55.3 0.0 copy-done
  55.3 0.0 copy-start.1
  55.3 0.0 copy-start.2
  55.3 0.0 copy-start.4
  55.4 0.0 copy-start.5
  55.4 0.0 copy-start.6
  55.4 0.0 copy-start.7
  55.4 0.0 copy-start.8
  55.4 0.0 copy-start.9
  55.4 0.0 copy-start.10
  55.4 0.0 copy-start.11
  55.4 1.2 %columns.1 = (f32[272,768]{1,0:T(8,128)S(1)}, f32[80,768]{1,0:T(8,128)S(1)}, f32[24,768]{1,0:T(8,128)S(1)}) custom-call(f32[1088,128]{1,0:T(8,128)S(1)} %get-tuple-element.11.raw_ref, f32[272,128]{1,0:T(8,128)S(1)} %get-tuple-element.12.to_right_ref, f32[272,128]{1,0:T(8,128)S(1)} %collective-permute-done.from_right_ref, ...), custom_call_target="tpu_custom_call" | custom-call | tf_op jit(solution)/shard_map/columns/pallas_call | solution.py:348
  56.6 1.4 %collective-permute-start.2 = (f32[80,768]{1,0:T(8,128)S(1)}, f32[80,768]{1,0:T(8,128)S(1)}, u32[]{:S(2)}, u32[]{:S(2)}) collective-permute-start(f32[80,768]{1,0:T(8,128)S(1)} %get-tuple-element.15), channel_id=1, source_target_pairs={{0,120},{8,0},{16,8},{24,16},{32,24},{40,32},{48,40},{56,48},{64,5... | collective-permute-start | bytes 737288 | tf_op jit(solution)/shard_map/ppermute | solution.py:418
  58.0 0.7 collective-permute-start.3
  58.7 7.0 %collective-permute-done.3.above_ref = f32[24,768]{1,0:T(8,128)S(1)} collective-permute-done((f32[24,768]{1,0:T(8,128)S(1)}, f32[24,768]{1,0:T(8,128)S(1)}, u32[]{:S(2)}, u32[]{:S(2)}) %collective-permute-start.3) | collective-permute-done | bytes 73760 | tf_op jit(solution)/shard_map/ppermute | solution.py:418
  65.7 0.0 collective-permute-done.2.below_ref
  65.7 0.0 copy-done.1
  65.7 0.0 copy-done.2
  65.7 0.0 copy-done.4
  65.7 0.0 copy-done.5
  65.7 0.0 copy-done.6
  65.7 0.0 copy-done.7
  65.7 0.0 copy-done.8
  65.8 0.0 copy-done.9
  65.8 0.0 copy-done.10
  65.8 0.0 copy-done.11
  65.8 4.3 %levels.1 = (f32[128,256]{1,0:T(8,128)}, f32[64,128]{1,0:T(8,128)}, f32[32,64]{1,0:T(8,128)}, f32[16,32]{1,0:T(8,128)}, f32[16,32]{1,0:T(8,128)}) custom-call(f32[272,768]{1,0:T(8,128)S(1)} %get-tuple-element.14.own_ref, f32[80,768]{1,0:T(8,128)S(1)} %collective-permute-done.2.below_ref, f32[24,768]{1,0:T(8,128)S(1)} %collective-permute-done.3.above_ref, ...), custom_call_target="tpu_custom_call" | custom-call | tf_op jit(solution)/shard_map/levels/pallas_call | solution.py:407
Async XLA Ops:
  0.6 1.4 %copy-start.14 = (s32[512]{0:T(512)S(1)}, s32[512]{0:T(512)}, u32[]{:S(2)}) copy-start(s32[512]{0:T(512)} %param.20) | copy-start | bytes 6148
  0.6 1.4 %copy-start.13 = (s32[512]{0:T(512)S(1)}, s32[512]{0:T(512)}, u32[]{:S(2)}) copy-start(s32[512]{0:T(512)} %param.19) | copy-start | bytes 6148
  0.7 1.4 %copy-start.12 = (s32[512]{0:T(512)S(1)}, s32[512]{0:T(512)}, u32[]{:S(2)}) copy-start(s32[512]{0:T(512)} %param.18) | copy-start | bytes 6148
  0.7 1.4 %copy-start.3 = (f32[512,256]{1,0:T(8,128)S(1)}, f32[512,256]{1,0:T(8,128)}, u32[]{:S(2)}) copy-start(f32[512,256]{1,0:T(8,128)} %w_ref.1) | copy-start | bytes 1572868
  11.8 43.5 %copy-start = (bf16[2,768,768]{2,1,0:T(8,128)(2,1)S(1)}, bf16[2,768,768]{2,1,0:T(8,128)(2,1)}, u32[]{:S(2)}) copy-start(bf16[2,768,768]{2,1,0:T(8,128)(2,1)} %constant.22.clone.table_ref) | copy-start | bytes 7077892
  49.6 2.6 %collective-permute-start = (f32[272,128]{1,0:T(8,128)S(1)}, f32[272,128]{1,0:T(8,128)S(1)}, u32[]{:S(2)}, u32[]{:S(2)}) collective-permute-start(f32[272,128]{1,0:T(8,128)S(1)} %get-tuple-element.13), channel_id=1, source_target_pairs={{0,7},{1,0},{2,1},{3,2},{4,3},{5,4},{6,5},{7,6},{8,15},{9,8},{10,9... | collective-permute-start | bytes 417800 | tf_op jit(solution)/shard_map/ppermute | solution.py:418
  49.6 5.7 %collective-permute-start.1 = (f32[272,128]{1,0:T(8,128)S(1)}, f32[272,128]{1,0:T(8,128)S(1)}, u32[]{:S(2)}, u32[]{:S(2)}) collective-permute-start(f32[272,128]{1,0:T(8,128)S(1)} %get-tuple-element.12.to_right_ref), channel_id=1, source_target_pairs={{0,1},{1,2},{2,3},{3,4},{4,5},{5,6},{6,7},{7,0},{8,9},{9,10},{10,1... | collective-permute-start | bytes 417800 | tf_op jit(solution)/shard_map/ppermute | solution.py:418
  55.3 10.4 %copy-start.1 = (bf16[2,384,512]{2,1,0:T(8,128)(2,1)S(1)}, bf16[2,384,512]{2,1,0:T(8,128)(2,1)}, u32[]{:S(2)}) copy-start(bf16[2,384,512]{2,1,0:T(8,128)(2,1)} %constant.23.clone.refs_0_) | copy-start | bytes 2359300
  55.3 10.4 %copy-start.2 = (bf16[2,384,376]{2,1,0:T(8,128)(2,1)S(1)}, bf16[2,384,376]{2,1,0:T(8,128)(2,1)}, u32[]{:S(2)}) copy-start(bf16[2,384,376]{2,1,0:T(8,128)(2,1)} %constant.26.clone.refs_3_) | copy-start | bytes 1732612
  55.3 10.4 %copy-start.4 = (bf16[2,256,256]{2,1,0:T(8,128)(2,1)S(1)}, bf16[2,256,256]{2,1,0:T(8,128)(2,1)}, u32[]{:S(2)}) copy-start(bf16[2,256,256]{2,1,0:T(8,128)(2,1)} %constant.24.clone.refs_1_) | copy-start | bytes 786436
  55.4 10.4 %copy-start.5 = (bf16[384,256]{1,0:T(8,128)(2,1)S(1)}, bf16[384,256]{1,0:T(8,128)(2,1)}, u32[]{:S(2)}) copy-start(bf16[384,256]{1,0:T(8,128)(2,1)} %constant.30.clone.refs_7_) | copy-start | bytes 589828
  55.4 10.4 %copy-start.6 = (bf16[2,192,192]{2,1,0:T(8,128)(2,1)S(1)}, bf16[2,192,192]{2,1,0:T(8,128)(2,1)}, u32[]{:S(2)}) copy-start(bf16[2,192,192]{2,1,0:T(8,128)(2,1)} %constant.27.clone.refs_4_) | copy-start | bytes 442372
  55.4 10.4 %copy-start.7 = (bf16[2,128,256]{2,1,0:T(8,128)(2,1)S(1)}, bf16[2,128,256]{2,1,0:T(8,128)(2,1)}, u32[]{:S(2)}) copy-start(bf16[2,128,256]{2,1,0:T(8,128)(2,1)} %constant.25.clone.refs_2_) | copy-start | bytes 393220
  55.4 10.4 %copy-start.8 = (bf16[256,128]{1,0:T(8,128)(2,1)S(1)}, bf16[256,128]{1,0:T(8,128)(2,1)}, u32[]{:S(2)}) copy-start(bf16[256,128]{1,0:T(8,128)(2,1)} %constant.31.clone.refs_8_) | copy-start | bytes 196612
  55.4 10.4 %copy-start.9 = (bf16[2,96,96]{2,1,0:T(8,128)(2,1)S(1)}, bf16[2,96,96]{2,1,0:T(8,128)(2,1)}, u32[]{:S(2)}) copy-start(bf16[2,96,96]{2,1,0:T(8,128)(2,1)} %constant.28.clone.refs_5_) | copy-start | bytes 110596
  55.4 10.3 %copy-start.10 = (bf16[128,128]{1,0:T(8,128)(2,1)S(1)}, bf16[128,128]{1,0:T(8,128)(2,1)}, u32[]{:S(2)}) copy-start(bf16[128,128]{1,0:T(8,128)(2,1)} %constant.32.clone.refs_9_) | copy-start | bytes 98308
  55.4 10.3 %copy-start.11 = (bf16[2,48,48]{2,1,0:T(8,128)(2,1)S(1)}, bf16[2,48,48]{2,1,0:T(8,128)(2,1)}, u32[]{:S(2)}) copy-start(bf16[2,48,48]{2,1,0:T(8,128)(2,1)} %constant.29.clone.refs_6_) | copy-start | bytes 27652
  56.6 9.1 %collective-permute-start.2 = (f32[80,768]{1,0:T(8,128)S(1)}, f32[80,768]{1,0:T(8,128)S(1)}, u32[]{:S(2)}, u32[]{:S(2)}) collective-permute-start(f32[80,768]{1,0:T(8,128)S(1)} %get-tuple-element.15), channel_id=1, source_target_pairs={{0,120},{8,0},{16,8},{24,16},{32,24},{40,32},{48,40},{56,48},{64,5... | collective-permute-start | bytes 737288 | tf_op jit(solution)/shard_map/ppermute | solution.py:418
  58.0 7.7 %collective-permute-start.3 = (f32[24,768]{1,0:T(8,128)S(1)}, f32[24,768]{1,0:T(8,128)S(1)}, u32[]{:S(2)}, u32[]{:S(2)}) collective-permute-start(f32[24,768]{1,0:T(8,128)S(1)} %get-tuple-element.16), channel_id=1, source_target_pairs={{0,8},{8,16},{16,24},{24,32},{32,40},{40,48},{48,56},{56,64},{64,7... | collective-permute-start | bytes 221192 | tf_op jit(solution)/shard_map/ppermute | solution.py:418

commit v2 on v1

--- a/solution.py
+++ b/solution.py
@@ -122,15 +122,59 @@
     return lax.broadcasted_iota(jnp.int32, shape, dim)
 
 
-GROUPS_PER_STEP = 4
-
-
-def deposit_kernel(off_ref, w_ref, counts_ref, owners_ref, slot_ref, out_ref, cnt_ref, patch_ref, edge_ref):
+GROUPS_PER_STEP = 16
+STEPS = BRICKS // 8 // GROUPS_PER_STEP
+STEP_BRICKS = BRICKS // STEPS
+MESSAGE = 20
+
+
+def deposit_kernel(
+    off_hbm,
+    w_hbm,
+    counts_hbm,
+    owners_hbm,
+    slot_hbm,
+    out_ref,
+    off_ref,
+    w_ref,
+    counts_ref,
+    owners_ref,
+    slot_ref,
+    cnt_ref,
+    patch_ref,
+    edge_ref,
+    small_sem,
+    off_sem,
+    w_sem,
+):
+    small = [
+        pltpu.make_async_copy(src, dst, small_sem.at[n])
+        for n, (src, dst) in enumerate(
+            ((owners_hbm, owners_ref), (slot_hbm, slot_ref), (counts_hbm, counts_ref))
+        )
+    ]
+    for copy in small:
+        copy.start()
+
+    def fetch(index):
+        off_rows = pl.ds(index * 4 * STEP_BRICKS, 4 * STEP_BRICKS)
+        w_rows = pl.ds(index * STEP_BRICKS, STEP_BRICKS)
+        return (
+            pltpu.make_async_copy(off_hbm.at[off_rows], off_ref.at[off_rows], off_sem.at[index]),
+            pltpu.make_async_copy(w_hbm.at[w_rows], w_ref.at[w_rows], w_sem.at[index]),
+        )
+
+    for index in range(STEPS):
+        for copy in fetch(index):
+            copy.start()
+    for copy in small:
+        copy.wait()
+
     owners = owners_ref[...]
     dest = (iota((N_DEST, BRICKS), 0) == owners).astype(f32)
     before = (iota((BRICKS, BRICKS), 0) < iota((BRICKS, BRICKS), 1)).astype(bf16)
     ranks = jnp.sum(mm(dest.astype(bf16), before) * dest, axis=0, keepdims=True)
-    position = owners * CAP + ranks.astype(jnp.int32)
+    position = ranks.astype(jnp.int32) * N_DEST + owners
 
     slot = slot_ref[...]
     grid_row = slot // 32
@@ -154,8 +198,9 @@
         return jnp.maximum(0.0, 1.0 - jnp.abs(x - at))
 
     def one_group(start):
-        rows_at = off_ref[pl.ds(start, 8), 0:PMAX]
-        cols_at = off_ref[pl.ds(start, 8), PMAX : 2 * PMAX]
+        first = pl.multiple_of(start * 4, 32)
+        rows_at = jnp.concatenate([off_ref[pl.ds(first + 2 * half, 8, stride=4), :] for half in range(2)], axis=1)
+        cols_at = jnp.concatenate([off_ref[pl.ds(first + 2 * half + 1, 8, stride=4), :] for half in range(2)], axis=1)
         count = cnt_ref[pl.ds(start, 8), 0:128]
         count = jnp.concatenate([count, count], axis=1)
         weight = jnp.where(particle < count, w_ref[pl.ds(start, 8), :], 0.0)
@@ -186,36 +231,57 @@
         edge_ref[pl.ds(start, 8), :] = edge
 
     def step(index, carry):
+        for copy in fetch(index):
+            copy.wait()
         for sub_group in range(GROUPS_PER_STEP):
             one_group(pl.multiple_of((index * GROUPS_PER_STEP + sub_group) * 8, 8))
         return carry
 
-    lax.fori_loop(0, BRICKS // 8 // GROUPS_PER_STEP, step, 0)
+    lax.fori_loop(0, STEPS, step, 0)
 
     gather = (iota((128, 128), 1) == iota((128, 128), 0) // 8 + 16).astype(bf16)
     edge_high, edge_low = hi_lo(edge_ref[...])
-    patch_ref[:, 256:384] = patch_ref[:, 256:384] + (mm(edge_high, gather) + mm(edge_low, gather))
-
-    high, low = hi_lo(patch_ref[...])
-    for chunk in range(4):
-        rows = SLOTS // 4
-        pick = (iota((rows, BRICKS), 0) + chunk * rows == position).astype(bf16)
-        out_ref[chunk * rows : (chunk + 1) * rows, :] = mm(pick, high) + mm(pick, low)
+    third = patch_ref[:, 256:384] + (mm(edge_high, gather) + mm(edge_low, gather))
+
+    high, low = hi_lo(patch_ref[:, 0:256])
+    ends = jnp.concatenate(hi_lo(third), axis=1)
+    lane_wide = iota((N_DEST, 128), 1)
+    for pair in range(4):
+        edges = []
+        for rank in (2 * pair, 2 * pair + 1):
+            pick = (iota((N_DEST, BRICKS), 0) + rank * N_DEST == position).astype(bf16)
+            inner = mm(pick, high) + mm(pick, low)
+            out_ref[pl.ds(rank, N_DEST, stride=MESSAGE), :] = inner[:, 0:128]
+            out_ref[pl.ds(8 + rank, N_DEST, stride=MESSAGE), :] = inner[:, 128:256]
+            both = mm(pick, ends)
+            edges.append(both[:, 0:128] + both[:, 128:256])
+        joined = jnp.where(lane_wide < 64, edges[0], pltpu.roll(edges[1], 64, 1))
+        out_ref[pl.ds(16 + pair, N_DEST, stride=MESSAGE), :] = joined
 
 
 def deposit_and_pack(offsets, weights, counts, owners, slots):
+    flat = offsets.reshape(BRICKS, 2, 2, 128).transpose(0, 2, 1, 3).reshape(4 * BRICKS, 128)
     return pl.pallas_call(
         deposit_kernel,
-        out_shape=jax.ShapeDtypeStruct((SLOTS, 384), f32),
+        out_shape=jax.ShapeDtypeStruct((N_DEST * MESSAGE, 128), f32),
+        in_specs=[pl.BlockSpec(memory_space=pltpu.MemorySpace.HBM)] * 5,
         scratch_shapes=[
+            pltpu.VMEM((4 * BRICKS, 128), f32),
+            pltpu.VMEM((BRICKS, PMAX), f32),
+            pltpu.VMEM((1, BRICKS), jnp.int32),
+            pltpu.VMEM((1, BRICKS), jnp.int32),
+            pltpu.VMEM((1, BRICKS), jnp.int32),
             pltpu.VMEM((BRICKS, 256), f32),
             pltpu.VMEM((BRICKS, 384), f32),
             pltpu.VMEM((BRICKS, 128), f32),
+            pltpu.SemaphoreType.DMA((3,)),
+            pltpu.SemaphoreType.DMA((STEPS,)),
+            pltpu.SemaphoreType.DMA((STEPS,)),
         ],
         compiler_params=pltpu.CompilerParams(vmem_limit_bytes=40 << 20),
         name="deposit",
     )(
-        offsets.reshape(BRICKS, 2 * PMAX),
+        flat,
         weights,
         counts.reshape(1, BRICKS),
         owners.reshape(1, BRICKS),
@@ -225,12 +291,23 @@
 
 def place_kernel(x_ref, raw_ref, left_ref, right_ref, grid_ref):
     lane8 = iota((8, 128), 1)
+    upper = jnp.concatenate([x_ref[pl.ds(rank, N_DEST, stride=MESSAGE), :] for rank in range(8)], axis=0)
+    lower = jnp.concatenate([x_ref[pl.ds(8 + rank, N_DEST, stride=MESSAGE), :] for rank in range(8)], axis=0)
+    ends = []
+    for pair in range(4):
+        joined = x_ref[pl.ds(16 + pair, N_DEST, stride=MESSAGE), :]
+        ends += [joined, pltpu.roll(joined, 64, 1)]
+    ends_high, ends_low = hi_lo(jnp.concatenate(ends, axis=0))
     weigh = jnp.where(lane8 == 40, 16.0, jnp.where(lane8 == 41, 1.0, 0.0)).astype(bf16)
-    slot = mm_nt(weigh, x_ref[:, 256:384].astype(bf16))[0:1, :].astype(jnp.int32)
-    high, low = hi_lo(x_ref[...])
+    slot = mm_nt(weigh, ends_high)[0:1, :].astype(jnp.int32)
+    high, low = hi_lo(jnp.concatenate([upper, lower], axis=1))
+    ends = jnp.concatenate([ends_high, ends_low], axis=1)
     for chunk in range(4):
+        rows = slice(chunk * 128, (chunk + 1) * 128)
         pick = (iota((128, SLOTS), 0) + chunk * 128 == slot).astype(bf16)
-        grid_ref[chunk * 128 : (chunk + 1) * 128, :] = mm(pick, high) + mm(pick, low)
+        grid_ref[rows, 0:256] = mm(pick, high) + mm(pick, low)
+        both = mm(pick, ends)
+        grid_ref[rows, 256:384] = both[:, 0:128] + both[:, 128:256]
 
     group = lane8 // 16
     masks = {d: (group // d) % 2 == 0 for d in (1, 2, 4)}
@@ -425,9 +502,9 @@
     picks = [jnp.asarray(t) for t in picks]
     packed = deposit_and_pack(offsets, lens_weight, counts, owners, brick_slot)
     arrived = lax.all_to_all(
-        packed.reshape(N_DEST, CAP, 384), ("rows", "cols"), split_axis=0, concat_axis=0, tiled=True
+        packed.reshape(N_DEST, MESSAGE // 4, 4, 128), ("rows", "cols"), split_axis=0, concat_axis=0, tiled=True
     )
-    raw, to_left, to_right = place_and_fold(arrived.reshape(SLOTS, 384))
+    raw, to_left, to_right = place_and_fold(arrived.reshape(N_DEST * MESSAGE, 128))
     from_right = shifted(to_left, "cols", -1)
     from_left = shifted(to_right, "cols", 1)
     own, to_up, to_down = first_columns(raw, to_right, from_right, from_left, cols[0])

time: 70.3 us -> 67.8 us (0.964)
  local copies, waits for them, and re-layouts: 1.44 us -> 4.37 us
  blocking collectives: 35.7 us -> 32.9 us
  Pallas kernels: 17.3 us -> 14.6 us
    unnamed x31 -> x32, local copies, waits for them, and re-layouts: 1.44 us -> 4.37 us
    all_to_all x1, blocking collectives: 35.7 us -> 32.9 us  [on_device(): lax.all_to_all(packed.reshape(N_DEST, MESSAGE // 4, 4, 128), ('rows', 'co...]
    pallas_call x1, Pallas kernels: 9.77 us -> 7.19 us  [deposit_and_pack(): pl.pallas_call(deposit_kernel, out_shape=jax.ShapeDtypeStruct((N_DEST * M...]
where the time goes in v2:
time: 67.8 us; the launch traced here: 67.5 us
  blocking collectives  32.9 us (49%)
  Pallas kernels  14.6 us (22%)
  waiting for transfers between devices  12.2 us (18%)
  local copies, waits for them, and re-layouts  4.37 us (6%)
  starting transfers between devices  2.61 us (4%)
  between operations  0.82 us (1%)
    all_to_all x1, blocking collectives, on_device(): lax.all_to_all(packed.reshape(N_DEST, MESSAGE // 4, 4, 128), ('rows', 'co...  32.9 us
    ppermute x4, waiting for transfers between devices, shifted(): return lax.ppermute(x, axis, [(i, (i + by) % size) for i in range(size)])  12.2 us
    pallas_call x1, Pallas kernels, deposit_and_pack(): pl.pallas_call(deposit_kernel, out_shape=jax.ShapeDtypeStruct((N_DEST * M...  7.19 us
    unnamed x32, local copies, waits for them, and re-layouts  4.37 us
    pallas_call x1, Pallas kernels, all_levels(): pl.pallas_call(levels_kernel, out_shape=tuple((jax.ShapeDtypeStruct(shape...  4.33 us
    ppermute x4, starting transfers between devices, shifted(): return lax.ppermute(x, axis, [(i, (i + by) % size) for i in range(size)])  2.61 us
    pallas_call x1, Pallas kernels, place_and_fold(): pl.pallas_call(place_kernel, out_shape=(jax.ShapeDtypeStruct((4 * TILE_RO...  1.88 us
  transfers between devices with their start and end apart: 4, of which 3 were waited for; matrix products, arithmetic and copies ran while one was open for 0% of the time, Pallas kernels for 0%

profile of v2, /device:TPU:0, one launch (start us, length us, event | category | flops | bytes accessed | tf_op | source)
XLA Modules:
  0.0 67.5 jit_solution(16781727497916189460)
XLA Ops:
  0.6 0.0 copy-start.1
  0.6 1.2 %copy-done.1 = f32[512,2,256]{2,1,0:T(2,128)S(1)} copy-done((f32[512,2,256]{2,1,0:T(2,128)S(1)}, f32[512,2,256]{2,1,0:T(2,128)}, u32[]{:S(2)}) %copy-start.1) | copy-done | bytes 1048600
  1.9 0.0 copy-start.4
  1.9 1.0 %copy-done.4 = f32[512,256]{1,0:T(8,128)S(1)} copy-done((f32[512,256]{1,0:T(8,128)S(1)}, f32[512,256]{1,0:T(8,128)}, u32[]{:S(2)}) %copy-start.4) | copy-done | bytes 524312
  2.9 0.0 copy-start.13
  2.9 0.7 %copy-done.13 = s32[512]{0:T(512)S(1)} copy-done((s32[512]{0:T(512)S(1)}, s32[512]{0:T(512)}, u32[]{:S(2)}) %copy-start.13) | copy-done | bytes 2072
  3.6 0.0 copy-start.14
  3.6 0.7 %copy-done.14 = s32[512]{0:T(512)S(1)} copy-done((s32[512]{0:T(512)S(1)}, s32[512]{0:T(512)}, u32[]{:S(2)}) %copy-start.14) | copy-done | bytes 2072
  4.3 0.0 copy-start.15
  4.3 0.7 %copy-done.15 = s32[512]{0:T(512)S(1)} copy-done((s32[512]{0:T(512)S(1)}, s32[512]{0:T(512)}, u32[]{:S(2)}) %copy-start.15) | copy-done | bytes 2072
  4.9 7.2 %deposit.1 = f32[2560,128]{1,0:T(8,128)S(1)} custom-call(f32[2048,128]{1,0:T(8,128)S(1)} %bitcast.12, f32[512,256]{1,0:T(8,128)S(1)} %copy-done.4, s32[1,512]{1,0:T(1,128)S(1)} %bitcast.13, s32[1,512]{1,0:T(1,128)S(1)} %bitcast.14, s32[1,512]{1,0:T(1,128)S(1)} %bitcast.15), custom_call_target="tpu_custom_call" | custom-call | tf_op jit(solution)/shard_map/deposit/pallas_call | solution.py:264
  12.1 0.0 copy-start
  12.2 32.9 %all_to_all.5 = f32[128,5,4,128]{3,2,1,0:T(4,128)S(1)} all-to-all(f32[128,5,4,128]{3,2,1,0:T(4,128)S(1)} %bitcast.11), channel_id=1, replica_groups=mesh['rows'=16,'cols'=8] {'rows','cols'}, dimensions={0} | all-to-all | bytes 2621440 | tf_op jit(solution)/shard_map/all_to_all | solution.py:504
  45.1 1.9 %place.1 = (f32[1088,128]{1,0:T(8,128)S(1)}, f32[272,128]{1,0:T(8,128)S(1)}, f32[272,128]{1,0:T(8,128)S(1)}) custom-call(f32[2560,128]{1,0:T(8,128)S(1)} %bitcast.10), custom_call_target="tpu_custom_call" | custom-call | tf_op jit(solution)/shard_map/place/pallas_call | solution.py:387
  47.0 0.0 collective-permute-start
  47.0 0.5 collective-permute-start.1
  47.5 2.1 %collective-permute-done.from_right_ref = f32[272,128]{1,0:T(8,128)S(1)} collective-permute-done((f32[272,128]{1,0:T(8,128)S(1)}, f32[272,128]{1,0:T(8,128)S(1)}, u32[]{:S(2)}, u32[]{:S(2)}) %collective-permute-start) | collective-permute-done | bytes 139296 | tf_op jit(solution)/shard_map/ppermute | solution.py:495
  49.6 3.1 %collective-permute-done.1.from_left_ref = f32[272,128]{1,0:T(8,128)S(1)} collective-permute-done((f32[272,128]{1,0:T(8,128)S(1)}, f32[272,128]{1,0:T(8,128)S(1)}, u32[]{:S(2)}, u32[]{:S(2)}) %collective-permute-start.1) | collective-permute-done | bytes 139296 | tf_op jit(solution)/shard_map/ppermute | solution.py:495
  52.7 0.0 copy-done
  52.7 0.0 copy-start.2
  52.7 0.0 copy-start.3
  52.7 0.0 copy-start.5
  52.7 0.0 copy-start.6
  52.7 0.0 copy-start.7
  52.7 0.0 copy-start.8
  52.8 0.0 copy-start.9
  52.8 0.0 copy-start.10
  52.8 0.0 copy-start.11
  52.8 0.0 copy-start.12
  52.8 1.2 %columns.1 = (f32[272,768]{1,0:T(8,128)S(1)}, f32[80,768]{1,0:T(8,128)S(1)}, f32[24,768]{1,0:T(8,128)S(1)}) custom-call(f32[1088,128]{1,0:T(8,128)S(1)} %get-tuple-element.11.raw_ref, f32[272,128]{1,0:T(8,128)S(1)} %get-tuple-element.12.to_right_ref, f32[272,128]{1,0:T(8,128)S(1)} %collective-permute-done.from_right_ref, ...), custom_call_target="tpu_custom_call" | custom-call | tf_op jit(solution)/shard_map/columns/pallas_call | solution.py:425
  54.0 1.5 %collective-permute-start.2 = (f32[80,768]{1,0:T(8,128)S(1)}, f32[80,768]{1,0:T(8,128)S(1)}, u32[]{:S(2)}, u32[]{:S(2)}) collective-permute-start(f32[80,768]{1,0:T(8,128)S(1)} %get-tuple-element.15), channel_id=1, source_target_pairs={{0,120},{8,0},{16,8},{24,16},{32,24},{40,32},{48,40},{56,48},{64,5... | collective-permute-start | bytes 737288 | tf_op jit(solution)/shard_map/ppermute | solution.py:495
  55.4 0.6 collective-permute-start.3
  56.1 7.0 %collective-permute-done.3.above_ref = f32[24,768]{1,0:T(8,128)S(1)} collective-permute-done((f32[24,768]{1,0:T(8,128)S(1)}, f32[24,768]{1,0:T(8,128)S(1)}, u32[]{:S(2)}, u32[]{:S(2)}) %collective-permute-start.3) | collective-permute-done | bytes 73760 | tf_op jit(solution)/shard_map/ppermute | solution.py:495
  63.1 0.0 collective-permute-done.2.below_ref
  63.1 0.0 copy-done.2
  63.1 0.0 copy-done.3
  63.1 0.0 copy-done.5
  63.1 0.0 copy-done.6
  63.1 0.0 copy-done.7
  63.2 0.0 copy-done.8
  63.2 0.0 copy-done.9
  63.2 0.0 copy-done.10
  63.2 0.0 copy-done.11
  63.2 0.0 copy-done.12
  63.2 4.3 %levels.1 = (f32[128,256]{1,0:T(8,128)}, f32[64,128]{1,0:T(8,128)}, f32[32,64]{1,0:T(8,128)}, f32[16,32]{1,0:T(8,128)}, f32[16,32]{1,0:T(8,128)}) custom-call(f32[272,768]{1,0:T(8,128)S(1)} %get-tuple-element.14.own_ref, f32[80,768]{1,0:T(8,128)S(1)} %collective-permute-done.2.below_ref, f32[24,768]{1,0:T(8,128)S(1)} %collective-permute-done.3.above_ref, ...), custom_call_target="tpu_custom_call" | custom-call | tf_op jit(solution)/shard_map/levels/pallas_call | solution.py:484
Async XLA Ops:
  0.6 1.2 %copy-start.1 = (f32[512,2,256]{2,1,0:T(2,128)S(1)}, f32[512,2,256]{2,1,0:T(2,128)}, u32[]{:S(2)}) copy-start(f32[512,2,256]{2,1,0:T(2,128)} %param.16) | copy-start | bytes 3145732
  1.9 1.0 %copy-start.4 = (f32[512,256]{1,0:T(8,128)S(1)}, f32[512,256]{1,0:T(8,128)}, u32[]{:S(2)}) copy-start(f32[512,256]{1,0:T(8,128)} %w_hbm.1) | copy-start | bytes 1572868
  2.9 0.7 %copy-start.13 = (s32[512]{0:T(512)S(1)}, s32[512]{0:T(512)}, u32[]{:S(2)}) copy-start(s32[512]{0:T(512)} %param.18) | copy-start | bytes 6148
  3.6 0.7 %copy-start.14 = (s32[512]{0:T(512)S(1)}, s32[512]{0:T(512)}, u32[]{:S(2)}) copy-start(s32[512]{0:T(512)} %param.19) | copy-start | bytes 6148
  4.3 0.7 %copy-start.15 = (s32[512]{0:T(512)S(1)}, s32[512]{0:T(512)}, u32[]{:S(2)}) copy-start(s32[512]{0:T(512)} %param.20) | copy-start | bytes 6148
  12.1 40.6 %copy-start = (bf16[2,768,768]{2,1,0:T(8,128)(2,1)S(1)}, bf16[2,768,768]{2,1,0:T(8,128)(2,1)}, u32[]{:S(2)}) copy-start(bf16[2,768,768]{2,1,0:T(8,128)(2,1)} %constant.22.clone.table_ref) | copy-start | bytes 7077892
  47.0 2.6 %collective-permute-start = (f32[272,128]{1,0:T(8,128)S(1)}, f32[272,128]{1,0:T(8,128)S(1)}, u32[]{:S(2)}, u32[]{:S(2)}) collective-permute-start(f32[272,128]{1,0:T(8,128)S(1)} %get-tuple-element.13), channel_id=1, source_target_pairs={{0,7},{1,0},{2,1},{3,2},{4,3},{5,4},{6,5},{7,6},{8,15},{9,8},{10,9... | collective-permute-start | bytes 417800 | tf_op jit(solution)/shard_map/ppermute | solution.py:495
  47.0 5.7 %collective-permute-start.1 = (f32[272,128]{1,0:T(8,128)S(1)}, f32[272,128]{1,0:T(8,128)S(1)}, u32[]{:S(2)}, u32[]{:S(2)}) collective-permute-start(f32[272,128]{1,0:T(8,128)S(1)} %get-tuple-element.12.to_right_ref), channel_id=1, source_target_pairs={{0,1},{1,2},{2,3},{3,4},{4,5},{5,6},{6,7},{7,0},{8,9},{9,10},{10,1... | collective-permute-start | bytes 417800 | tf_op jit(solution)/shard_map/ppermute | solution.py:495
  52.7 10.4 %copy-start.2 = (bf16[2,384,512]{2,1,0:T(8,128)(2,1)S(1)}, bf16[2,384,512]{2,1,0:T(8,128)(2,1)}, u32[]{:S(2)}) copy-start(bf16[2,384,512]{2,1,0:T(8,128)(2,1)} %constant.23.clone.refs_0_) | copy-start | bytes 2359300
  52.7 10.4 %copy-start.3 = (bf16[2,384,376]{2,1,0:T(8,128)(2,1)S(1)}, bf16[2,384,376]{2,1,0:T(8,128)(2,1)}, u32[]{:S(2)}) copy-start(bf16[2,384,376]{2,1,0:T(8,128)(2,1)} %constant.26.clone.refs_3_) | copy-start | bytes 1732612
  52.7 10.4 %copy-start.5 = (bf16[2,256,256]{2,1,0:T(8,128)(2,1)S(1)}, bf16[2,256,256]{2,1,0:T(8,128)(2,1)}, u32[]{:S(2)}) copy-start(bf16[2,256,256]{2,1,0:T(8,128)(2,1)} %constant.24.clone.refs_1_) | copy-start | bytes 786436
  52.7 10.4 %copy-start.6 = (bf16[384,256]{1,0:T(8,128)(2,1)S(1)}, bf16[384,256]{1,0:T(8,128)(2,1)}, u32[]{:S(2)}) copy-start(bf16[384,256]{1,0:T(8,128)(2,1)} %constant.30.clone.refs_7_) | copy-start | bytes 589828
  52.7 10.4 %copy-start.7 = (bf16[2,192,192]{2,1,0:T(8,128)(2,1)S(1)}, bf16[2,192,192]{2,1,0:T(8,128)(2,1)}, u32[]{:S(2)}) copy-start(bf16[2,192,192]{2,1,0:T(8,128)(2,1)} %constant.27.clone.refs_4_) | copy-start | bytes 442372
  52.7 10.4 %copy-start.8 = (bf16[2,128,256]{2,1,0:T(8,128)(2,1)S(1)}, bf16[2,128,256]{2,1,0:T(8,128)(2,1)}, u32[]{:S(2)}) copy-start(bf16[2,128,256]{2,1,0:T(8,128)(2,1)} %constant.25.clone.refs_2_) | copy-start | bytes 393220
  52.8 10.4 %copy-start.9 = (bf16[256,128]{1,0:T(8,128)(2,1)S(1)}, bf16[256,128]{1,0:T(8,128)(2,1)}, u32[]{:S(2)}) copy-start(bf16[256,128]{1,0:T(8,128)(2,1)} %constant.31.clone.refs_8_) | copy-start | bytes 196612
  52.8 10.4 %copy-start.10 = (bf16[2,96,96]{2,1,0:T(8,128)(2,1)S(1)}, bf16[2,96,96]{2,1,0:T(8,128)(2,1)}, u32[]{:S(2)}) copy-start(bf16[2,96,96]{2,1,0:T(8,128)(2,1)} %constant.28.clone.refs_5_) | copy-start | bytes 110596
  52.8 10.4 %copy-start.11 = (bf16[128,128]{1,0:T(8,128)(2,1)S(1)}, bf16[128,128]{1,0:T(8,128)(2,1)}, u32[]{:S(2)}) copy-start(bf16[128,128]{1,0:T(8,128)(2,1)} %constant.32.clone.refs_9_) | copy-start | bytes 98308
  52.8 10.4 %copy-start.12 = (bf16[2,48,48]{2,1,0:T(8,128)(2,1)S(1)}, bf16[2,48,48]{2,1,0:T(8,128)(2,1)}, u32[]{:S(2)}) copy-start(bf16[2,48,48]{2,1,0:T(8,128)(2,1)} %constant.29.clone.refs_6_) | copy-start | bytes 27652
  54.0 9.1 %collective-permute-start.2 = (f32[80,768]{1,0:T(8,128)S(1)}, f32[80,768]{1,0:T(8,128)S(1)}, u32[]{:S(2)}, u32[]{:S(2)}) collective-permute-start(f32[80,768]{1,0:T(8,128)S(1)} %get-tuple-element.15), channel_id=1, source_target_pairs={{0,120},{8,0},{16,8},{24,16},{32,24},{40,32},{48,40},{56,48},{64,5... | collective-permute-start | bytes 737288 | tf_op jit(solution)/shard_map/ppermute | solution.py:495
  55.4 7.7 %collective-permute-start.3 = (f32[24,768]{1,0:T(8,128)S(1)}, f32[24,768]{1,0:T(8,128)S(1)}, u32[]{:S(2)}, u32[]{:S(2)}) collective-permute-start(f32[24,768]{1,0:T(8,128)S(1)} %get-tuple-element.16), channel_id=1, source_target_pairs={{0,8},{8,16},{16,24},{24,32},{32,40},{40,48},{48,56},{56,64},{64,7... | collective-permute-start | bytes 221192 | tf_op jit(solution)/shard_map/ppermute | solution.py:495

commit v3 on v2

--- a/solution.py
+++ b/solution.py
@@ -78,30 +78,52 @@
     return np.stack([high, low])
 
 
+HALO_ROWS = ((0, 8), (120, 168), (184, 192), (192, 200), (312, 328), (376, 384))
+
+
 @functools.lru_cache(maxsize=1)
 def tables():
     col_spans = spans(C_DEV)
     row_spans = spans(R_DEV)
-    col_src = list(range(C_DEV))
-    col_src += [C_DEV + j if j < 76 else None for j in range(128)]
-    col_src += [0, C_DEV] + [None] * 110 + [j - 16 for j in range(16)]
+    inner = level_table(list(range(384)), 128, (0, 128, 0, 128))
+    right = [C_DEV + j if j < 76 else None for j in range(128)] + [None] * 128
+    mixed = [None] * 128 + list(range(8)) + [None] * 104 + [j - 16 for j in range(16)]
+    room = COL_ROOM[0]
+    beyond = level_table(right, room, (256, 292, 256, 264)) + level_table(mixed, room, (-8, 0, -8, 0))
+    partial = level_table(right, room, (254, 256, 254, 256))
+    outer = np.concatenate(
+        [
+            beyond[:, 256:384],
+            beyond[:, room + 256 : room + 384],
+            partial[:, 128:256],
+            partial[:, room + 128 : room + 256],
+        ],
+        axis=1,
+    )
     row_src = [i if i < 257 else None for i in range(TILE_ROWS)]
     row_src += [R_DEV + i if i < 76 else None for i in range(UP_ROWS)]
     row_src += [i - 16 if i < 17 else None for i in range(DOWN_ROWS)]
     cols, rows = [], []
     for level in range(4):
-        cols.append(level_table(col_src, COL_ROOM[level], col_spans[level]))
+        if level:
+            cols.append(level_table(col_src, COL_ROOM[level], col_spans[level]))
         rows.append(level_table(row_src, ROW_ROOM[level], row_spans[level]).T)
         col_src = room_sources(COL_ROOM[level], col_spans[level][0], col_spans[level][1])
         row_src = room_sources(ROW_ROOM[level], row_spans[level][0], row_spans[level][1])
-    picks = []
-    for level in range(3):
-        _, _, high_from, high_to = col_spans[level + 1]
-        pick = np.zeros((COL_ROOM[level], COL_ROOM[level + 1]), np.float64)
-        for k in range(high_from, high_to):
-            pick[(2 * k) % COL_ROOM[level], k % COL_ROOM[level + 1]] = 1.0
-        picks.append(pick.astype(jnp.bfloat16))
-    return [split(t) for t in cols], [split(t) for t in rows], picks
+    first = rows[0]
+    near = np.concatenate([first[start:stop, TILE_ROWS:] for start, stop in HALO_ROWS], axis=0)
+    rest = np.ones(first.shape[0], bool)
+    for start, stop in HALO_ROWS:
+        rest[start:stop] = False
+    assert not first[rest, TILE_ROWS:].any()
+    return {
+        "inner": split(inner),
+        "outer": split(outer),
+        "own": split(first[:, :TILE_ROWS]),
+        "near": split(near),
+        "cols": [split(t) for t in cols],
+        "rows": [split(t) for t in rows[1:]],
+    }
 
 
 def hi_lo(x):
@@ -280,16 +302,26 @@
         ],
         compiler_params=pltpu.CompilerParams(vmem_limit_bytes=40 << 20),
         name="deposit",
-    )(
+    )(*(pltpu.with_memory_space_constraint(x, pltpu.MemorySpace.HBM) for x in (
         flat,
         weights,
         counts.reshape(1, BRICKS),
         owners.reshape(1, BRICKS),
         slots.reshape(1, BRICKS),
-    )
-
-
-def place_kernel(x_ref, raw_ref, left_ref, right_ref, grid_ref):
+    )))
+
+
+def mm3(data, table):
+    high, low = hi_lo(data)
+    return mm(high, table[0]) + (mm(low, table[0]) + mm(high, table[1]))
+
+
+def mm3_left(table, data):
+    high, low = hi_lo(data)
+    return mm(table[0], high) + (mm(table[0], low) + mm(table[1], high))
+
+
+def place(x_ref, grid_ref, blocks):
     lane8 = iota((8, 128), 1)
     upper = jnp.concatenate([x_ref[pl.ds(rank, N_DEST, stride=MESSAGE), :] for rank in range(8)], axis=0)
     lower = jnp.concatenate([x_ref[pl.ds(8 + rank, N_DEST, stride=MESSAGE), :] for rank in range(8)], axis=0)
@@ -302,125 +334,167 @@
     slot = mm_nt(weigh, ends_high)[0:1, :].astype(jnp.int32)
     high, low = hi_lo(jnp.concatenate([upper, lower], axis=1))
     ends = jnp.concatenate([ends_high, ends_low], axis=1)
-    for chunk in range(4):
-        rows = slice(chunk * 128, (chunk + 1) * 128)
-        pick = (iota((128, SLOTS), 0) + chunk * 128 == slot).astype(bf16)
+    row = iota((128, SLOTS), 0)
+    for at, block in enumerate(blocks):
+        rows = slice(at * 128, (at + 1) * 128)
+        pick = ((row // 16) * 64 + row % 16 + block * 16 == slot).astype(bf16)
         grid_ref[rows, 0:256] = mm(pick, high) + mm(pick, low)
         both = mm(pick, ends)
         grid_ref[rows, 256:384] = both[:, 0:128] + both[:, 128:256]
 
-    group = lane8 // 16
-    masks = {d: (group // d) % 2 == 0 for d in (1, 2, 4)}
-
-    def swap_groups(tiles):
-        for d in (1, 2, 4):
-            new = list(tiles)
-            for a in range(8):
-                if (a // d) % 2 == 0:
-                    one, two = tiles[a], tiles[a + d]
-                    new[a] = jnp.where(masks[d], one, pltpu.roll(two, 16 * d, 1))
-                    new[a + d] = jnp.where(masks[d], pltpu.roll(one, 128 - 16 * d, 1), two)
-            tiles = new
-        return tiles
-
-    def tiles_of(third, across, half):
-        at = across * 16 + half * 8
-        return swap_groups(
-            [grid_ref[low_col * 64 + at : low_col * 64 + at + 8, third * 128 : (third + 1) * 128] for low_col in range(8)]
-        )
-
-    first_lane = lane8 == 0
-    group_start = lane8 % 16 == 0
-    for across in range(4):
-        raw_ref[across * TILE_ROWS + 256 : (across + 1) * TILE_ROWS, :] = jnp.zeros((TILE_ROWS - 256, 128), f32)
-    right_ref[256:TILE_ROWS, :] = jnp.zeros((TILE_ROWS - 256, 128), f32)
-    left_ref[256:TILE_ROWS, :] = jnp.zeros((TILE_ROWS - 256, 128), f32)
-
-    previous = None
-    for across in range(4):
-        rows = [[None, None] for _ in range(17)]
-        turned = [[None, None] for _ in range(17)]
+
+def swap_groups(tiles):
+    group = iota((8, 128), 1) // 16
+    for d in (1, 2, 4):
+        mask = (group // d) % 2 == 0
+        new = list(tiles)
+        for a in range(8):
+            if (a // d) % 2 == 0:
+                one, two = tiles[a], tiles[a + d]
+                new[a] = jnp.where(mask, one, pltpu.roll(two, 16 * d, 1))
+                new[a + d] = jnp.where(mask, pltpu.roll(one, 128 - 16 * d, 1), two)
+        tiles = new
+    return tiles
+
+
+def turn(side, corner):
+    turned = [[pltpu.roll(side[half], 16 - i, 1) for half in range(2)] for i in range(16)]
+    return turned + [[pltpu.roll(corner[half], 16, 1) for half in range(2)]]
+
+
+def unpack_block(grid_ref, at):
+    rows = [[None, None] for _ in range(17)]
+    side, corner = [None, None], [None, None]
+    for half in range(2):
+        parts = []
+        for third in range(3):
+            parts.append(
+                swap_groups(
+                    [
+                        grid_ref[at * 128 + col * 16 + half * 8 : at * 128 + col * 16 + half * 8 + 8, third * 128 : (third + 1) * 128]
+                        for col in range(8)
+                    ]
+                )
+            )
+        for i in range(8):
+            rows[i][half] = parts[0][i]
+            rows[8 + i][half] = parts[1][i]
+        rows[16][half] = parts[2][0]
+        side[half] = parts[2][1]
+        corner[half] = parts[2][2]
+    return rows, side, corner
+
+
+def add_spills(rows, turned, previous):
+    lane8 = iota((8, 128), 1)
+    out = []
+    for i in range(17):
+        pair = []
         for half in range(2):
-            upper = tiles_of(0, across, half)
-            lower = tiles_of(1, across, half)
-            edges = tiles_of(2, across, half)
-            for i in range(8):
-                rows[i][half] = upper[i]
-                rows[8 + i][half] = lower[i]
-            rows[16][half] = edges[0]
-            for i in range(16):
-                turned[i][half] = pltpu.roll(edges[1], 16 - i, 1)
-            turned[16][half] = pltpu.roll(edges[2], 16, 1)
-            for i in range(17):
-                before = jnp.zeros((8, 128), f32) if previous is None else previous[i][half]
-                spill = jnp.where(first_lane, before, jnp.where(group_start, turned[i][half], 0.0))
-                rows[i][half] = rows[i][half] + spill
+            spill = jnp.where(lane8 % 16 == 0, turned[i][half], 0.0)
+            first = 0.0 if previous is None else previous[i][half]
+            pair.append(rows[i][half] + jnp.where(lane8 == 0, first, spill))
+        out.append(pair)
+    return out
+
+
+def store_block(rows, ref):
+    sub = iota((8, 128), 0)
+    down = [pltpu.roll(rows[16][half], 1, 0) for half in range(2)]
+    for i in range(16):
+        low, high = rows[i]
+        if i == 0:
+            low = low + jnp.where(sub == 0, 0.0, down[0])
+            high = high + jnp.where(sub == 0, down[0], down[1])
+        ref[pl.ds(i, 8, stride=16), :] = low
+        ref[pl.ds(128 + i, 8, stride=16), :] = high
+    ref[256:264, :] = jnp.where(sub == 0, down[1], 0.0)
+    ref[264:TILE_ROWS, :] = jnp.zeros((8, 128), f32)
+
+
+def place_edges_kernel(x_ref, first_ref, last_ref, right_ref, carry_ref, grid_ref):
+    place(x_ref, grid_ref, (0, 3))
+    lane8 = iota((8, 128), 1)
+    rows, side, corner = unpack_block(grid_ref, 0)
+    store_block(add_spills(rows, turn(side, corner), None), first_ref)
+    for half in range(2):
+        carry_ref[half * 8 : half * 8 + 8, :] = side[half]
+        carry_ref[16 + half * 8 : 24 + half * 8, :] = corner[half]
+    rows, side, corner = unpack_block(grid_ref, 1)
+    turned = turn(side, corner)
+    rows = add_spills(rows, turned, None)
+    store_block(rows, last_ref)
+    store_block(
+        [[jnp.where(lane8 == 0, turned[i][half], rows[i][half]) for half in range(2)] for i in range(17)], right_ref
+    )
+
+
+def place_edges(arrived):
+    tile = jax.ShapeDtypeStruct((TILE_ROWS, 128), f32)
+    return pl.pallas_call(
+        place_edges_kernel,
+        out_shape=(tile, tile, tile, jax.ShapeDtypeStruct((32, 128), f32)),
+        scratch_shapes=[pltpu.VMEM((256, 384), f32)],
+        compiler_params=pltpu.CompilerParams(vmem_limit_bytes=32 << 20),
+        cost_estimate=pl.CostEstimate(flops=600_000_000, bytes_accessed=2_000_000, transcendentals=0),
+        name="place_edges",
+    )(arrived)
+
+
+def place_inner_kernel(x_ref, carry_ref, first_ref, last_ref, inner_ref, own_ref, grid_ref, second_ref, third_ref, fix_ref):
+    place(x_ref, grid_ref, (1, 2))
+    lane8 = iota((8, 128), 1)
+    previous = turn(
+        [carry_ref[half * 8 : half * 8 + 8, :] for half in range(2)],
+        [carry_ref[16 + half * 8 : 24 + half * 8, :] for half in range(2)],
+    )
+    for at, ref in enumerate((second_ref, third_ref)):
+        rows, side, corner = unpack_block(grid_ref, at)
+        turned = turn(side, corner)
+        store_block(add_spills(rows, turned, previous), ref)
         previous = turned
-        def finish(parts, i, ref, top):
-            if i == 0:
-                down_low = pltpu.roll(parts[16][0], 1, 0)
-                down_high = pltpu.roll(parts[16][1], 1, 0)
-                sub = iota((8, 128), 0)
-                low = parts[0][0] + jnp.where(sub == 0, 0.0, down_low)
-                high_part = parts[0][1] + jnp.where(sub == 0, down_low, down_high)
-                both = (low, high_part)
-                ref[top + 256 : top + 257, :] = parts[16][1][7:8, :]
-            else:
-                both = (parts[i][0], parts[i][1])
-            ref[pl.ds(top + i, 8, stride=16), :] = both[0]
-            ref[pl.ds(top + 128 + i, 8, stride=16), :] = both[1]
-
-        for i in range(16):
-            finish(rows, i, raw_ref, across * TILE_ROWS)
-        if across == 0:
-            for i in range(16):
-                finish(rows, i, left_ref, 0)
-        if across == 3:
-            with_spill = [
-                [jnp.where(first_lane, turned[i][half], rows[i][half]) for half in range(2)] for i in range(17)
-            ]
-            for i in range(16):
-                finish(with_spill, i, right_ref, 0)
-
-
-def place_and_fold(arrived):
+    store_block([[jnp.where(lane8 == 0, previous[i][half], 0.0) for half in range(2)] for i in range(17)], fix_ref)
+    left = jnp.concatenate([first_ref[...], second_ref[...], third_ref[...]], axis=1)
+    right = jnp.concatenate([third_ref[...], last_ref[...] + fix_ref[...]], axis=1)
+    own_ref[:, 0:256] = mm3(left, inner_ref)
+    own_ref[:, 256:512] = mm3(right, inner_ref[:, 0:256, :])
+
+
+def place_inner(arrived, carry, first, last, inner):
+    tile = pltpu.VMEM((TILE_ROWS, 128), f32)
     return pl.pallas_call(
-        place_kernel,
-        out_shape=(
-            jax.ShapeDtypeStruct((4 * TILE_ROWS, 128), f32),
-            jax.ShapeDtypeStruct((TILE_ROWS, 128), f32),
-            jax.ShapeDtypeStruct((TILE_ROWS, 128), f32),
-        ),
-        scratch_shapes=[pltpu.VMEM((BRICKS, 384), f32)],
-        compiler_params=pltpu.CompilerParams(vmem_limit_bytes=40 << 20),
-        name="place",
-    )(arrived)
-
-
-def mm3(data, table_ref):
-    high, low = hi_lo(data)
-    return mm(high, table_ref[0]) + (mm(low, table_ref[0]) + mm(high, table_ref[1]))
-
-
-def mm3_left(table_ref, data):
-    high, low = hi_lo(data)
-    return mm(table_ref[0], high) + (mm(table_ref[0], low) + mm(table_ref[1], high))
-
-
-def columns_kernel(raw_ref, to_right_ref, from_right_ref, from_left_ref, table_ref, out_ref, up_ref, down_ref):
+        place_inner_kernel,
+        out_shape=jax.ShapeDtypeStruct((TILE_ROWS, 512), f32),
+        scratch_shapes=[pltpu.VMEM((256, 384), f32), tile, tile, tile],
+        compiler_params=pltpu.CompilerParams(vmem_limit_bytes=32 << 20),
+        cost_estimate=pl.CostEstimate(flops=800_000_000, bytes_accessed=3_000_000, transcendentals=0),
+        name="place_inner",
+    )(arrived, carry, first, last, inner)
+
+
+def columns_kernel(own_ref, first_ref, to_right_ref, from_right_ref, from_left_ref, outer_ref, out_ref, up_ref, down_ref):
     lane = iota((TILE_ROWS, 128), 1)
-    from_left = jnp.where(lane == 1, pltpu.roll(to_right_ref[...], 1, 1), from_left_ref[...])
-    data = jnp.concatenate(
-        [raw_ref[across * TILE_ROWS : (across + 1) * TILE_ROWS, :] for across in range(4)]
-        + [from_right_ref[...], from_left],
-        axis=1,
-    )
-    out_ref[...] = mm3(data, table_ref)
-    up_ref[...] = out_ref[0:UP_ROWS, :]
-    down_ref[...] = out_ref[DOWN_FROM : DOWN_FROM + DOWN_ROWS, :]
-
-
-def first_columns(raw, to_right, from_right, from_left, table):
+    from_left = from_left_ref[...]
+    spill = jnp.where(lane == 0, from_left, 0.0)
+    right = from_right_ref[...] + jnp.where(lane == 0, to_right_ref[...], 0.0)
+    mixed = jnp.where(lane < 8, first_ref[...] + spill, jnp.where(lane >= 112, from_left, 0.0))
+    outer = mm3(jnp.concatenate([right, mixed], axis=1), outer_ref)
+    pieces = [
+        own_ref[:, 0:128] + taps_low[0] * spill,
+        own_ref[:, 256:384] + outer[:, 256:384],
+        outer[:, 0:128],
+        own_ref[:, 128:256] + taps_high[0] * spill,
+        own_ref[:, 384:512] + outer[:, 384:512],
+        outer[:, 128:256],
+    ]
+    for at, piece in enumerate(pieces):
+        cols = slice(at * 128, (at + 1) * 128)
+        out_ref[:, cols] = piece
+        up_ref[:, cols] = piece[0:UP_ROWS]
+        down_ref[:, cols] = piece[DOWN_FROM : DOWN_FROM + DOWN_ROWS]
+
+
+def outer_columns(own, first, to_right, from_right, from_left, outer):
     width = 2 * COL_ROOM[0]
     return pl.pallas_call(
         columns_kernel,
@@ -429,26 +503,50 @@
             jax.ShapeDtypeStruct((UP_ROWS, width), f32),
             jax.ShapeDtypeStruct((DOWN_ROWS, width), f32),
         ),
-        compiler_params=pltpu.CompilerParams(vmem_limit_bytes=40 << 20),
+        compiler_params=pltpu.CompilerParams(vmem_limit_bytes=32 << 20),
+        cost_estimate=pl.CostEstimate(flops=220_000_000, bytes_accessed=2_000_000, transcendentals=0),
         name="columns",
-    )(raw, to_right, from_right, from_left, table)
-
-
-def levels_kernel(own_ref, below_ref, above_ref, *refs):
+    )(own, first, to_right, from_right, from_left, outer)
+
+
+def own_rows_kernel(own_ref, table_ref, out_ref):
+    for at in range(3):
+        cols = slice(at * 256, (at + 1) * 256)
+        out_ref[:, cols] = mm3_left(table_ref, own_ref[:, cols])
+
+
+def own_rows(own, table):
+    return pl.pallas_call(
+        own_rows_kernel,
+        out_shape=jax.ShapeDtypeStruct((2 * ROW_ROOM[0], 2 * COL_ROOM[0]), f32),
+        compiler_params=pltpu.CompilerParams(vmem_limit_bytes=32 << 20),
+        cost_estimate=pl.CostEstimate(flops=480_000_000, bytes_accessed=2_000_000, transcendentals=0),
+        name="own_rows",
+    )(own, table)
+
+
+def levels_kernel(part_ref, below_ref, above_ref, near_ref, *refs):
     col_refs = (None,) + refs[0:3]
-    row_refs = refs[3:7]
-    pick_refs = refs[7:10]
-    leader_refs = refs[10:14]
-    approx_ref = refs[14]
-    peak_ref = refs[15]
-    current = jnp.concatenate([own_ref[...], below_ref[...], above_ref[...]], axis=0)
+    row_refs = (None,) + refs[3:6]
+    leader_refs = refs[6:10]
+    approx_ref = refs[10]
+    peak_ref = refs[11]
+    near = mm3_left(near_ref, jnp.concatenate([below_ref[...], above_ref[...]], axis=0))
+    pieces = []
+    at, done = 0, 0
+    for start, stop in HALO_ROWS:
+        if start > done:
+            pieces.append(part_ref[done:start, :])
+        pieces.append(part_ref[start:stop, :] + near[at : at + stop - start])
+        at += stop - start
+        done = stop
+    both = jnp.concatenate(pieces, axis=0)
     peak = None
     for level in range(4):
         room_r = ROW_ROOM[level]
         room_c = COL_ROOM[level]
         if level:
-            current = mm3(current, col_refs[level])
-        both = mm3_left(row_refs[level], current)
+            both = mm3_left(row_refs[level], mm3(current, col_refs[level]))
         current = both[:room_r, :room_c]
         detail_a = both[:room_r, room_c:]
         detail_b = both[room_r:, :room_c]
@@ -474,20 +572,23 @@
                     )
                 )
             high, low = hi_lo(jnp.concatenate(pooled, axis=1) if len(pooled) > 1 else pooled[0])
-            pick = pick_refs[level][...]
+            room_n = COL_ROOM[level + 1]
+            out = iota((room_c, room_n), 1)
+            source = 2 * out + jnp.where(out < 3 * room_n // 4, 0, room_c - 2 * room_n)
+            pick = (iota((room_c, room_n), 0) == source).astype(bf16)
             peak = mm(high, pick) + mm(low, pick)
     approx_ref[...] = current[: R_DEV >> 4, : C_DEV >> 4]
 
 
-def all_levels(own, below, above, cols, rows, picks):
+def all_levels(part, below, above, near, cols, rows):
     shapes = [(R_DEV >> level, C_DEV >> level) for level in (1, 2, 3, 4, 4)]
     return pl.pallas_call(
         levels_kernel,
         out_shape=tuple(jax.ShapeDtypeStruct(shape, f32) for shape in shapes),
         scratch_shapes=[pltpu.VMEM((3 * ROW_ROOM[0], 128), f32)],
-        compiler_params=pltpu.CompilerParams(vmem_limit_bytes=48 << 20),
+        compiler_params=pltpu.CompilerParams(vmem_limit_bytes=32 << 20),
         name="levels",
-    )(own, below, above, *cols[1:], *rows, *picks)
+    )(part, below, above, near, *cols, *rows)
 
 
 def shifted(x, axis, by):
@@ -495,22 +596,25 @@
     return lax.ppermute(x, axis, [(i, (i + by) % size) for i in range(size)])
 
 
+def transform(arrived):
+    table = jax.tree.map(jnp.asarray, tables())
+    first, last, to_right, carry = place_edges(arrived)
+    from_right = shifted(first, "cols", -1)
+    from_left = shifted(to_right, "cols", 1)
+    inner = place_inner(arrived, carry, first, last, table["inner"])
+    own, to_up, to_down = outer_columns(inner, first, to_right, from_right, from_left, table["outer"])
+    below = shifted(to_up, "rows", -1)
+    above = shifted(to_down, "rows", 1)
+    part = own_rows(own, table["own"])
+    return all_levels(part, below, above, table["near"], table["cols"], table["rows"])
+
+
 def on_device(offsets, lens_weight, counts, owners, brick_slot):
-    cols, rows, picks = tables()
-    cols = [jnp.asarray(t) for t in cols]
-    rows = [jnp.asarray(t) for t in rows]
-    picks = [jnp.asarray(t) for t in picks]
     packed = deposit_and_pack(offsets, lens_weight, counts, owners, brick_slot)
     arrived = lax.all_to_all(
         packed.reshape(N_DEST, MESSAGE // 4, 4, 128), ("rows", "cols"), split_axis=0, concat_axis=0, tiled=True
     )
-    raw, to_left, to_right = place_and_fold(arrived.reshape(N_DEST * MESSAGE, 128))
-    from_right = shifted(to_left, "cols", -1)
-    from_left = shifted(to_right, "cols", 1)
-    own, to_up, to_down = first_columns(raw, to_right, from_right, from_left, cols[0])
-    below = shifted(to_up, "rows", -1)
-    above = shifted(to_down, "rows", 1)
-    return all_levels(own, below, above, cols, rows, picks)
+    return transform(arrived.reshape(N_DEST * MESSAGE, 128))
 
 
 def solution(mesh):

time: 67.8 us -> 60 us (0.88)
  waiting for transfers between devices: 12.2 us -> 6.48 us
  local copies, waits for them, and re-layouts: 4.37 us -> 0.06 us
  starting transfers between devices: 2.61 us -> 5.06 us
    ppermute x4, waiting for transfers between devices: 12.2 us -> 6.48 us  [shifted(): return lax.ppermute(x, axis, [(i, (i + by) % size) for i in range(size)])]
    unnamed x32 -> x20, local copies, waits for them, and re-layouts: 4.37 us -> 0.06 us
    ppermute x4, starting transfers between devices: 2.61 us -> 5.06 us  [shifted(): return lax.ppermute(x, axis, [(i, (i + by) % size) for i in range(size)])]
    pallas_call x1, Pallas kernels: 4.33 us -> 2.51 us  [all_levels(): pl.pallas_call(levels_kernel, out_shape=tuple((jax.ShapeDtypeStruct(shape...]
    pallas_call x2 -> x4, Pallas kernels: 3.04 us -> 4.48 us  [the longest x1 1.81 us: place_inner(): pl.pallas_call(place_inner_kernel, out_shape=jax.ShapeDtypeStruct((TILE_R...]
  transfers between devices with their start and end apart: 4 -> 4, of which waited for: 3 -> 2; matrix products, arithmetic and copies ran while one was open for 0% -> 0% of each run, Pallas kernels for 0% -> 5%
where the time goes in v3:
time: 60 us; the launch traced here: 59.8 us
  blocking collectives  32.9 us (55%)
  Pallas kernels  14.5 us (24%)
  waiting for transfers between devices  6.48 us (11%)
  starting transfers between devices  5.06 us (8%)
  between operations  0.79 us (1%)
    all_to_all x1, blocking collectives, on_device(): lax.all_to_all(packed.reshape(N_DEST, MESSAGE // 4, 4, 128), ('rows', 'co...  32.9 us
    pallas_call x1, Pallas kernels, deposit_and_pack(): pl.pallas_call(deposit_kernel, out_shape=jax.ShapeDtypeStruct((N_DEST * M...  7.53 us
    ppermute x4, waiting for transfers between devices, shifted(): return lax.ppermute(x, axis, [(i, (i + by) % size) for i in range(size)])  6.48 us
    ppermute x4, starting transfers between devices, shifted(): return lax.ppermute(x, axis, [(i, (i + by) % size) for i in range(size)])  5.06 us
    pallas_call x1, Pallas kernels, all_levels(): pl.pallas_call(levels_kernel, out_shape=tuple((jax.ShapeDtypeStruct(shape...  2.51 us
    pallas_call x1, Pallas kernels, place_inner(): pl.pallas_call(place_inner_kernel, out_shape=jax.ShapeDtypeStruct((TILE_R...  1.81 us
    pallas_call x1, Pallas kernels, place_edges(): pl.pallas_call(place_edges_kernel, out_shape=(tile, tile, tile, jax.Shape...  1.22 us
  transfers between devices with their start and end apart: 4, of which 2 were waited for; matrix products, arithmetic and copies ran while one was open for 0% of the time, Pallas kernels for 5%

profile of v3, /device:TPU:0, one launch (start us, length us, event | category | flops | bytes accessed | tf_op | source)
XLA Modules:
  0.0 59.8 jit_solution(14151917890712896941)
XLA Ops:
  0.6 7.5 %deposit.1 = f32[2560,128]{1,0:T(8,128)S(1)} custom-call(f32[2048,128]{1,0:T(8,128)} %bitcast.13, f32[512,256]{1,0:T(8,128)} %w_hbm.1, s32[1,512]{1,0:T(1,128)} %bitcast.14, s32[1,512]{1,0:T(1,128)} %bitcast.15, s32[1,512]{1,0:T(1,128)} %bitcast.16), custom_call_target="tpu_custom_call" | custom-call | tf_op jit(solution)/shard_map/deposit/pallas_call | solution.py:286
  8.2 32.9 %all_to_all.5 = f32[128,5,4,128]{3,2,1,0:T(4,128)S(1)} all-to-all(f32[128,5,4,128]{3,2,1,0:T(4,128)S(1)} %bitcast.10), channel_id=1, replica_groups=mesh['rows'=16,'cols'=8] {'rows','cols'}, dimensions={0} | all-to-all | bytes 2621440 | tf_op jit(solution)/shard_map/all_to_all | solution.py:614
  41.1 0.0 copy-start.9
  41.1 1.2 %place_edges.1 = (f32[272,128]{1,0:T(8,128)S(1)}, f32[272,128]{1,0:T(8,128)S(1)}, f32[272,128]{1,0:T(8,128)S(1)}, f32[32,128]{1,0:T(8,128)S(1)}) custom-call(f32[2560,128]{1,0:T(8,128)S(1)} %bitcast.11), custom_call_target="tpu_custom_call" | custom-call | flops 600000000 | bytes 2000000 | tf_op jit(solution)/shard_map/place_edges/pallas_call | solution.py:434
  42.3 0.0 collective-permute-start.1
  42.4 2.9 %collective-permute-start = (f32[272,128]{1,0:T(8,128)S(1)}, f32[272,128]{1,0:T(8,128)S(1)}, u32[]{:S(2)}, u32[]{:S(2)}) collective-permute-start(f32[272,128]{1,0:T(8,128)S(1)} %get-tuple-element.13.first_ref), channel_id=1, source_target_pairs={{0,7},{1,0},{2,1},{3,2},{4,3},{5,4},{6,5},{7,6},{8,15},{9,8},{10,9... | collective-permute-start | bytes 417800 | tf_op jit(solution)/shard_map/ppermute | solution.py:596
  45.3 0.0 copy-done.9
  45.3 0.0 copy-start.2
  45.3 1.8 %place_inner.1.own_ref = f32[272,512]{1,0:T(8,128)S(1)} custom-call(f32[2560,128]{1,0:T(8,128)S(1)} %bitcast.12, f32[32,128]{1,0:T(8,128)S(1)} %get-tuple-element.12.carry_ref, f32[272,128]{1,0:T(8,128)S(1)} %get-tuple-element.13.first_ref, f32[272,128]{1,0:T(8,128)S(1)} %get-tuple-element.14.last_ref, bf16[2,384,256]{2,1,0:T(8,128)(2,1)S(1)} %copy-done.9), custom_call_target="tpu_custom_call" | custom-call | flops 800000000 | bytes 3000000 | tf_op jit(solution)/shard_map/place_inner/pallas_call | solution.py:465
  47.1 0.0 copy-start.1
  47.1 0.9 %collective-permute-done.1.from_left_ref = f32[272,128]{1,0:T(8,128)S(1)} collective-permute-done((f32[272,128]{1,0:T(8,128)S(1)}, f32[272,128]{1,0:T(8,128)S(1)}, u32[]{:S(2)}, u32[]{:S(2)}) %collective-permute-start.1) | collective-permute-done | bytes 139296 | tf_op jit(solution)/shard_map/ppermute | solution.py:596
  48.0 0.0 collective-permute-done.from_right_ref
  48.0 0.0 copy-done.2
  48.0 0.4 columns.1
  48.4 0.0 copy-start
  48.5 0.0 copy-start.3
  48.5 0.0 copy-start.4
  48.5 0.0 copy-start.5
  48.5 0.0 copy-start.6
  48.5 0.0 copy-start.7
  48.5 0.0 copy-start.8
  48.5 1.1 %collective-permute-start.2 = (f32[80,768]{1,0:T(8,128)S(1)}, f32[80,768]{1,0:T(8,128)S(1)}, u32[]{:S(2)}, u32[]{:S(2)}) collective-permute-start(f32[80,768]{1,0:T(8,128)S(1)} %get-tuple-element.17), channel_id=1, source_target_pairs={{0,120},{8,0},{16,8},{24,16},{32,24},{40,32},{48,40},{56,48},{64,5... | collective-permute-start | bytes 737288 | tf_op jit(solution)/shard_map/ppermute | solution.py:596
  49.6 1.0 %collective-permute-start.3 = (f32[24,768]{1,0:T(8,128)S(1)}, f32[24,768]{1,0:T(8,128)S(1)}, u32[]{:S(2)}, u32[]{:S(2)}) collective-permute-start(f32[24,768]{1,0:T(8,128)S(1)} %get-tuple-element.18), channel_id=1, source_target_pairs={{0,8},{8,16},{16,24},{24,32},{32,40},{40,48},{48,56},{56,64},{64,7... | collective-permute-start | bytes 221192 | tf_op jit(solution)/shard_map/ppermute | solution.py:596
  50.6 0.0 copy-done.1
  50.6 1.1 %own_rows.1.part_ref = f32[384,768]{1,0:T(8,128)S(1)} custom-call(f32[272,768]{1,0:T(8,128)S(1)} %get-tuple-element.16.own_ref, bf16[2,384,272]{2,1,0:T(8,128)(2,1)S(1)} %copy-done.1), custom_call_target="tpu_custom_call" | custom-call | flops 480000000 | bytes 2000000 | tf_op jit(solution)/shard_map/own_rows/pallas_call | solution.py:519
  51.7 5.6 %collective-permute-done.3.above_ref = f32[24,768]{1,0:T(8,128)S(1)} collective-permute-done((f32[24,768]{1,0:T(8,128)S(1)}, f32[24,768]{1,0:T(8,128)S(1)}, u32[]{:S(2)}, u32[]{:S(2)}) %collective-permute-start.3) | collective-permute-done | bytes 73760 | tf_op jit(solution)/shard_map/ppermute | solution.py:596
  57.3 0.0 collective-permute-done.2.below_ref
  57.3 0.0 copy-done
  57.3 0.0 copy-done.3
  57.3 0.0 copy-done.4
  57.3 0.0 copy-done.5
  57.3 0.0 copy-done.6
  57.3 0.0 copy-done.7
  57.3 0.0 copy-done.8
  57.3 2.5 %levels.1 = (f32[128,256]{1,0:T(8,128)}, f32[64,128]{1,0:T(8,128)}, f32[32,64]{1,0:T(8,128)}, f32[16,32]{1,0:T(8,128)}, f32[16,32]{1,0:T(8,128)}) custom-call(f32[384,768]{1,0:T(8,128)S(1)} %own_rows.1.part_ref, f32[80,768]{1,0:T(8,128)S(1)} %collective-permute-done.2.below_ref, f32[24,768]{1,0:T(8,128)S(1)} %collective-permute-done.3.above_ref, ...), custom_call_target="tpu_custom_call" | custom-call | tf_op jit(solution)/shard_map/levels/pallas_call | solution.py:585
Async XLA Ops:
  41.1 4.2 %copy-start.9 = (bf16[2,384,256]{2,1,0:T(8,128)(2,1)S(1)}, bf16[2,384,256]{2,1,0:T(8,128)(2,1)}, u32[]{:S(2)}) copy-start(bf16[2,384,256]{2,1,0:T(8,128)(2,1)} %constant.23.clone.inner_ref) | copy-start | bytes 1179652
  42.3 5.7 %collective-permute-start.1 = (f32[272,128]{1,0:T(8,128)S(1)}, f32[272,128]{1,0:T(8,128)S(1)}, u32[]{:S(2)}, u32[]{:S(2)}) collective-permute-start(f32[272,128]{1,0:T(8,128)S(1)} %get-tuple-element.15.to_right_ref), channel_id=1, source_target_pairs={{0,1},{1,2},{2,3},{3,4},{4,5},{5,6},{6,7},{7,0},{8,9},{9,10},{10,1... | collective-permute-start | bytes 417800 | tf_op jit(solution)/shard_map/ppermute | solution.py:596
  42.4 5.7 %collective-permute-start = (f32[272,128]{1,0:T(8,128)S(1)}, f32[272,128]{1,0:T(8,128)S(1)}, u32[]{:S(2)}, u32[]{:S(2)}) collective-permute-start(f32[272,128]{1,0:T(8,128)S(1)} %get-tuple-element.13.first_ref), channel_id=1, source_target_pairs={{0,7},{1,0},{2,1},{3,2},{4,3},{5,4},{6,5},{7,6},{8,15},{9,8},{10,9... | collective-permute-start | bytes 417800 | tf_op jit(solution)/shard_map/ppermute | solution.py:596
  45.3 2.7 %copy-start.2 = (bf16[2,256,512]{2,1,0:T(8,128)(2,1)S(1)}, bf16[2,256,512]{2,1,0:T(8,128)(2,1)}, u32[]{:S(2)}) copy-start(bf16[2,256,512]{2,1,0:T(8,128)(2,1)} %constant.25.clone.outer_ref) | copy-start | bytes 1572868
  47.1 3.5 %copy-start.1 = (bf16[2,384,272]{2,1,0:T(8,128)(2,1)S(1)}, bf16[2,384,272]{2,1,0:T(8,128)(2,1)}, u32[]{:S(2)}) copy-start(bf16[2,384,272]{2,1,0:T(8,128)(2,1)} %constant.26.clone.table_ref) | copy-start | bytes 1253380
  48.4 8.8 %copy-start = (bf16[2,384,512]{2,1,0:T(8,128)(2,1)S(1)}, bf16[2,384,512]{2,1,0:T(8,128)(2,1)}, u32[]{:S(2)}) copy-start(bf16[2,384,512]{2,1,0:T(8,128)(2,1)} %constant.20.clone.refs_0_) | copy-start | bytes 2359300
  48.5 8.8 %copy-start.3 = (bf16[2,256,256]{2,1,0:T(8,128)(2,1)S(1)}, bf16[2,256,256]{2,1,0:T(8,128)(2,1)}, u32[]{:S(2)}) copy-start(bf16[2,256,256]{2,1,0:T(8,128)(2,1)} %constant.21.clone.refs_1_) | copy-start | bytes 786436
  48.5 8.8 %copy-start.4 = (bf16[2,192,192]{2,1,0:T(8,128)(2,1)S(1)}, bf16[2,192,192]{2,1,0:T(8,128)(2,1)}, u32[]{:S(2)}) copy-start(bf16[2,192,192]{2,1,0:T(8,128)(2,1)} %constant.27.clone.refs_3_) | copy-start | bytes 442372
  48.5 8.8 %copy-start.5 = (bf16[2,128,256]{2,1,0:T(8,128)(2,1)S(1)}, bf16[2,128,256]{2,1,0:T(8,128)(2,1)}, u32[]{:S(2)}) copy-start(bf16[2,128,256]{2,1,0:T(8,128)(2,1)} %constant.22.clone.refs_2_) | copy-start | bytes 393220
  48.5 8.8 %copy-start.6 = (bf16[2,96,96]{2,1,0:T(8,128)(2,1)S(1)}, bf16[2,96,96]{2,1,0:T(8,128)(2,1)}, u32[]{:S(2)}) copy-start(bf16[2,96,96]{2,1,0:T(8,128)(2,1)} %constant.28.clone.refs_4_) | copy-start | bytes 110596
  48.5 8.8 %copy-start.7 = (bf16[2,96,104]{2,1,0:T(8,128)(2,1)S(1)}, bf16[2,96,104]{2,1,0:T(8,128)(2,1)}, u32[]{:S(2)}) copy-start(bf16[2,96,104]{2,1,0:T(8,128)(2,1)} %constant.24.clone.near_ref) | copy-start | bytes 119812
  48.5 8.8 %copy-start.8 = (bf16[2,48,48]{2,1,0:T(8,128)(2,1)S(1)}, bf16[2,48,48]{2,1,0:T(8,128)(2,1)}, u32[]{:S(2)}) copy-start(bf16[2,48,48]{2,1,0:T(8,128)(2,1)} %constant.29.clone.refs_5_) | copy-start | bytes 27652
  48.5 8.7 %collective-permute-start.2 = (f32[80,768]{1,0:T(8,128)S(1)}, f32[80,768]{1,0:T(8,128)S(1)}, u32[]{:S(2)}, u32[]{:S(2)}) collective-permute-start(f32[80,768]{1,0:T(8,128)S(1)} %get-tuple-element.17), channel_id=1, source_target_pairs={{0,120},{8,0},{16,8},{24,16},{32,24},{40,32},{48,40},{56,48},{64,5... | collective-permute-start | bytes 737288 | tf_op jit(solution)/shard_map/ppermute | solution.py:596
  49.6 7.7 %collective-permute-start.3 = (f32[24,768]{1,0:T(8,128)S(1)}, f32[24,768]{1,0:T(8,128)S(1)}, u32[]{:S(2)}, u32[]{:S(2)}) collective-permute-start(f32[24,768]{1,0:T(8,128)S(1)} %get-tuple-element.18), channel_id=1, source_target_pairs={{0,8},{8,16},{16,24},{24,32},{32,40},{40,48},{48,56},{56,64},{64,7... | collective-permute-start | bytes 221192 | tf_op jit(solution)/shard_map/ppermute | solution.py:596

commit v4 on v3

--- a/solution.py
+++ b/solution.py
@@ -103,19 +103,24 @@
     row_src = [i if i < 257 else None for i in range(TILE_ROWS)]
     row_src += [R_DEV + i if i < 76 else None for i in range(UP_ROWS)]
     row_src += [i - 16 if i < 17 else None for i in range(DOWN_ROWS)]
-    cols, rows = [], []
+    third = [256 + j if j < 36 else j - 128 if j >= 120 else None for j in range(128)] + [None] * 128
+    room = COL_ROOM[1]
+    rest = level_table(third, room, col_spans[1])
+    rest += level_table([None] * 128 + list(range(8)) + [None] * 120, room, (-4, 0, -4, 0))
+    rest = np.concatenate([rest[:, 128:256], rest[:, room + 128 : room + 256]], axis=1)
+    cols, rows = [rest], []
     for level in range(4):
-        if level:
+        if level > 1:
             cols.append(level_table(col_src, COL_ROOM[level], col_spans[level]))
         rows.append(level_table(row_src, ROW_ROOM[level], row_spans[level]).T)
         col_src = room_sources(COL_ROOM[level], col_spans[level][0], col_spans[level][1])
         row_src = room_sources(ROW_ROOM[level], row_spans[level][0], row_spans[level][1])
     first = rows[0]
     near = np.concatenate([first[start:stop, TILE_ROWS:] for start, stop in HALO_ROWS], axis=0)
-    rest = np.ones(first.shape[0], bool)
+    far = np.ones(first.shape[0], bool)
     for start, stop in HALO_ROWS:
-        rest[start:stop] = False
-    assert not first[rest, TILE_ROWS:].any()
+        far[start:stop] = False
+    assert not first[far, TILE_ROWS:].any()
     return {
         "inner": split(inner),
         "outer": split(outer),
@@ -144,8 +149,7 @@
     return lax.broadcasted_iota(jnp.int32, shape, dim)
 
 
-GROUPS_PER_STEP = 16
-STEPS = BRICKS // 8 // GROUPS_PER_STEP
+STEPS = 4
 STEP_BRICKS = BRICKS // STEPS
 MESSAGE = 20
 
@@ -216,50 +220,61 @@
     particle = iota((8, PMAX), 1).astype(f32)
     cell = iota((16, PMAX), 0).astype(f32)
 
-    def hat(x, at):
-        return jnp.maximum(0.0, 1.0 - jnp.abs(x - at))
+    zero = jnp.zeros((), bf16)
+    bit = {at: (lane >> at) % 2 == 1 for at in (3, 4, 5, 6)}
+
+    def choose(tiles, mask):
+        return [jnp.where(mask, odd, even) for even, odd in zip(tiles[0::2], tiles[1::2])]
 
     def one_group(start):
-        first = pl.multiple_of(start * 4, 32)
+        first = start * 4
         rows_at = jnp.concatenate([off_ref[pl.ds(first + 2 * half, 8, stride=4), :] for half in range(2)], axis=1)
         cols_at = jnp.concatenate([off_ref[pl.ds(first + 2 * half + 1, 8, stride=4), :] for half in range(2)], axis=1)
         count = cnt_ref[pl.ds(start, 8), 0:128]
         count = jnp.concatenate([count, count], axis=1)
         weight = jnp.where(particle < count, w_ref[pl.ds(start, 8), :], 0.0)
-        left = jnp.concatenate([hat(rows_at, float(i)) * weight for i in range(17)], axis=0).astype(bf16)
-        right = [hat(cols_at[(8 - g) % 8 : (8 - g) % 8 + 1, :], cell) for g in range(8)]
-        last = hat(cols_at, 16.0)
-        right = jnp.concatenate(right + [last] * 16, axis=0).astype(bf16)
-        full = mm_nt(left, right)
+        lag = rows_at * weight
+        left = []
+        for i in range(17):
+            left.append(weight - jnp.abs(lag))
+            lag = lag - weight
+        left = jnp.maximum(jnp.concatenate(left, axis=0).astype(bf16), zero)
+        right = []
+        for g in range(8):
+            at = first + 4 * ((8 - g) % 8) + 1
+            column = jnp.concatenate([off_ref[pl.ds(at + 2 * half, 8, stride=0), :] for half in range(2)], axis=1)
+            right += [1.0 - jnp.abs(column - cell[0:8]), 1.0 - jnp.abs(column - cell[8:16])]
+        last = cols_at - 15.0
+        right = [jnp.maximum(jnp.concatenate(right, axis=0).astype(bf16), zero)]
+        right += [jnp.maximum(jnp.concatenate([last, last], axis=0).astype(bf16), zero)] * 8
+        full = mm_nt(left, jnp.concatenate(right, axis=0))
         halves = []
         for half in range(2):
-            acc = None
+            pairs = []
             for pair in range(4):
                 at = (half * 8 + pair * 2) * 8
                 even = pltpu.roll(full[at : at + 8, 0:128], 0, 1, stride=16, stride_axis=0)
                 odd = pltpu.roll(full[at + 8 : at + 16, 0:128], 16, 1, stride=16, stride_axis=0)
-                both = jnp.where(lane // 16 == 0, even, odd)
-                acc = both if pair == 0 else jnp.where(lane // 32 == pair, pltpu.roll(both, 32 * pair, 1), acc)
-            halves.append(acc)
+                both = jnp.where(bit[4], odd, even)
+                pairs.append(pltpu.roll(both, 32 * pair, 1) if pair else both)
+            halves.append(choose(choose(pairs, bit[5]), bit[6])[0])
         bottom = pltpu.roll(full[128:136, 0:128], 0, 1, stride=16, stride_axis=0)
         corner = jnp.sum(jnp.where(lane == sub, full[128:136, 128:256], 0.0), axis=1, keepdims=True)
         third = jnp.where(lane < 16, bottom, jnp.where(lane == 32, corner, 0.0))
-        edge = jnp.zeros((8, 128), f32)
-        for i in range(16):
-            edge = jnp.where(lane == 8 * i + sub, full[8 * i : 8 * i + 8, 128:256], edge)
+        edge = [full[8 * i : 8 * i + 8, 128:256] for i in range(16)]
+        for at in range(3, 7):
+            edge = choose(edge, bit[at])
+        edge = jnp.where(lane % 8 == sub, edge[0], 0.0)
         patch_ref[pl.ds(start, 8), 0:128] = halves[0]
         patch_ref[pl.ds(start, 8), 128:256] = halves[1]
         patch_ref[pl.ds(start, 8), 256:384] = third + cnt_ref[pl.ds(start, 8), 128:256]
         edge_ref[pl.ds(start, 8), :] = edge
 
-    def step(index, carry):
+    for index in range(STEPS):
         for copy in fetch(index):
             copy.wait()
-        for sub_group in range(GROUPS_PER_STEP):
-            one_group(pl.multiple_of((index * GROUPS_PER_STEP + sub_group) * 8, 8))
-        return carry
-
-    lax.fori_loop(0, STEPS, step, 0)
+    for group in range(BRICKS // 8):
+        one_group(group * 8)
 
     gather = (iota((128, 128), 1) == iota((128, 128), 0) // 8 + 16).astype(bf16)
     edge_high, edge_low = hi_lo(edge_ref[...])
@@ -525,7 +540,7 @@
     )(own, table)
 
 
-def levels_kernel(part_ref, below_ref, above_ref, near_ref, *refs):
+def levels_kernel(part_ref, below_ref, above_ref, near_ref, inner_ref, *refs):
     col_refs = (None,) + refs[0:3]
     row_refs = (None,) + refs[3:6]
     leader_refs = refs[6:10]
@@ -545,7 +560,12 @@
     for level in range(4):
         room_r = ROW_ROOM[level]
         room_c = COL_ROOM[level]
-        if level:
+        if level == 1:
+            main = mm3(current, inner_ref)
+            rest = mm3(jnp.concatenate([current[:, 256:384], current[:, 0:128]], axis=1), col_refs[1])
+            parts = (main[:, 0:128], rest[:, 0:128], main[:, 128:256], rest[:, 128:256])
+            both = mm3_left(row_refs[1], jnp.concatenate(parts, axis=1))
+        elif level:
             both = mm3_left(row_refs[level], mm3(current, col_refs[level]))
         current = both[:room_r, :room_c]
         detail_a = both[:room_r, room_c:]
@@ -580,7 +600,7 @@
     approx_ref[...] = current[: R_DEV >> 4, : C_DEV >> 4]
 
 
-def all_levels(part, below, above, near, cols, rows):
+def all_levels(part, below, above, near, inner, cols, rows):
     shapes = [(R_DEV >> level, C_DEV >> level) for level in (1, 2, 3, 4, 4)]
     return pl.pallas_call(
         levels_kernel,
@@ -588,7 +608,7 @@
         scratch_shapes=[pltpu.VMEM((3 * ROW_ROOM[0], 128), f32)],
         compiler_params=pltpu.CompilerParams(vmem_limit_bytes=32 << 20),
         name="levels",
-    )(part, below, above, near, *cols, *rows)
+    )(part, below, above, near, inner, *cols, *rows)
 
 
 def shifted(x, axis, by):
@@ -606,7 +626,7 @@
     below = shifted(to_up, "rows", -1)
     above = shifted(to_down, "rows", 1)
     part = own_rows(own, table["own"])
-    return all_levels(part, below, above, table["near"], table["cols"], table["rows"])
+    return all_levels(part, below, above, table["near"], table["inner"], table["cols"], table["rows"])
 
 
 def on_device(offsets, lens_weight, counts, owners, brick_slot):

time: 60 us -> 58.8 us (0.980)
  Pallas kernels: 14.5 us -> 13.3 us
    pallas_call x1, Pallas kernels: 7.53 us -> 6.09 us  [deposit_and_pack(): pl.pallas_call(deposit_kernel, out_shape=jax.ShapeDtypeStruct((N_DEST * M...]
where the time goes in v4:
time: 58.8 us; the launch traced here: 58.6 us
  blocking collectives  32.9 us (56%)
  Pallas kernels  13.3 us (23%)
  waiting for transfers between devices  6.49 us (11%)
  starting transfers between devices  5.06 us (9%)
  between operations  0.79 us (1%)
    all_to_all x1, blocking collectives, on_device(): lax.all_to_all(packed.reshape(N_DEST, MESSAGE // 4, 4, 128), ('rows', 'co...  32.9 us
    ppermute x4, waiting for transfers between devices, shifted(): return lax.ppermute(x, axis, [(i, (i + by) % size) for i in range(size)])  6.49 us
    pallas_call x1, Pallas kernels, deposit_and_pack(): pl.pallas_call(deposit_kernel, out_shape=jax.ShapeDtypeStruct((N_DEST * M...  6.09 us
    ppermute x4, starting transfers between devices, shifted(): return lax.ppermute(x, axis, [(i, (i + by) % size) for i in range(size)])  5.06 us
    pallas_call x1, Pallas kernels, all_levels(): pl.pallas_call(levels_kernel, out_shape=tuple((jax.ShapeDtypeStruct(shape...  2.75 us
    pallas_call x1, Pallas kernels, place_inner(): pl.pallas_call(place_inner_kernel, out_shape=jax.ShapeDtypeStruct((TILE_R...  1.8 us
    pallas_call x1, Pallas kernels, place_edges(): pl.pallas_call(place_edges_kernel, out_shape=(tile, tile, tile, jax.Shape...  1.22 us
  transfers between devices with their start and end apart: 4, of which 2 were waited for; matrix products, arithmetic and copies ran while one was open for 0% of the time, Pallas kernels for 5%

profile of v4, /device:TPU:0, one launch (start us, length us, event | category | flops | bytes accessed | tf_op | source)
XLA Modules:
  0.0 58.6 jit_solution(996342613380940836)
XLA Ops:
  0.6 6.1 %deposit.1 = f32[2560,128]{1,0:T(8,128)S(1)} custom-call(f32[2048,128]{1,0:T(8,128)} %bitcast.13, f32[512,256]{1,0:T(8,128)} %w_hbm.1, s32[1,512]{1,0:T(1,128)} %bitcast.14, s32[1,512]{1,0:T(1,128)} %bitcast.15, s32[1,512]{1,0:T(1,128)} %bitcast.16), custom_call_target="tpu_custom_call" | custom-call | tf_op jit(solution)/shard_map/deposit/pallas_call | solution.py:301
  6.7 32.9 %all_to_all.5 = f32[128,5,4,128]{3,2,1,0:T(4,128)S(1)} all-to-all(f32[128,5,4,128]{3,2,1,0:T(4,128)S(1)} %bitcast.10), channel_id=1, replica_groups=mesh['rows'=16,'cols'=8] {'rows','cols'}, dimensions={0} | all-to-all | bytes 2621440 | tf_op jit(solution)/shard_map/all_to_all | solution.py:634
  39.7 0.0 copy-start.2
  39.7 1.2 %place_edges.1 = (f32[272,128]{1,0:T(8,128)S(1)}, f32[272,128]{1,0:T(8,128)S(1)}, f32[272,128]{1,0:T(8,128)S(1)}, f32[32,128]{1,0:T(8,128)S(1)}) custom-call(f32[2560,128]{1,0:T(8,128)S(1)} %bitcast.11), custom_call_target="tpu_custom_call" | custom-call | flops 600000000 | bytes 2000000 | tf_op jit(solution)/shard_map/place_edges/pallas_call | solution.py:449
  40.9 0.0 collective-permute-start.1
  40.9 2.9 %collective-permute-start = (f32[272,128]{1,0:T(8,128)S(1)}, f32[272,128]{1,0:T(8,128)S(1)}, u32[]{:S(2)}, u32[]{:S(2)}) collective-permute-start(f32[272,128]{1,0:T(8,128)S(1)} %get-tuple-element.13.first_ref), channel_id=1, source_target_pairs={{0,7},{1,0},{2,1},{3,2},{4,3},{5,4},{6,5},{7,6},{8,15},{9,8},{10,9... | collective-permute-start | bytes 417800 | tf_op jit(solution)/shard_map/ppermute | solution.py:616
  43.9 0.0 copy-done.2
  43.9 0.0 copy-start.1
  43.9 1.8 %place_inner.1.own_ref = f32[272,512]{1,0:T(8,128)S(1)} custom-call(f32[2560,128]{1,0:T(8,128)S(1)} %bitcast.12, f32[32,128]{1,0:T(8,128)S(1)} %get-tuple-element.12.carry_ref, f32[272,128]{1,0:T(8,128)S(1)} %get-tuple-element.13.first_ref, f32[272,128]{1,0:T(8,128)S(1)} %get-tuple-element.14.last_ref, bf16[2,384,256]{2,1,0:T(8,128)(2,1)S(1)} %copy-done.2), custom_call_target="tpu_custom_call" | custom-call | flops 800000000 | bytes 3000000 | tf_op jit(solution)/shard_map/place_inner/pallas_call | solution.py:480
  45.7 0.0 copy-start
  45.7 0.9 %collective-permute-done.1.from_left_ref = f32[272,128]{1,0:T(8,128)S(1)} collective-permute-done((f32[272,128]{1,0:T(8,128)S(1)}, f32[272,128]{1,0:T(8,128)S(1)}, u32[]{:S(2)}, u32[]{:S(2)}) %collective-permute-start.1) | collective-permute-done | bytes 139296 | tf_op jit(solution)/shard_map/ppermute | solution.py:616
  46.6 0.0 collective-permute-done.from_right_ref
  46.6 0.0 copy-done.1
  46.6 0.4 columns.1
  47.0 0.0 copy-start.3
  47.0 0.0 copy-start.4
  47.0 0.0 copy-start.5
  47.0 0.0 copy-start.6
  47.1 0.0 copy-start.7
  47.1 0.0 copy-start.8
  47.1 0.0 copy-start.9
  47.1 1.1 %collective-permute-start.2 = (f32[80,768]{1,0:T(8,128)S(1)}, f32[80,768]{1,0:T(8,128)S(1)}, u32[]{:S(2)}, u32[]{:S(2)}) collective-permute-start(f32[80,768]{1,0:T(8,128)S(1)} %get-tuple-element.17), channel_id=1, source_target_pairs={{0,120},{8,0},{16,8},{24,16},{32,24},{40,32},{48,40},{56,48},{64,5... | collective-permute-start | bytes 737288 | tf_op jit(solution)/shard_map/ppermute | solution.py:616
  48.2 1.0 %collective-permute-start.3 = (f32[24,768]{1,0:T(8,128)S(1)}, f32[24,768]{1,0:T(8,128)S(1)}, u32[]{:S(2)}, u32[]{:S(2)}) collective-permute-start(f32[24,768]{1,0:T(8,128)S(1)} %get-tuple-element.18), channel_id=1, source_target_pairs={{0,8},{8,16},{16,24},{24,32},{32,40},{40,48},{48,56},{56,64},{64,7... | collective-permute-start | bytes 221192 | tf_op jit(solution)/shard_map/ppermute | solution.py:616
  49.2 0.0 copy-done
  49.2 1.1 %own_rows.1.part_ref = f32[384,768]{1,0:T(8,128)S(1)} custom-call(f32[272,768]{1,0:T(8,128)S(1)} %get-tuple-element.16.own_ref, bf16[2,384,272]{2,1,0:T(8,128)(2,1)S(1)} %copy-done), custom_call_target="tpu_custom_call" | custom-call | flops 480000000 | bytes 2000000 | tf_op jit(solution)/shard_map/own_rows/pallas_call | solution.py:534
  50.3 5.6 %collective-permute-done.3.above_ref = f32[24,768]{1,0:T(8,128)S(1)} collective-permute-done((f32[24,768]{1,0:T(8,128)S(1)}, f32[24,768]{1,0:T(8,128)S(1)}, u32[]{:S(2)}, u32[]{:S(2)}) %collective-permute-start.3) | collective-permute-done | bytes 73760 | tf_op jit(solution)/shard_map/ppermute | solution.py:616
  55.8 0.0 collective-permute-done.2.below_ref
  55.8 0.0 copy-done.3
  55.8 0.0 copy-done.4
  55.8 0.0 copy-done.5
  55.9 0.0 copy-done.6
  55.9 0.0 copy-done.7
  55.9 0.0 copy-done.8
  55.9 0.0 copy-done.9
  55.9 2.7 %levels.1 = (f32[128,256]{1,0:T(8,128)}, f32[64,128]{1,0:T(8,128)}, f32[32,64]{1,0:T(8,128)}, f32[16,32]{1,0:T(8,128)}, f32[16,32]{1,0:T(8,128)}) custom-call(f32[384,768]{1,0:T(8,128)S(1)} %own_rows.1.part_ref, f32[80,768]{1,0:T(8,128)S(1)} %collective-permute-done.2.below_ref, f32[24,768]{1,0:T(8,128)S(1)} %collective-permute-done.3.above_ref, ...), custom_call_target="tpu_custom_call" | custom-call | tf_op jit(solution)/shard_map/levels/pallas_call | solution.py:605
Async XLA Ops:
  39.7 4.2 %copy-start.2 = (bf16[2,384,256]{2,1,0:T(8,128)(2,1)S(1)}, bf16[2,384,256]{2,1,0:T(8,128)(2,1)}, u32[]{:S(2)}) copy-start(bf16[2,384,256]{2,1,0:T(8,128)(2,1)} %constant.23.clone.inner_ref) | copy-start | bytes 1179652
  40.9 5.7 %collective-permute-start.1 = (f32[272,128]{1,0:T(8,128)S(1)}, f32[272,128]{1,0:T(8,128)S(1)}, u32[]{:S(2)}, u32[]{:S(2)}) collective-permute-start(f32[272,128]{1,0:T(8,128)S(1)} %get-tuple-element.15.to_right_ref), channel_id=1, source_target_pairs={{0,1},{1,2},{2,3},{3,4},{4,5},{5,6},{6,7},{7,0},{8,9},{9,10},{10,1... | collective-permute-start | bytes 417800 | tf_op jit(solution)/shard_map/ppermute | solution.py:616
  40.9 5.7 %collective-permute-start = (f32[272,128]{1,0:T(8,128)S(1)}, f32[272,128]{1,0:T(8,128)S(1)}, u32[]{:S(2)}, u32[]{:S(2)}) collective-permute-start(f32[272,128]{1,0:T(8,128)S(1)} %get-tuple-element.13.first_ref), channel_id=1, source_target_pairs={{0,7},{1,0},{2,1},{3,2},{4,3},{5,4},{6,5},{7,6},{8,15},{9,8},{10,9... | collective-permute-start | bytes 417800 | tf_op jit(solution)/shard_map/ppermute | solution.py:616
  43.9 2.7 %copy-start.1 = (bf16[2,256,512]{2,1,0:T(8,128)(2,1)S(1)}, bf16[2,256,512]{2,1,0:T(8,128)(2,1)}, u32[]{:S(2)}) copy-start(bf16[2,256,512]{2,1,0:T(8,128)(2,1)} %constant.25.clone.outer_ref) | copy-start | bytes 1572868
  45.7 3.5 %copy-start = (bf16[2,384,272]{2,1,0:T(8,128)(2,1)S(1)}, bf16[2,384,272]{2,1,0:T(8,128)(2,1)}, u32[]{:S(2)}) copy-start(bf16[2,384,272]{2,1,0:T(8,128)(2,1)} %constant.26.clone.table_ref) | copy-start | bytes 1253380
  47.0 8.8 %copy-start.3 = (bf16[2,256,256]{2,1,0:T(8,128)(2,1)S(1)}, bf16[2,256,256]{2,1,0:T(8,128)(2,1)}, u32[]{:S(2)}) copy-start(bf16[2,256,256]{2,1,0:T(8,128)(2,1)} %constant.21.clone.refs_1_) | copy-start | bytes 786436
  47.0 8.8 %copy-start.4 = (bf16[2,256,256]{2,1,0:T(8,128)(2,1)S(1)}, bf16[2,256,256]{2,1,0:T(8,128)(2,1)}, u32[]{:S(2)}) copy-start(bf16[2,256,256]{2,1,0:T(8,128)(2,1)} %constant.20.clone.refs_0_) | copy-start | bytes 786436
  47.0 8.8 %copy-start.5 = (bf16[2,192,192]{2,1,0:T(8,128)(2,1)S(1)}, bf16[2,192,192]{2,1,0:T(8,128)(2,1)}, u32[]{:S(2)}) copy-start(bf16[2,192,192]{2,1,0:T(8,128)(2,1)} %constant.27.clone.refs_3_) | copy-start | bytes 442372
  47.0 8.8 %copy-start.6 = (bf16[2,128,256]{2,1,0:T(8,128)(2,1)S(1)}, bf16[2,128,256]{2,1,0:T(8,128)(2,1)}, u32[]{:S(2)}) copy-start(bf16[2,128,256]{2,1,0:T(8,128)(2,1)} %constant.22.clone.refs_2_) | copy-start | bytes 393220
  47.1 8.8 %copy-start.7 = (bf16[2,96,96]{2,1,0:T(8,128)(2,1)S(1)}, bf16[2,96,96]{2,1,0:T(8,128)(2,1)}, u32[]{:S(2)}) copy-start(bf16[2,96,96]{2,1,0:T(8,128)(2,1)} %constant.28.clone.refs_4_) | copy-start | bytes 110596
  47.1 8.8 %copy-start.8 = (bf16[2,96,104]{2,1,0:T(8,128)(2,1)S(1)}, bf16[2,96,104]{2,1,0:T(8,128)(2,1)}, u32[]{:S(2)}) copy-start(bf16[2,96,104]{2,1,0:T(8,128)(2,1)} %constant.24.clone.near_ref) | copy-start | bytes 119812
  47.1 8.8 %copy-start.9 = (bf16[2,48,48]{2,1,0:T(8,128)(2,1)S(1)}, bf16[2,48,48]{2,1,0:T(8,128)(2,1)}, u32[]{:S(2)}) copy-start(bf16[2,48,48]{2,1,0:T(8,128)(2,1)} %constant.29.clone.refs_5_) | copy-start | bytes 27652
  47.1 8.7 %collective-permute-start.2 = (f32[80,768]{1,0:T(8,128)S(1)}, f32[80,768]{1,0:T(8,128)S(1)}, u32[]{:S(2)}, u32[]{:S(2)}) collective-permute-start(f32[80,768]{1,0:T(8,128)S(1)} %get-tuple-element.17), channel_id=1, source_target_pairs={{0,120},{8,0},{16,8},{24,16},{32,24},{40,32},{48,40},{56,48},{64,5... | collective-permute-start | bytes 737288 | tf_op jit(solution)/shard_map/ppermute | solution.py:616
  48.2 7.7 %collective-permute-start.3 = (f32[24,768]{1,0:T(8,128)S(1)}, f32[24,768]{1,0:T(8,128)S(1)}, u32[]{:S(2)}, u32[]{:S(2)}) collective-permute-start(f32[24,768]{1,0:T(8,128)S(1)} %get-tuple-element.18), channel_id=1, source_target_pairs={{0,8},{8,16},{16,24},{24,32},{32,40},{40,48},{48,56},{56,64},{64,7... | collective-permute-start | bytes 221192 | tf_op jit(solution)/shard_map/ppermute | solution.py:616

commit v5 on v4

--- a/solution.py
+++ b/solution.py
@@ -78,7 +78,10 @@
     return np.stack([high, low])
 
 
-HALO_ROWS = ((0, 8), (120, 168), (184, 192), (192, 200), (312, 328), (376, 384))
+ABOVE_ROWS = ((0, 8), (184, 192), (192, 200), (376, 384))
+BELOW_ROWS = ((120, 136), (312, 328), (136, 168))
+UP_MESSAGE = 6 * 16 + 6 * 16 + 3 * 32
+LEFT_MESSAGE = TILE_ROWS // 2 + 40
 
 
 @functools.lru_cache(maxsize=1)
@@ -116,16 +119,21 @@
         col_src = room_sources(COL_ROOM[level], col_spans[level][0], col_spans[level][1])
         row_src = room_sources(ROW_ROOM[level], row_spans[level][0], row_spans[level][1])
     first = rows[0]
-    near = np.concatenate([first[start:stop, TILE_ROWS:] for start, stop in HALO_ROWS], axis=0)
-    far = np.ones(first.shape[0], bool)
-    for start, stop in HALO_ROWS:
-        far[start:stop] = False
-    assert not first[far, TILE_ROWS:].any()
+    below = first[:, TILE_ROWS : TILE_ROWS + UP_ROWS]
+    above = first[:, TILE_ROWS + UP_ROWS :]
+    for part, kept in ((below, BELOW_ROWS), (above, ABOVE_ROWS)):
+        far = np.ones(first.shape[0], bool)
+        for start, stop in kept:
+            far[start:stop] = False
+        assert not part[far].any()
+    below = np.concatenate([below[start:stop] for start, stop in BELOW_ROWS], axis=0)
+    above = np.concatenate([above[start:stop] for start, stop in ABOVE_ROWS], axis=0)
     return {
         "inner": split(inner),
         "outer": split(outer),
         "own": split(first[:, :TILE_ROWS]),
-        "near": split(near),
+        "below": split(below),
+        "above": split(above),
         "cols": [split(t) for t in cols],
         "rows": [split(t) for t in rows[1:]],
     }
@@ -427,7 +435,7 @@
     ref[264:TILE_ROWS, :] = jnp.zeros((8, 128), f32)
 
 
-def place_edges_kernel(x_ref, first_ref, last_ref, right_ref, carry_ref, grid_ref):
+def place_edges_kernel(x_ref, first_ref, last_ref, left_ref, right_ref, carry_ref, grid_ref, side_ref):
     place(x_ref, grid_ref, (0, 3))
     lane8 = iota((8, 128), 1)
     rows, side, corner = unpack_block(grid_ref, 0)
@@ -440,16 +448,37 @@
     rows = add_spills(rows, turned, None)
     store_block(rows, last_ref)
     store_block(
-        [[jnp.where(lane8 == 0, turned[i][half], rows[i][half]) for half in range(2)] for i in range(17)], right_ref
-    )
+        [[jnp.where(lane8 == 0, turned[i][half], rows[i][half]) for half in range(2)] for i in range(17)], side_ref
+    )
+    right = [jnp.zeros((8, 128), f32)] * 5
+    left = [jnp.zeros((8, 128), f32)] * 5
+    for tile in range(33):
+        group, at = divmod(tile, 5)
+        rows8 = slice(tile * 8, tile * 8 + 8)
+        both = side_ref[rows8, :]
+        moved = jnp.where(lane8 == 112 + group, pltpu.roll(both, 112 + group, 1), right[at])
+        right[at] = jnp.where(lane8 // 16 == group, pltpu.roll(both, 16 * group + 16, 1), moved)
+        turned64 = pltpu.roll(first_ref[rows8, :], (64 + 16 * group) % 128, 1) if group != 4 else first_ref[rows8, :]
+        left[at] = jnp.where(lane8 // 16 == group, turned64, left[at])
+    for at in range(5):
+        right_ref[at * 8 : at * 8 + 8, :] = right[at]
+        left_ref[136 + at * 8 : 144 + at * 8, :] = left[at]
+    lane = iota((136, 128), 1)
+    left_ref[0:136, :] = jnp.where(lane < 64, first_ref[0:136, :], pltpu.roll(first_ref[136:272, :], 64, 1))
 
 
 def place_edges(arrived):
     tile = jax.ShapeDtypeStruct((TILE_ROWS, 128), f32)
     return pl.pallas_call(
         place_edges_kernel,
-        out_shape=(tile, tile, tile, jax.ShapeDtypeStruct((32, 128), f32)),
-        scratch_shapes=[pltpu.VMEM((256, 384), f32)],
+        out_shape=(
+            tile,
+            tile,
+            jax.ShapeDtypeStruct((LEFT_MESSAGE, 128), f32),
+            jax.ShapeDtypeStruct((40, 128), f32),
+            jax.ShapeDtypeStruct((32, 128), f32),
+        ),
+        scratch_shapes=[pltpu.VMEM((256, 384), f32), pltpu.VMEM((TILE_ROWS, 128), f32)],
         compiler_params=pltpu.CompilerParams(vmem_limit_bytes=32 << 20),
         cost_estimate=pl.CostEstimate(flops=600_000_000, bytes_accessed=2_000_000, transcendentals=0),
         name="place_edges",
@@ -487,13 +516,35 @@
     )(arrived, carry, first, last, inner)
 
 
-def columns_kernel(own_ref, first_ref, to_right_ref, from_right_ref, from_left_ref, outer_ref, out_ref, up_ref, down_ref):
-    lane = iota((TILE_ROWS, 128), 1)
-    from_left = from_left_ref[...]
-    spill = jnp.where(lane == 0, from_left, 0.0)
-    right = from_right_ref[...] + jnp.where(lane == 0, to_right_ref[...], 0.0)
-    mixed = jnp.where(lane < 8, first_ref[...] + spill, jnp.where(lane >= 112, from_left, 0.0))
-    outer = mm3(jnp.concatenate([right, mixed], axis=1), outer_ref)
+def columns_kernel(
+    own_ref, first_ref, to_right_ref, from_right_ref, from_left_ref, outer_ref, below_ref, out_ref, up_ref, down_ref
+):
+    lane8 = iota((8, 128), 1)
+    none = jnp.zeros((8, 128), f32)
+    spills, rows = [], []
+    for tile in range(TILE_ROWS // 8):
+        group, at = divmod(tile, 5)
+        own = first_ref[tile * 8 : tile * 8 + 8, :]
+        if tile == 33:
+            spills.append(none)
+            rows.append(jnp.concatenate([none, jnp.where(lane8 < 8, own, 0.0)], axis=1))
+            continue
+        packed = from_left_ref[at * 8 : at * 8 + 8, :]
+        spill = jnp.where(lane8 == 0, pltpu.roll(packed, 16 - group, 1), 0.0)
+        near = pltpu.roll(packed, 112 - 16 * group, 1)
+        spills.append(spill)
+        mixed = jnp.where(lane8 < 8, own + spill, jnp.where(lane8 >= 112, near, 0.0))
+        wide = from_right_ref[(tile % 17) * 8 : (tile % 17) * 8 + 8, :]
+        if tile >= 17:
+            wide = pltpu.roll(wide, 64, 1)
+        rest = from_right_ref[136 + at * 8 : 144 + at * 8, :]
+        if group != 4:
+            rest = pltpu.roll(rest, (64 - 16 * group) % 128, 1)
+        over = jnp.where(lane8 == 0, pltpu.roll(to_right_ref[at * 8 : at * 8 + 8, :], 16 - group, 1), 0.0)
+        right = jnp.where(lane8 < 64, wide, jnp.where(lane8 < 80, rest, 0.0)) + over
+        rows.append(jnp.concatenate([right, mixed], axis=1))
+    spill = jnp.concatenate(spills, axis=0)
+    outer = mm3(jnp.concatenate(rows, axis=0), outer_ref)
     pieces = [
         own_ref[:, 0:128] + taps_low[0] * spill,
         own_ref[:, 256:384] + outer[:, 256:384],
@@ -502,26 +553,34 @@
         own_ref[:, 384:512] + outer[:, 384:512],
         outer[:, 128:256],
     ]
+    low = mm3_left(below_ref, jnp.concatenate([piece[0:UP_ROWS] for piece in pieces[0:3]], axis=1))
+    high = mm3_left(below_ref[:, 0:32, :], jnp.concatenate([piece[0:UP_ROWS] for piece in pieces[3:6]], axis=1))
+    for at in range(3):
+        cols = slice(at * 128, (at + 1) * 128)
+        for part in range(2):
+            rows16 = slice(part * 16, part * 16 + 16)
+            up_ref[part * 96 + at * 16 : part * 96 + at * 16 + 16, :] = low[rows16, cols]
+            up_ref[part * 96 + 48 + at * 16 : part * 96 + 64 + at * 16, :] = high[rows16, cols]
+        up_ref[192 + at * 32 : 224 + at * 32, :] = low[32:64, cols]
     for at, piece in enumerate(pieces):
         cols = slice(at * 128, (at + 1) * 128)
         out_ref[:, cols] = piece
-        up_ref[:, cols] = piece[0:UP_ROWS]
         down_ref[:, cols] = piece[DOWN_FROM : DOWN_FROM + DOWN_ROWS]
 
 
-def outer_columns(own, first, to_right, from_right, from_left, outer):
+def outer_columns(own, first, to_right, from_right, from_left, outer, below):
     width = 2 * COL_ROOM[0]
     return pl.pallas_call(
         columns_kernel,
         out_shape=(
             jax.ShapeDtypeStruct((TILE_ROWS, width), f32),
-            jax.ShapeDtypeStruct((UP_ROWS, width), f32),
+            jax.ShapeDtypeStruct((UP_MESSAGE, 128), f32),
             jax.ShapeDtypeStruct((DOWN_ROWS, width), f32),
         ),
         compiler_params=pltpu.CompilerParams(vmem_limit_bytes=32 << 20),
         cost_estimate=pl.CostEstimate(flops=220_000_000, bytes_accessed=2_000_000, transcendentals=0),
         name="columns",
-    )(own, first, to_right, from_right, from_left, outer)
+    )(own, first, to_right, from_right, from_left, outer, below)
 
 
 def own_rows_kernel(own_ref, table_ref, out_ref):
@@ -540,22 +599,30 @@
     )(own, table)
 
 
-def levels_kernel(part_ref, below_ref, above_ref, near_ref, inner_ref, *refs):
+def levels_kernel(part_ref, below_ref, above_ref, table_ref, inner_ref, *refs):
     col_refs = (None,) + refs[0:3]
     row_refs = (None,) + refs[3:6]
     leader_refs = refs[6:10]
     approx_ref = refs[10]
     peak_ref = refs[11]
-    near = mm3_left(near_ref, jnp.concatenate([below_ref[...], above_ref[...]], axis=0))
-    pieces = []
-    at, done = 0, 0
-    for start, stop in HALO_ROWS:
-        if start > done:
-            pieces.append(part_ref[done:start, :])
-        pieces.append(part_ref[start:stop, :] + near[at : at + stop - start])
-        at += stop - start
-        done = stop
-    both = jnp.concatenate(pieces, axis=0)
+    near = mm3_left(table_ref, above_ref[...])
+    half = COL_ROOM[0]
+    sixes = [
+        jnp.concatenate([below_ref[part * 96 + at * 16 : part * 96 + at * 16 + 16, :] for at in range(6)], axis=1)
+        for part in range(2)
+    ]
+    threes = jnp.concatenate([below_ref[192 + at * 32 : 224 + at * 32, :] for at in range(3)], axis=1)
+    threes = jnp.concatenate([threes, jnp.zeros((32, half), f32)], axis=1)
+    added = {0: near[0:8], 184: near[8:16], 192: near[16:24], 376: near[24:32]}
+    added.update({120: sixes[0], 136: threes, 312: sixes[1]})
+    cuts = sorted({0, 8, 120, 136, 168, 184, 192, 200, 312, 328, 376, 384})
+    both = jnp.concatenate(
+        [
+            part_ref[start:stop, :] + added[start] if start in added else part_ref[start:stop, :]
+            for start, stop in zip(cuts, cuts[1:])
+        ],
+        axis=0,
+    )
     peak = None
     for level in range(4):
         room_r = ROW_ROOM[level]
@@ -618,15 +685,17 @@
 
 def transform(arrived):
     table = jax.tree.map(jnp.asarray, tables())
-    first, last, to_right, carry = place_edges(arrived)
-    from_right = shifted(first, "cols", -1)
+    first, last, to_left, to_right, carry = place_edges(arrived)
+    from_right = shifted(to_left, "cols", -1)
     from_left = shifted(to_right, "cols", 1)
     inner = place_inner(arrived, carry, first, last, table["inner"])
-    own, to_up, to_down = outer_columns(inner, first, to_right, from_right, from_left, table["outer"])
+    own, to_up, to_down = outer_columns(
+        inner, first, to_right, from_right, from_left, table["outer"], table["below"]
+    )
     below = shifted(to_up, "rows", -1)
     above = shifted(to_down, "rows", 1)
     part = own_rows(own, table["own"])
-    return all_levels(part, below, above, table["near"], table["inner"], table["cols"], table["rows"])
+    return all_levels(part, below, above, table["above"], table["inner"], table["cols"], table["rows"])
 
 
 def on_device(offsets, lens_weight, counts, owners, brick_slot):

time: 58.8 us -> 58.3 us (level)
  starting transfers between devices: 5.06 us -> 2.61 us
  waiting for transfers between devices: 6.49 us -> 8.05 us
    ppermute x4, starting transfers between devices: 5.06 us -> 2.61 us  [shifted(): return lax.ppermute(x, axis, [(i, (i + by) % size) for i in range(size)])]
    ppermute x4, waiting for transfers between devices: 6.49 us -> 8.05 us  [shifted(): return lax.ppermute(x, axis, [(i, (i + by) % size) for i in range(size)])]
where the time goes in v5:
time: 58.3 us; the launch traced here: 58.2 us
  blocking collectives  32.9 us (56%)
  Pallas kernels  13.7 us (23%)
  waiting for transfers between devices  8.05 us (14%)
  starting transfers between devices  2.61 us (4%)
  between operations  0.79 us (1%)
    all_to_all x1, blocking collectives, on_device(): lax.all_to_all(packed.reshape(N_DEST, MESSAGE // 4, 4, 128), ('rows', 'co...  32.9 us
    ppermute x4, waiting for transfers between devices, shifted(): return lax.ppermute(x, axis, [(i, (i + by) % size) for i in range(size)])  8.05 us
    pallas_call x1, Pallas kernels, deposit_and_pack(): pl.pallas_call(deposit_kernel, out_shape=jax.ShapeDtypeStruct((N_DEST * M...  6.09 us
    pallas_call x1, Pallas kernels, all_levels(): pl.pallas_call(levels_kernel, out_shape=tuple((jax.ShapeDtypeStruct(shape...  2.65 us
    ppermute x4, starting transfers between devices, shifted(): return lax.ppermute(x, axis, [(i, (i + by) % size) for i in range(size)])  2.61 us
    pallas_call x1, Pallas kernels, place_inner(): pl.pallas_call(place_inner_kernel, out_shape=jax.ShapeDtypeStruct((TILE_R...  1.81 us
    pallas_call x1, Pallas kernels, place_edges(): pl.pallas_call(place_edges_kernel, out_shape=(tile, tile, jax.ShapeDtypeS...  1.38 us
  transfers between devices with their start and end apart: 4, of which 2 were waited for; matrix products, arithmetic and copies ran while one was open for 0% of the time, Pallas kernels for 5%

profile of v5, /device:TPU:0, one launch (start us, length us, event | category | flops | bytes accessed | tf_op | source)
XLA Modules:
  0.0 58.2 jit_solution(8190693206751101290)
XLA Ops:
  0.6 6.1 %deposit.1 = f32[2560,128]{1,0:T(8,128)S(1)} custom-call(f32[2048,128]{1,0:T(8,128)} %bitcast.13, f32[512,256]{1,0:T(8,128)} %w_hbm.1, s32[1,512]{1,0:T(1,128)} %bitcast.14, s32[1,512]{1,0:T(1,128)} %bitcast.15, s32[1,512]{1,0:T(1,128)} %bitcast.16), custom_call_target="tpu_custom_call" | custom-call | tf_op jit(solution)/shard_map/deposit/pallas_call | solution.py:309
  6.7 32.9 %all_to_all.5 = f32[128,5,4,128]{3,2,1,0:T(4,128)S(1)} all-to-all(f32[128,5,4,128]{3,2,1,0:T(4,128)S(1)} %bitcast.10), channel_id=1, replica_groups=mesh['rows'=16,'cols'=8] {'rows','cols'}, dimensions={0} | all-to-all | bytes 2621440 | tf_op jit(solution)/shard_map/all_to_all | solution.py:703
  39.7 0.0 copy-start.2
  39.7 1.4 %place_edges.1 = (f32[272,128]{1,0:T(8,128)S(1)}, f32[272,128]{1,0:T(8,128)S(1)}, f32[176,128]{1,0:T(8,128)S(1)}, f32[40,128]{1,0:T(8,128)S(1)}, f32[32,128]{1,0:T(8,128)S(1)}) custom-call(f32[2560,128]{1,0:T(8,128)S(1)} %bitcast.11), custom_call_target="tpu_custom_call" | custom-call | flops 600000000 | bytes 2000000 | tf_op jit(solution)/shard_map/place_edges/pallas_call | solution.py:472
  41.1 0.0 collective-permute-start
  41.1 0.5 collective-permute-start.1
  41.6 0.0 copy-done.2
  41.6 0.0 copy-start.1
  41.6 0.0 copy-start.8
  41.6 1.8 %place_inner.1.own_ref = f32[272,512]{1,0:T(8,128)S(1)} custom-call(f32[2560,128]{1,0:T(8,128)S(1)} %bitcast.12, f32[32,128]{1,0:T(8,128)S(1)} %get-tuple-element.13.carry_ref, f32[272,128]{1,0:T(8,128)S(1)} %get-tuple-element.14.first_ref, f32[272,128]{1,0:T(8,128)S(1)} %get-tuple-element.15.last_ref, bf16[2,384,256]{2,1,0:T(8,128)(2,1)S(1)} %copy-done.2), custom_call_target="tpu_custom_call" | custom-call | flops 800000000 | bytes 3000000 | tf_op jit(solution)/shard_map/place_inner/pallas_call | solution.py:509
  43.4 0.0 copy-start
  43.4 2.1 %collective-permute-done.1.from_left_ref = f32[40,128]{1,0:T(8,128)S(1)} collective-permute-done((f32[40,128]{1,0:T(8,128)S(1)}, f32[40,128]{1,0:T(8,128)S(1)}, u32[]{:S(2)}, u32[]{:S(2)}) %collective-permute-start.1) | collective-permute-done | bytes 20512 | tf_op jit(solution)/shard_map/ppermute | solution.py:683
  45.5 0.0 collective-permute-done.from_right_ref
  45.5 0.0 copy-done.1
  45.5 0.0 copy-done.8
  45.5 0.7 %columns.1 = (f32[272,768]{1,0:T(8,128)S(1)}, f32[288,128]{1,0:T(8,128)S(1)}, f32[24,768]{1,0:T(8,128)S(1)}) custom-call(f32[272,512]{1,0:T(8,128)S(1)} %place_inner.1.own_ref, f32[272,128]{1,0:T(8,128)S(1)} %get-tuple-element.14.first_ref, f32[40,128]{1,0:T(8,128)S(1)} %get-tuple-element.16.to_right_ref, ...), custom_call_target="tpu_custom_call" | custom-call | flops 220000000 | bytes 2000000 | tf_op jit(solution)/shard_map/columns/pallas_call | solution.py:573
  46.2 0.0 copy-start.3
  46.2 0.0 copy-start.4
  46.3 0.0 copy-start.5
  46.3 0.0 copy-start.6
  46.3 0.0 copy-start.7
  46.3 0.0 copy-start.9
  46.3 0.0 copy-start.10
  46.3 1.5 %collective-permute-start.2 = (f32[288,128]{1,0:T(8,128)S(1)}, f32[288,128]{1,0:T(8,128)S(1)}, u32[]{:S(2)}, u32[]{:S(2)}) collective-permute-start(f32[288,128]{1,0:T(8,128)S(1)} %get-tuple-element.19), channel_id=1, source_target_pairs={{0,120},{8,0},{16,8},{24,16},{32,24},{40,32},{48,40},{56,48},{64,5... | collective-permute-start | bytes 442376 | tf_op jit(solution)/shard_map/ppermute | solution.py:683
  47.8 0.6 %collective-permute-start.3 = (f32[24,768]{1,0:T(8,128)S(1)}, f32[24,768]{1,0:T(8,128)S(1)}, u32[]{:S(2)}, u32[]{:S(2)}) collective-permute-start(f32[24,768]{1,0:T(8,128)S(1)} %get-tuple-element.20), channel_id=1, source_target_pairs={{0,8},{8,16},{16,24},{24,32},{32,40},{40,48},{48,56},{56,64},{64,7... | collective-permute-start | bytes 221192 | tf_op jit(solution)/shard_map/ppermute | solution.py:683
  48.4 0.0 copy-done
  48.4 1.1 %own_rows.1.part_ref = f32[384,768]{1,0:T(8,128)S(1)} custom-call(f32[272,768]{1,0:T(8,128)S(1)} %get-tuple-element.18.own_ref, bf16[2,384,272]{2,1,0:T(8,128)(2,1)S(1)} %copy-done), custom_call_target="tpu_custom_call" | custom-call | flops 480000000 | bytes 2000000 | tf_op jit(solution)/shard_map/own_rows/pallas_call | solution.py:593
  49.5 6.0 %collective-permute-done.3.above_ref = f32[24,768]{1,0:T(8,128)S(1)} collective-permute-done((f32[24,768]{1,0:T(8,128)S(1)}, f32[24,768]{1,0:T(8,128)S(1)}, u32[]{:S(2)}, u32[]{:S(2)}) %collective-permute-start.3) | collective-permute-done | bytes 73760 | tf_op jit(solution)/shard_map/ppermute | solution.py:683
  55.4 0.0 collective-permute-done.2.below_ref
  55.5 0.0 copy-done.3
  55.5 0.0 copy-done.4
  55.5 0.0 copy-done.5
  55.5 0.0 copy-done.6
  55.5 0.0 copy-done.7
  55.5 0.0 copy-done.9
  55.5 0.0 copy-done.10
  55.5 2.7 %levels.1 = (f32[128,256]{1,0:T(8,128)}, f32[64,128]{1,0:T(8,128)}, f32[32,64]{1,0:T(8,128)}, f32[16,32]{1,0:T(8,128)}, f32[16,32]{1,0:T(8,128)}) custom-call(f32[384,768]{1,0:T(8,128)S(1)} %own_rows.1.part_ref, f32[288,128]{1,0:T(8,128)S(1)} %collective-permute-done.2.below_ref, f32[24,768]{1,0:T(8,128)S(1)} %collective-permute-done.3.above_ref, ...), custom_call_target="tpu_custom_call" | custom-call | tf_op jit(solution)/shard_map/levels/pallas_call | solution.py:672
Async XLA Ops:
  39.7 1.9 %copy-start.2 = (bf16[2,384,256]{2,1,0:T(8,128)(2,1)S(1)}, bf16[2,384,256]{2,1,0:T(8,128)(2,1)}, u32[]{:S(2)}) copy-start(bf16[2,384,256]{2,1,0:T(8,128)(2,1)} %constant.27.clone.inner_ref) | copy-start | bytes 1179652
  41.1 4.5 %collective-permute-start = (f32[176,128]{1,0:T(8,128)S(1)}, f32[176,128]{1,0:T(8,128)S(1)}, u32[]{:S(2)}, u32[]{:S(2)}) collective-permute-start(f32[176,128]{1,0:T(8,128)S(1)} %get-tuple-element.17), channel_id=1, source_target_pairs={{0,7},{1,0},{2,1},{3,2},{4,3},{5,4},{6,5},{7,6},{8,15},{9,8},{10,9... | collective-permute-start | bytes 270344 | tf_op jit(solution)/shard_map/ppermute | solution.py:683
  41.1 4.4 %collective-permute-start.1 = (f32[40,128]{1,0:T(8,128)S(1)}, f32[40,128]{1,0:T(8,128)S(1)}, u32[]{:S(2)}, u32[]{:S(2)}) collective-permute-start(f32[40,128]{1,0:T(8,128)S(1)} %get-tuple-element.16.to_right_ref), channel_id=1, source_target_pairs={{0,1},{1,2},{2,3},{3,4},{4,5},{5,6},{6,7},{7,0},{8,9},{9,10},{10,1... | collective-permute-start | bytes 61448 | tf_op jit(solution)/shard_map/ppermute | solution.py:683
  41.6 3.9 %copy-start.1 = (bf16[2,256,512]{2,1,0:T(8,128)(2,1)S(1)}, bf16[2,256,512]{2,1,0:T(8,128)(2,1)}, u32[]{:S(2)}) copy-start(bf16[2,256,512]{2,1,0:T(8,128)(2,1)} %constant.28.clone.outer_ref) | copy-start | bytes 1572868
  41.6 3.9 %copy-start.8 = (bf16[2,64,80]{2,1,0:T(8,128)(2,1)S(1)}, bf16[2,64,80]{2,1,0:T(8,128)(2,1)}, u32[]{:S(2)}) copy-start(bf16[2,64,80]{2,1,0:T(8,128)(2,1)} %constant.23.clone.below_ref) | copy-start | bytes 61444
  43.4 5.0 %copy-start = (bf16[2,384,272]{2,1,0:T(8,128)(2,1)S(1)}, bf16[2,384,272]{2,1,0:T(8,128)(2,1)}, u32[]{:S(2)}) copy-start(bf16[2,384,272]{2,1,0:T(8,128)(2,1)} %constant.29.clone.table_ref) | copy-start | bytes 1253380
  46.2 9.2 %copy-start.3 = (bf16[2,256,256]{2,1,0:T(8,128)(2,1)S(1)}, bf16[2,256,256]{2,1,0:T(8,128)(2,1)}, u32[]{:S(2)}) copy-start(bf16[2,256,256]{2,1,0:T(8,128)(2,1)} %constant.25.clone.refs_1_) | copy-start | bytes 786436
  46.2 9.2 %copy-start.4 = (bf16[2,256,256]{2,1,0:T(8,128)(2,1)S(1)}, bf16[2,256,256]{2,1,0:T(8,128)(2,1)}, u32[]{:S(2)}) copy-start(bf16[2,256,256]{2,1,0:T(8,128)(2,1)} %constant.24.clone.refs_0_) | copy-start | bytes 786436
  46.3 9.2 %copy-start.5 = (bf16[2,192,192]{2,1,0:T(8,128)(2,1)S(1)}, bf16[2,192,192]{2,1,0:T(8,128)(2,1)}, u32[]{:S(2)}) copy-start(bf16[2,192,192]{2,1,0:T(8,128)(2,1)} %constant.30.clone.refs_3_) | copy-start | bytes 442372
  46.3 9.2 %copy-start.6 = (bf16[2,128,256]{2,1,0:T(8,128)(2,1)S(1)}, bf16[2,128,256]{2,1,0:T(8,128)(2,1)}, u32[]{:S(2)}) copy-start(bf16[2,128,256]{2,1,0:T(8,128)(2,1)} %constant.26.clone.refs_2_) | copy-start | bytes 393220
  46.3 9.2 %copy-start.7 = (bf16[2,96,96]{2,1,0:T(8,128)(2,1)S(1)}, bf16[2,96,96]{2,1,0:T(8,128)(2,1)}, u32[]{:S(2)}) copy-start(bf16[2,96,96]{2,1,0:T(8,128)(2,1)} %constant.31.clone.refs_4_) | copy-start | bytes 110596
  46.3 9.2 %copy-start.9 = (bf16[2,48,48]{2,1,0:T(8,128)(2,1)S(1)}, bf16[2,48,48]{2,1,0:T(8,128)(2,1)}, u32[]{:S(2)}) copy-start(bf16[2,48,48]{2,1,0:T(8,128)(2,1)} %constant.32.clone.refs_5_) | copy-start | bytes 27652
  46.3 9.2 %copy-start.10 = (bf16[2,32,24]{2,1,0:T(8,128)(2,1)S(1)}, bf16[2,32,24]{2,1,0:T(8,128)(2,1)}, u32[]{:S(2)}) copy-start(bf16[2,32,24]{2,1,0:T(8,128)(2,1)} %constant.22.clone.table_ref) | copy-start | bytes 9220
  46.3 9.1 %collective-permute-start.2 = (f32[288,128]{1,0:T(8,128)S(1)}, f32[288,128]{1,0:T(8,128)S(1)}, u32[]{:S(2)}, u32[]{:S(2)}) collective-permute-start(f32[288,128]{1,0:T(8,128)S(1)} %get-tuple-element.19), channel_id=1, source_target_pairs={{0,120},{8,0},{16,8},{24,16},{32,24},{40,32},{48,40},{56,48},{64,5... | collective-permute-start | bytes 442376 | tf_op jit(solution)/shard_map/ppermute | solution.py:683
  47.8 7.7 %collective-permute-start.3 = (f32[24,768]{1,0:T(8,128)S(1)}, f32[24,768]{1,0:T(8,128)S(1)}, u32[]{:S(2)}, u32[]{:S(2)}) collective-permute-start(f32[24,768]{1,0:T(8,128)S(1)} %get-tuple-element.20), channel_id=1, source_target_pairs={{0,8},{8,16},{16,24},{24,32},{32,40},{40,48},{48,56},{56,64},{64,7... | collective-permute-start | bytes 221192 | tf_op jit(solution)/shard_map/ppermute | solution.py:683

commit v6 on v5

--- a/solution.py
+++ b/solution.py
@@ -80,7 +80,8 @@
 
 ABOVE_ROWS = ((0, 8), (184, 192), (192, 200), (376, 384))
 BELOW_ROWS = ((120, 136), (312, 328), (136, 168))
-UP_MESSAGE = 6 * 16 + 6 * 16 + 3 * 32
+UP_MESSAGE = 5 * 16 + 5 * 16 + 3 * 32
+DOWN_MESSAGE = 5 * 16 + 8
 LEFT_MESSAGE = TILE_ROWS // 2 + 40
 
 
@@ -516,6 +517,16 @@
     )(arrived, carry, first, last, inner)
 
 
+def pack_tiles(tiles):
+    lane = iota(tiles[0].shape, 1)
+    shared = jnp.where((lane >= 56) & (lane < 72), pltpu.roll(tiles[5], 64, 1), tiles[2])
+    return [tiles[0], tiles[1], shared, tiles[3], tiles[4]]
+
+
+def unpack_tiles(tiles):
+    return jnp.concatenate([*tiles, pltpu.roll(tiles[2], 64, 1)], axis=1)
+
+
 def columns_kernel(
     own_ref, first_ref, to_right_ref, from_right_ref, from_left_ref, outer_ref, below_ref, out_ref, up_ref, down_ref
 ):
@@ -555,17 +566,19 @@
     ]
     low = mm3_left(below_ref, jnp.concatenate([piece[0:UP_ROWS] for piece in pieces[0:3]], axis=1))
     high = mm3_left(below_ref[:, 0:32, :], jnp.concatenate([piece[0:UP_ROWS] for piece in pieces[3:6]], axis=1))
+    for part in range(2):
+        rows16 = slice(part * 16, part * 16 + 16)
+        fives = pack_tiles([half[rows16, at * 128 : (at + 1) * 128] for half in (low, high) for at in range(3)])
+        for at, tile in enumerate(fives):
+            up_ref[part * 80 + at * 16 : part * 80 + at * 16 + 16, :] = tile
     for at in range(3):
-        cols = slice(at * 128, (at + 1) * 128)
-        for part in range(2):
-            rows16 = slice(part * 16, part * 16 + 16)
-            up_ref[part * 96 + at * 16 : part * 96 + at * 16 + 16, :] = low[rows16, cols]
-            up_ref[part * 96 + 48 + at * 16 : part * 96 + 64 + at * 16, :] = high[rows16, cols]
-        up_ref[192 + at * 32 : 224 + at * 32, :] = low[32:64, cols]
+        up_ref[160 + at * 32 : 192 + at * 32, :] = low[32:64, at * 128 : (at + 1) * 128]
+    for at, tile in enumerate(pack_tiles([piece[DOWN_FROM : DOWN_FROM + 24] for piece in pieces])):
+        down_ref[at * 16 : at * 16 + 16, :] = tile[0:16]
+        down_ref[80 + at : 81 + at, :] = tile[16:17]
+    down_ref[85:88, :] = jnp.zeros((3, 128), f32)
     for at, piece in enumerate(pieces):
-        cols = slice(at * 128, (at + 1) * 128)
-        out_ref[:, cols] = piece
-        down_ref[:, cols] = piece[DOWN_FROM : DOWN_FROM + DOWN_ROWS]
+        out_ref[:, at * 128 : (at + 1) * 128] = piece
 
 
 def outer_columns(own, first, to_right, from_right, from_left, outer, below):
@@ -575,7 +588,7 @@
         out_shape=(
             jax.ShapeDtypeStruct((TILE_ROWS, width), f32),
             jax.ShapeDtypeStruct((UP_MESSAGE, 128), f32),
-            jax.ShapeDtypeStruct((DOWN_ROWS, width), f32),
+            jax.ShapeDtypeStruct((DOWN_MESSAGE, 128), f32),
         ),
         compiler_params=pltpu.CompilerParams(vmem_limit_bytes=32 << 20),
         cost_estimate=pl.CostEstimate(flops=220_000_000, bytes_accessed=2_000_000, transcendentals=0),
@@ -605,13 +618,24 @@
     leader_refs = refs[6:10]
     approx_ref = refs[10]
     peak_ref = refs[11]
-    near = mm3_left(table_ref, above_ref[...])
+    sub = iota((8, 128), 0)
+    above = [
+        jnp.concatenate(
+            [
+                above_ref[at * 16 : at * 16 + 16, :],
+                jnp.where(sub == 0, above_ref[80 + at : 81 + at, :], 0.0),
+            ],
+            axis=0,
+        )
+        for at in range(5)
+    ]
+    near = mm3_left(table_ref, unpack_tiles(above))
     half = COL_ROOM[0]
     sixes = [
-        jnp.concatenate([below_ref[part * 96 + at * 16 : part * 96 + at * 16 + 16, :] for at in range(6)], axis=1)
+        unpack_tiles([below_ref[part * 80 + at * 16 : part * 80 + at * 16 + 16, :] for at in range(5)])
         for part in range(2)
     ]
-    threes = jnp.concatenate([below_ref[192 + at * 32 : 224 + at * 32, :] for at in range(3)], axis=1)
+    threes = jnp.concatenate([below_ref[160 + at * 32 : 192 + at * 32, :] for at in range(3)], axis=1)
     threes = jnp.concatenate([threes, jnp.zeros((32, half), f32)], axis=1)
     added = {0: near[0:8], 184: near[8:16], 192: near[16:24], 376: near[24:32]}
     added.update({120: sixes[0], 136: threes, 312: sixes[1]})
@@ -692,8 +716,8 @@
     own, to_up, to_down = outer_columns(
         inner, first, to_right, from_right, from_left, table["outer"], table["below"]
     )
+    above = shifted(to_down, "rows", 1)
     below = shifted(to_up, "rows", -1)
-    above = shifted(to_down, "rows", 1)
     part = own_rows(own, table["own"])
     return all_levels(part, below, above, table["above"], table["inner"], table["cols"], table["rows"])
 

time: 58.3 us -> 58.1 us (level)
  no operation moved by 1% of the time
where the time goes in v6:
time: 58.1 us; the launch traced here: 58 us
  blocking collectives  32.9 us (57%)
  Pallas kernels  13.9 us (24%)
  waiting for transfers between devices  7.73 us (13%)
  starting transfers between devices  2.61 us (4%)
  between operations  0.78 us (1%)
    all_to_all x1, blocking collectives, on_device(): lax.all_to_all(packed.reshape(N_DEST, MESSAGE // 4, 4, 128), ('rows', 'co...  32.9 us
    ppermute x4, waiting for transfers between devices, shifted(): return lax.ppermute(x, axis, [(i, (i + by) % size) for i in range(size)])  7.73 us
    pallas_call x1, Pallas kernels, deposit_and_pack(): pl.pallas_call(deposit_kernel, out_shape=jax.ShapeDtypeStruct((N_DEST * M...  6.09 us
    pallas_call x1, Pallas kernels, all_levels(): pl.pallas_call(levels_kernel, out_shape=tuple((jax.ShapeDtypeStruct(shape...  2.7 us
    ppermute x4, starting transfers between devices, shifted(): return lax.ppermute(x, axis, [(i, (i + by) % size) for i in range(size)])  2.61 us
    pallas_call x1, Pallas kernels, place_inner(): pl.pallas_call(place_inner_kernel, out_shape=jax.ShapeDtypeStruct((TILE_R...  1.81 us
    pallas_call x1, Pallas kernels, place_edges(): pl.pallas_call(place_edges_kernel, out_shape=(tile, tile, jax.ShapeDtypeS...  1.39 us
  transfers between devices with their start and end apart: 4, of which 2 were waited for; matrix products, arithmetic and copies ran while one was open for 0% of the time, Pallas kernels for 5%

profile of v6, /device:TPU:0, one launch (start us, length us, event | category | flops | bytes accessed | tf_op | source)
XLA Modules:
  0.0 58.0 jit_solution(11222394485525927482)
XLA Ops:
  0.6 6.1 %deposit.1 = f32[2560,128]{1,0:T(8,128)S(1)} custom-call(f32[2048,128]{1,0:T(8,128)} %bitcast.13, f32[512,256]{1,0:T(8,128)} %w_hbm.1, s32[1,512]{1,0:T(1,128)} %bitcast.14, s32[1,512]{1,0:T(1,128)} %bitcast.15, s32[1,512]{1,0:T(1,128)} %bitcast.16), custom_call_target="tpu_custom_call" | custom-call | tf_op jit(solution)/shard_map/deposit/pallas_call | solution.py:310
  6.7 32.9 %all_to_all.5 = f32[128,5,4,128]{3,2,1,0:T(4,128)S(1)} all-to-all(f32[128,5,4,128]{3,2,1,0:T(4,128)S(1)} %bitcast.10), channel_id=1, replica_groups=mesh['rows'=16,'cols'=8] {'rows','cols'}, dimensions={0} | all-to-all | bytes 2621440 | tf_op jit(solution)/shard_map/all_to_all | solution.py:727
  39.7 0.0 copy-start.2
  39.7 1.4 %place_edges.1 = (f32[272,128]{1,0:T(8,128)S(1)}, f32[272,128]{1,0:T(8,128)S(1)}, f32[176,128]{1,0:T(8,128)S(1)}, f32[40,128]{1,0:T(8,128)S(1)}, f32[32,128]{1,0:T(8,128)S(1)}) custom-call(f32[2560,128]{1,0:T(8,128)S(1)} %bitcast.11), custom_call_target="tpu_custom_call" | custom-call | flops 600000000 | bytes 2000000 | tf_op jit(solution)/shard_map/place_edges/pallas_call | solution.py:473
  41.1 0.0 collective-permute-start
  41.1 0.5 collective-permute-start.1
  41.6 0.0 copy-done.2
  41.6 0.0 copy-start.1
  41.6 0.0 copy-start.8
  41.6 1.8 %place_inner.1.own_ref = f32[272,512]{1,0:T(8,128)S(1)} custom-call(f32[2560,128]{1,0:T(8,128)S(1)} %bitcast.12, f32[32,128]{1,0:T(8,128)S(1)} %get-tuple-element.13.carry_ref, f32[272,128]{1,0:T(8,128)S(1)} %get-tuple-element.14.first_ref, f32[272,128]{1,0:T(8,128)S(1)} %get-tuple-element.15.last_ref, bf16[2,384,256]{2,1,0:T(8,128)(2,1)S(1)} %copy-done.2), custom_call_target="tpu_custom_call" | custom-call | flops 800000000 | bytes 3000000 | tf_op jit(solution)/shard_map/place_inner/pallas_call | solution.py:510
  43.4 0.0 copy-start
  43.4 2.1 %collective-permute-done.1.from_left_ref = f32[40,128]{1,0:T(8,128)S(1)} collective-permute-done((f32[40,128]{1,0:T(8,128)S(1)}, f32[40,128]{1,0:T(8,128)S(1)}, u32[]{:S(2)}, u32[]{:S(2)}) %collective-permute-start.1) | collective-permute-done | bytes 20512 | tf_op jit(solution)/shard_map/ppermute | solution.py:707
  45.5 0.0 collective-permute-done.from_right_ref
  45.5 0.0 copy-done.1
  45.5 0.0 copy-done.8
  45.5 0.8 %columns.1 = (f32[272,768]{1,0:T(8,128)S(1)}, f32[256,128]{1,0:T(8,128)S(1)}, f32[88,128]{1,0:T(8,128)S(1)}) custom-call(f32[272,512]{1,0:T(8,128)S(1)} %place_inner.1.own_ref, f32[272,128]{1,0:T(8,128)S(1)} %get-tuple-element.14.first_ref, f32[40,128]{1,0:T(8,128)S(1)} %get-tuple-element.16.to_right_ref, ...), custom_call_target="tpu_custom_call" | custom-call | flops 220000000 | bytes 2000000 | tf_op jit(solution)/shard_map/columns/pallas_call | solution.py:586
  46.3 0.0 copy-start.3
  46.3 0.0 copy-start.4
  46.3 0.0 copy-start.5
  46.3 0.0 copy-start.6
  46.3 0.0 copy-start.7
  46.4 0.0 copy-start.9
  46.4 0.0 copy-start.10
  46.4 1.5 %collective-permute-start.2 = (f32[256,128]{1,0:T(8,128)S(1)}, f32[256,128]{1,0:T(8,128)S(1)}, u32[]{:S(2)}, u32[]{:S(2)}) collective-permute-start(f32[256,128]{1,0:T(8,128)S(1)} %get-tuple-element.19), channel_id=1, source_target_pairs={{0,120},{8,0},{16,8},{24,16},{32,24},{40,32},{48,40},{56,48},{64,5... | collective-permute-start | bytes 393224 | tf_op jit(solution)/shard_map/ppermute | solution.py:707
  47.8 0.6 %collective-permute-start.3 = (f32[88,128]{1,0:T(8,128)S(1)}, f32[88,128]{1,0:T(8,128)S(1)}, u32[]{:S(2)}, u32[]{:S(2)}) collective-permute-start(f32[88,128]{1,0:T(8,128)S(1)} %get-tuple-element.20), channel_id=1, source_target_pairs={{0,8},{8,16},{16,24},{24,32},{32,40},{40,48},{48,56},{56,64},{64,7... | collective-permute-start | bytes 135176 | tf_op jit(solution)/shard_map/ppermute | solution.py:707
  48.5 0.0 copy-done
  48.5 1.1 %own_rows.1.part_ref = f32[384,768]{1,0:T(8,128)S(1)} custom-call(f32[272,768]{1,0:T(8,128)S(1)} %get-tuple-element.18.own_ref, bf16[2,384,272]{2,1,0:T(8,128)(2,1)S(1)} %copy-done), custom_call_target="tpu_custom_call" | custom-call | flops 480000000 | bytes 2000000 | tf_op jit(solution)/shard_map/own_rows/pallas_call | solution.py:606
  49.6 5.6 %collective-permute-done.3.above_ref = f32[88,128]{1,0:T(8,128)S(1)} collective-permute-done((f32[88,128]{1,0:T(8,128)S(1)}, f32[88,128]{1,0:T(8,128)S(1)}, u32[]{:S(2)}, u32[]{:S(2)}) %collective-permute-start.3) | collective-permute-done | bytes 45088 | tf_op jit(solution)/shard_map/ppermute | solution.py:707
  55.2 0.0 collective-permute-done.2.below_ref
  55.2 0.0 copy-done.3
  55.2 0.0 copy-done.4
  55.2 0.0 copy-done.5
  55.2 0.0 copy-done.6
  55.2 0.0 copy-done.7
  55.3 0.0 copy-done.9
  55.3 0.0 copy-done.10
  55.3 2.7 %levels.1 = (f32[128,256]{1,0:T(8,128)}, f32[64,128]{1,0:T(8,128)}, f32[32,64]{1,0:T(8,128)}, f32[16,32]{1,0:T(8,128)}, f32[16,32]{1,0:T(8,128)}) custom-call(f32[384,768]{1,0:T(8,128)S(1)} %own_rows.1.part_ref, f32[256,128]{1,0:T(8,128)S(1)} %collective-permute-done.2.below_ref, f32[88,128]{1,0:T(8,128)S(1)} %collective-permute-done.3.above_ref, ...), custom_call_target="tpu_custom_call" | custom-call | tf_op jit(solution)/shard_map/levels/pallas_call | solution.py:696
Async XLA Ops:
  39.7 1.9 %copy-start.2 = (bf16[2,384,256]{2,1,0:T(8,128)(2,1)S(1)}, bf16[2,384,256]{2,1,0:T(8,128)(2,1)}, u32[]{:S(2)}) copy-start(bf16[2,384,256]{2,1,0:T(8,128)(2,1)} %constant.27.clone.inner_ref) | copy-start | bytes 1179652
  41.1 4.5 %collective-permute-start = (f32[176,128]{1,0:T(8,128)S(1)}, f32[176,128]{1,0:T(8,128)S(1)}, u32[]{:S(2)}, u32[]{:S(2)}) collective-permute-start(f32[176,128]{1,0:T(8,128)S(1)} %get-tuple-element.17), channel_id=1, source_target_pairs={{0,7},{1,0},{2,1},{3,2},{4,3},{5,4},{6,5},{7,6},{8,15},{9,8},{10,9... | collective-permute-start | bytes 270344 | tf_op jit(solution)/shard_map/ppermute | solution.py:707
  41.1 4.4 %collective-permute-start.1 = (f32[40,128]{1,0:T(8,128)S(1)}, f32[40,128]{1,0:T(8,128)S(1)}, u32[]{:S(2)}, u32[]{:S(2)}) collective-permute-start(f32[40,128]{1,0:T(8,128)S(1)} %get-tuple-element.16.to_right_ref), channel_id=1, source_target_pairs={{0,1},{1,2},{2,3},{3,4},{4,5},{5,6},{6,7},{7,0},{8,9},{9,10},{10,1... | collective-permute-start | bytes 61448 | tf_op jit(solution)/shard_map/ppermute | solution.py:707
  41.6 3.9 %copy-start.1 = (bf16[2,256,512]{2,1,0:T(8,128)(2,1)S(1)}, bf16[2,256,512]{2,1,0:T(8,128)(2,1)}, u32[]{:S(2)}) copy-start(bf16[2,256,512]{2,1,0:T(8,128)(2,1)} %constant.28.clone.outer_ref) | copy-start | bytes 1572868
  41.6 3.9 %copy-start.8 = (bf16[2,64,80]{2,1,0:T(8,128)(2,1)S(1)}, bf16[2,64,80]{2,1,0:T(8,128)(2,1)}, u32[]{:S(2)}) copy-start(bf16[2,64,80]{2,1,0:T(8,128)(2,1)} %constant.23.clone.below_ref) | copy-start | bytes 61444
  43.4 5.1 %copy-start = (bf16[2,384,272]{2,1,0:T(8,128)(2,1)S(1)}, bf16[2,384,272]{2,1,0:T(8,128)(2,1)}, u32[]{:S(2)}) copy-start(bf16[2,384,272]{2,1,0:T(8,128)(2,1)} %constant.29.clone.table_ref) | copy-start | bytes 1253380
  46.3 8.9 %copy-start.3 = (bf16[2,256,256]{2,1,0:T(8,128)(2,1)S(1)}, bf16[2,256,256]{2,1,0:T(8,128)(2,1)}, u32[]{:S(2)}) copy-start(bf16[2,256,256]{2,1,0:T(8,128)(2,1)} %constant.25.clone.refs_1_) | copy-start | bytes 786436
  46.3 8.9 %copy-start.4 = (bf16[2,256,256]{2,1,0:T(8,128)(2,1)S(1)}, bf16[2,256,256]{2,1,0:T(8,128)(2,1)}, u32[]{:S(2)}) copy-start(bf16[2,256,256]{2,1,0:T(8,128)(2,1)} %constant.24.clone.refs_0_) | copy-start | bytes 786436
  46.3 8.9 %copy-start.5 = (bf16[2,192,192]{2,1,0:T(8,128)(2,1)S(1)}, bf16[2,192,192]{2,1,0:T(8,128)(2,1)}, u32[]{:S(2)}) copy-start(bf16[2,192,192]{2,1,0:T(8,128)(2,1)} %constant.30.clone.refs_3_) | copy-start | bytes 442372
  46.3 8.9 %copy-start.6 = (bf16[2,128,256]{2,1,0:T(8,128)(2,1)S(1)}, bf16[2,128,256]{2,1,0:T(8,128)(2,1)}, u32[]{:S(2)}) copy-start(bf16[2,128,256]{2,1,0:T(8,128)(2,1)} %constant.26.clone.refs_2_) | copy-start | bytes 393220
  46.3 8.9 %copy-start.7 = (bf16[2,96,96]{2,1,0:T(8,128)(2,1)S(1)}, bf16[2,96,96]{2,1,0:T(8,128)(2,1)}, u32[]{:S(2)}) copy-start(bf16[2,96,96]{2,1,0:T(8,128)(2,1)} %constant.31.clone.refs_4_) | copy-start | bytes 110596
  46.4 8.9 %copy-start.9 = (bf16[2,48,48]{2,1,0:T(8,128)(2,1)S(1)}, bf16[2,48,48]{2,1,0:T(8,128)(2,1)}, u32[]{:S(2)}) copy-start(bf16[2,48,48]{2,1,0:T(8,128)(2,1)} %constant.32.clone.refs_5_) | copy-start | bytes 27652
  46.4 8.9 %copy-start.10 = (bf16[2,32,24]{2,1,0:T(8,128)(2,1)S(1)}, bf16[2,32,24]{2,1,0:T(8,128)(2,1)}, u32[]{:S(2)}) copy-start(bf16[2,32,24]{2,1,0:T(8,128)(2,1)} %constant.22.clone.table_ref) | copy-start | bytes 9220
  46.4 8.8 %collective-permute-start.2 = (f32[256,128]{1,0:T(8,128)S(1)}, f32[256,128]{1,0:T(8,128)S(1)}, u32[]{:S(2)}, u32[]{:S(2)}) collective-permute-start(f32[256,128]{1,0:T(8,128)S(1)} %get-tuple-element.19), channel_id=1, source_target_pairs={{0,120},{8,0},{16,8},{24,16},{32,24},{40,32},{48,40},{56,48},{64,5... | collective-permute-start | bytes 393224 | tf_op jit(solution)/shard_map/ppermute | solution.py:707
  47.8 7.4 %collective-permute-start.3 = (f32[88,128]{1,0:T(8,128)S(1)}, f32[88,128]{1,0:T(8,128)S(1)}, u32[]{:S(2)}, u32[]{:S(2)}) collective-permute-start(f32[88,128]{1,0:T(8,128)S(1)} %get-tuple-element.20), channel_id=1, source_target_pairs={{0,8},{8,16},{16,24},{24,32},{32,40},{40,48},{48,56},{56,64},{64,7... | collective-permute-start | bytes 135176 | tf_op jit(solution)/shard_map/ppermute | solution.py:707

commit v7 on v6

--- a/solution.py
+++ b/solution.py
@@ -528,7 +528,7 @@
 
 
 def columns_kernel(
-    own_ref, first_ref, to_right_ref, from_right_ref, from_left_ref, outer_ref, below_ref, out_ref, up_ref, down_ref
+    own_ref, first_ref, to_right_ref, from_right_ref, from_left_ref, outer_ref, out_ref, down_ref
 ):
     lane8 = iota((8, 128), 1)
     none = jnp.zeros((8, 128), f32)
@@ -564,15 +564,6 @@
         own_ref[:, 384:512] + outer[:, 384:512],
         outer[:, 128:256],
     ]
-    low = mm3_left(below_ref, jnp.concatenate([piece[0:UP_ROWS] for piece in pieces[0:3]], axis=1))
-    high = mm3_left(below_ref[:, 0:32, :], jnp.concatenate([piece[0:UP_ROWS] for piece in pieces[3:6]], axis=1))
-    for part in range(2):
-        rows16 = slice(part * 16, part * 16 + 16)
-        fives = pack_tiles([half[rows16, at * 128 : (at + 1) * 128] for half in (low, high) for at in range(3)])
-        for at, tile in enumerate(fives):
-            up_ref[part * 80 + at * 16 : part * 80 + at * 16 + 16, :] = tile
-    for at in range(3):
-        up_ref[160 + at * 32 : 192 + at * 32, :] = low[32:64, at * 128 : (at + 1) * 128]
     for at, tile in enumerate(pack_tiles([piece[DOWN_FROM : DOWN_FROM + 24] for piece in pieces])):
         down_ref[at * 16 : at * 16 + 16, :] = tile[0:16]
         down_ref[80 + at : 81 + at, :] = tile[16:17]
@@ -581,19 +572,41 @@
         out_ref[:, at * 128 : (at + 1) * 128] = piece
 
 
-def outer_columns(own, first, to_right, from_right, from_left, outer, below):
+def outer_columns(own, first, to_right, from_right, from_left, outer):
     width = 2 * COL_ROOM[0]
     return pl.pallas_call(
         columns_kernel,
         out_shape=(
             jax.ShapeDtypeStruct((TILE_ROWS, width), f32),
-            jax.ShapeDtypeStruct((UP_MESSAGE, 128), f32),
             jax.ShapeDtypeStruct((DOWN_MESSAGE, 128), f32),
         ),
         compiler_params=pltpu.CompilerParams(vmem_limit_bytes=32 << 20),
         cost_estimate=pl.CostEstimate(flops=220_000_000, bytes_accessed=2_000_000, transcendentals=0),
         name="columns",
-    )(own, first, to_right, from_right, from_left, outer, below)
+    )(own, first, to_right, from_right, from_left, outer)
+
+
+def upward_kernel(own_ref, below_ref, up_ref):
+    half = COL_ROOM[0]
+    low = mm3_left(below_ref, own_ref[0:UP_ROWS, 0:half])
+    high = mm3_left(below_ref[:, 0:32, :], own_ref[0:UP_ROWS, half : 2 * half])
+    for part in range(2):
+        rows16 = slice(part * 16, part * 16 + 16)
+        fives = pack_tiles([side[rows16, at * 128 : (at + 1) * 128] for side in (low, high) for at in range(3)])
+        for at, tile in enumerate(fives):
+            up_ref[part * 80 + at * 16 : part * 80 + at * 16 + 16, :] = tile
+    for at in range(3):
+        up_ref[160 + at * 32 : 192 + at * 32, :] = low[32:64, at * 128 : (at + 1) * 128]
+
+
+def upward(own, below):
+    return pl.pallas_call(
+        upward_kernel,
+        out_shape=jax.ShapeDtypeStruct((UP_MESSAGE, 128), f32),
+        compiler_params=pltpu.CompilerParams(vmem_limit_bytes=32 << 20),
+        cost_estimate=pl.CostEstimate(flops=2_000_000_000, bytes_accessed=6_000_000, transcendentals=0),
+        name="upward",
+    )(own, below)
 
 
 def own_rows_kernel(own_ref, table_ref, out_ref):
@@ -607,7 +620,7 @@
         own_rows_kernel,
         out_shape=jax.ShapeDtypeStruct((2 * ROW_ROOM[0], 2 * COL_ROOM[0]), f32),
         compiler_params=pltpu.CompilerParams(vmem_limit_bytes=32 << 20),
-        cost_estimate=pl.CostEstimate(flops=480_000_000, bytes_accessed=2_000_000, transcendentals=0),
+        cost_estimate=pl.CostEstimate(flops=4_800_000_000, bytes_accessed=20_000_000, transcendentals=0),
         name="own_rows",
     )(own, table)
 
@@ -713,11 +726,9 @@
     from_right = shifted(to_left, "cols", -1)
     from_left = shifted(to_right, "cols", 1)
     inner = place_inner(arrived, carry, first, last, table["inner"])
-    own, to_up, to_down = outer_columns(
-        inner, first, to_right, from_right, from_left, table["outer"], table["below"]
-    )
+    own, to_down = outer_columns(inner, first, to_right, from_right, from_left, table["outer"])
     above = shifted(to_down, "rows", 1)
-    below = shifted(to_up, "rows", -1)
+    below = shifted(upward(own, table["below"]), "rows", -1)
     part = own_rows(own, table["own"])
     return all_levels(part, below, above, table["above"], table["inner"], table["cols"], table["rows"])
 

time: 58.1 us -> 57.3 us (0.986)
  waiting for transfers between devices: 7.73 us -> 3.57 us
  starting transfers between devices: 2.61 us -> 5.94 us
    ppermute x4, waiting for transfers between devices: 7.73 us -> 3.57 us  [shifted(): return lax.ppermute(x, axis, [(i, (i + by) % size) for i in range(size)])]
    ppermute x4, starting transfers between devices: 2.61 us -> 5.94 us  [shifted(): return lax.ppermute(x, axis, [(i, (i + by) % size) for i in range(size)])]
  transfers between devices with their start and end apart: 4 -> 4, of which waited for: 2 -> 3; matrix products, arithmetic and copies ran while one was open for 0% -> 0% of each run, Pallas kernels for 5% -> 5%
where the time goes in v7:
time: 57.3 us; the launch traced here: 57.1 us
  blocking collectives  32.9 us (57%)
  Pallas kernels  13.9 us (24%)
  starting transfers between devices  5.94 us (10%)
  waiting for transfers between devices  3.57 us (6%)
  between operations  0.76 us (1%)
    all_to_all x1, blocking collectives, on_device(): lax.all_to_all(packed.reshape(N_DEST, MESSAGE // 4, 4, 128), ('rows', 'co...  32.9 us
    pallas_call x1, Pallas kernels, deposit_and_pack(): pl.pallas_call(deposit_kernel, out_shape=jax.ShapeDtypeStruct((N_DEST * M...  6.09 us
    ppermute x4, starting transfers between devices, shifted(): return lax.ppermute(x, axis, [(i, (i + by) % size) for i in range(size)])  5.94 us
    ppermute x4, waiting for transfers between devices, shifted(): return lax.ppermute(x, axis, [(i, (i + by) % size) for i in range(size)])  3.57 us
    pallas_call x1, Pallas kernels, all_levels(): pl.pallas_call(levels_kernel, out_shape=tuple((jax.ShapeDtypeStruct(shape...  2.69 us
    pallas_call x1, Pallas kernels, place_inner(): pl.pallas_call(place_inner_kernel, out_shape=jax.ShapeDtypeStruct((TILE_R...  1.8 us
    pallas_call x1, Pallas kernels, place_edges(): pl.pallas_call(place_edges_kernel, out_shape=(tile, tile, jax.ShapeDtypeS...  1.38 us
  transfers between devices with their start and end apart: 4, of which 3 were waited for; matrix products, arithmetic and copies ran while one was open for 0% of the time, Pallas kernels for 5%

profile of v7, /device:TPU:0, one launch (start us, length us, event | category | flops | bytes accessed | tf_op | source)
XLA Modules:
  0.0 57.1 jit_solution(15033620019720834653)
XLA Ops:
  0.6 6.1 %deposit.1 = f32[2560,128]{1,0:T(8,128)S(1)} custom-call(f32[2048,128]{1,0:T(8,128)} %bitcast.13, f32[512,256]{1,0:T(8,128)} %w_hbm.1, s32[1,512]{1,0:T(1,128)} %bitcast.14, s32[1,512]{1,0:T(1,128)} %bitcast.15, s32[1,512]{1,0:T(1,128)} %bitcast.16), custom_call_target="tpu_custom_call" | custom-call | tf_op jit(solution)/shard_map/deposit/pallas_call | solution.py:310
  6.7 32.9 %all_to_all.5 = f32[128,5,4,128]{3,2,1,0:T(4,128)S(1)} all-to-all(f32[128,5,4,128]{3,2,1,0:T(4,128)S(1)} %bitcast.10), channel_id=1, replica_groups=mesh['rows'=16,'cols'=8] {'rows','cols'}, dimensions={0} | all-to-all | bytes 2621440 | tf_op jit(solution)/shard_map/all_to_all | solution.py:738
  39.7 0.0 copy-start.1
  39.7 1.4 %place_edges.1 = (f32[272,128]{1,0:T(8,128)S(1)}, f32[272,128]{1,0:T(8,128)S(1)}, f32[176,128]{1,0:T(8,128)S(1)}, f32[40,128]{1,0:T(8,128)S(1)}, f32[32,128]{1,0:T(8,128)S(1)}) custom-call(f32[2560,128]{1,0:T(8,128)S(1)} %bitcast.11), custom_call_target="tpu_custom_call" | custom-call | flops 600000000 | bytes 2000000 | tf_op jit(solution)/shard_map/place_edges/pallas_call | solution.py:473
  41.1 0.0 collective-permute-start
  41.1 0.5 collective-permute-start.1
  41.6 0.0 copy-done.1
  41.6 0.0 copy-start
  41.6 1.8 %place_inner.1.own_ref = f32[272,512]{1,0:T(8,128)S(1)} custom-call(f32[2560,128]{1,0:T(8,128)S(1)} %bitcast.12, f32[32,128]{1,0:T(8,128)S(1)} %get-tuple-element.12.carry_ref, f32[272,128]{1,0:T(8,128)S(1)} %get-tuple-element.13.first_ref, f32[272,128]{1,0:T(8,128)S(1)} %get-tuple-element.14.last_ref, bf16[2,384,256]{2,1,0:T(8,128)(2,1)S(1)} %copy-done.1), custom_call_target="tpu_custom_call" | custom-call | flops 800000000 | bytes 3000000 | tf_op jit(solution)/shard_map/place_inner/pallas_call | solution.py:510
  43.4 0.0 copy-start.10
  43.4 2.1 %collective-permute-done.1.from_left_ref = f32[40,128]{1,0:T(8,128)S(1)} collective-permute-done((f32[40,128]{1,0:T(8,128)S(1)}, f32[40,128]{1,0:T(8,128)S(1)}, u32[]{:S(2)}, u32[]{:S(2)}) %collective-permute-start.1) | collective-permute-done | bytes 20512 | tf_op jit(solution)/shard_map/ppermute | solution.py:720
  45.5 0.0 collective-permute-done.from_right_ref
  45.5 0.0 copy-done
  45.5 0.6 columns.1
  46.1 0.7 %collective-permute-start.3 = (f32[88,128]{1,0:T(8,128)S(1)}, f32[88,128]{1,0:T(8,128)S(1)}, u32[]{:S(2)}, u32[]{:S(2)}) collective-permute-start(f32[88,128]{1,0:T(8,128)S(1)} %get-tuple-element.18), channel_id=1, source_target_pairs={{0,8},{8,16},{16,24},{24,32},{32,40},{40,48},{48,56},{56,64},{64,7... | collective-permute-start | bytes 135176 | tf_op jit(solution)/shard_map/ppermute | solution.py:720
  46.8 0.0 copy-done.10
  46.8 0.0 copy-start.9
  46.8 0.3 upward.1
  47.1 0.0 copy-start.2
  47.1 0.0 copy-start.3
  47.1 0.0 copy-start.4
  47.1 0.0 copy-start.5
  47.1 0.0 copy-start.6
  47.1 0.0 copy-start.7
  47.1 0.0 copy-start.8
  47.2 4.7 %collective-permute-start.2 = (f32[256,128]{1,0:T(8,128)S(1)}, f32[256,128]{1,0:T(8,128)S(1)}, u32[]{:S(2)}, u32[]{:S(2)}) collective-permute-start(f32[256,128]{1,0:T(8,128)S(1)} %upward.1), channel_id=1, source_target_pairs={{0,120},{8,0},{16,8},{24,16},{32,24},{40,32},{48,40},{56,48},{64,5... | collective-permute-start | bytes 393224 | tf_op jit(solution)/shard_map/ppermute | solution.py:720
  51.9 0.0 copy-done.9
  51.9 1.1 %own_rows.1.part_ref = f32[384,768]{1,0:T(8,128)S(1)} custom-call(f32[272,768]{1,0:T(8,128)S(1)} %get-tuple-element.17.own_ref, bf16[2,384,272]{2,1,0:T(8,128)(2,1)S(1)} %copy-done.9), custom_call_target="tpu_custom_call" | custom-call | flops 4800000000 | bytes 20000000 | tf_op jit(solution)/shard_map/own_rows/pallas_call | solution.py:619
  52.9 0.5 collective-permute-done.3.above_ref
  53.5 0.9 %collective-permute-done.2.below_ref = f32[256,128]{1,0:T(8,128)S(1)} collective-permute-done((f32[256,128]{1,0:T(8,128)S(1)}, f32[256,128]{1,0:T(8,128)S(1)}, u32[]{:S(2)}, u32[]{:S(2)}) %collective-permute-start.2) | collective-permute-done | bytes 131104 | tf_op jit(solution)/shard_map/ppermute | solution.py:720
  54.4 0.0 copy-done.2
  54.4 0.0 copy-done.3
  54.4 0.0 copy-done.4
  54.4 0.0 copy-done.5
  54.4 0.0 copy-done.6
  54.4 0.0 copy-done.7
  54.4 0.0 copy-done.8
  54.4 2.7 %levels.1 = (f32[128,256]{1,0:T(8,128)}, f32[64,128]{1,0:T(8,128)}, f32[32,64]{1,0:T(8,128)}, f32[16,32]{1,0:T(8,128)}, f32[16,32]{1,0:T(8,128)}) custom-call(f32[384,768]{1,0:T(8,128)S(1)} %own_rows.1.part_ref, f32[256,128]{1,0:T(8,128)S(1)} %collective-permute-done.2.below_ref, f32[88,128]{1,0:T(8,128)S(1)} %collective-permute-done.3.above_ref, ...), custom_call_target="tpu_custom_call" | custom-call | tf_op jit(solution)/shard_map/levels/pallas_call | solution.py:709
Async XLA Ops:
  39.7 1.9 %copy-start.1 = (bf16[2,384,256]{2,1,0:T(8,128)(2,1)S(1)}, bf16[2,384,256]{2,1,0:T(8,128)(2,1)}, u32[]{:S(2)}) copy-start(bf16[2,384,256]{2,1,0:T(8,128)(2,1)} %constant.27.clone.inner_ref) | copy-start | bytes 1179652
  41.1 4.5 %collective-permute-start = (f32[176,128]{1,0:T(8,128)S(1)}, f32[176,128]{1,0:T(8,128)S(1)}, u32[]{:S(2)}, u32[]{:S(2)}) collective-permute-start(f32[176,128]{1,0:T(8,128)S(1)} %get-tuple-element.16), channel_id=1, source_target_pairs={{0,7},{1,0},{2,1},{3,2},{4,3},{5,4},{6,5},{7,6},{8,15},{9,8},{10,9... | collective-permute-start | bytes 270344 | tf_op jit(solution)/shard_map/ppermute | solution.py:720
  41.1 4.4 %collective-permute-start.1 = (f32[40,128]{1,0:T(8,128)S(1)}, f32[40,128]{1,0:T(8,128)S(1)}, u32[]{:S(2)}, u32[]{:S(2)}) collective-permute-start(f32[40,128]{1,0:T(8,128)S(1)} %get-tuple-element.15.to_right_ref), channel_id=1, source_target_pairs={{0,1},{1,2},{2,3},{3,4},{4,5},{5,6},{6,7},{7,0},{8,9},{9,10},{10,1... | collective-permute-start | bytes 61448 | tf_op jit(solution)/shard_map/ppermute | solution.py:720
  41.6 3.9 %copy-start = (bf16[2,256,512]{2,1,0:T(8,128)(2,1)S(1)}, bf16[2,256,512]{2,1,0:T(8,128)(2,1)}, u32[]{:S(2)}) copy-start(bf16[2,256,512]{2,1,0:T(8,128)(2,1)} %constant.28.clone.outer_ref) | copy-start | bytes 1572868
  43.4 3.4 %copy-start.10 = (bf16[2,64,80]{2,1,0:T(8,128)(2,1)S(1)}, bf16[2,64,80]{2,1,0:T(8,128)(2,1)}, u32[]{:S(2)}) copy-start(bf16[2,64,80]{2,1,0:T(8,128)(2,1)} %constant.23.clone.below_ref) | copy-start | bytes 61444
  46.1 7.4 %collective-permute-start.3 = (f32[88,128]{1,0:T(8,128)S(1)}, f32[88,128]{1,0:T(8,128)S(1)}, u32[]{:S(2)}, u32[]{:S(2)}) collective-permute-start(f32[88,128]{1,0:T(8,128)S(1)} %get-tuple-element.18), channel_id=1, source_target_pairs={{0,8},{8,16},{16,24},{24,32},{32,40},{40,48},{48,56},{56,64},{64,7... | collective-permute-start | bytes 135176 | tf_op jit(solution)/shard_map/ppermute | solution.py:720
  46.8 5.0 %copy-start.9 = (bf16[2,384,272]{2,1,0:T(8,128)(2,1)S(1)}, bf16[2,384,272]{2,1,0:T(8,128)(2,1)}, u32[]{:S(2)}) copy-start(bf16[2,384,272]{2,1,0:T(8,128)(2,1)} %constant.29.clone.table_ref) | copy-start | bytes 1253380
  47.1 7.3 %copy-start.2 = (bf16[2,256,256]{2,1,0:T(8,128)(2,1)S(1)}, bf16[2,256,256]{2,1,0:T(8,128)(2,1)}, u32[]{:S(2)}) copy-start(bf16[2,256,256]{2,1,0:T(8,128)(2,1)} %constant.25.clone.refs_1_) | copy-start | bytes 786436
  47.1 7.3 %copy-start.3 = (bf16[2,256,256]{2,1,0:T(8,128)(2,1)S(1)}, bf16[2,256,256]{2,1,0:T(8,128)(2,1)}, u32[]{:S(2)}) copy-start(bf16[2,256,256]{2,1,0:T(8,128)(2,1)} %constant.24.clone.refs_0_) | copy-start | bytes 786436
  47.1 7.3 %copy-start.4 = (bf16[2,192,192]{2,1,0:T(8,128)(2,1)S(1)}, bf16[2,192,192]{2,1,0:T(8,128)(2,1)}, u32[]{:S(2)}) copy-start(bf16[2,192,192]{2,1,0:T(8,128)(2,1)} %constant.30.clone.refs_3_) | copy-start | bytes 442372
  47.1 7.3 %copy-start.5 = (bf16[2,128,256]{2,1,0:T(8,128)(2,1)S(1)}, bf16[2,128,256]{2,1,0:T(8,128)(2,1)}, u32[]{:S(2)}) copy-start(bf16[2,128,256]{2,1,0:T(8,128)(2,1)} %constant.26.clone.refs_2_) | copy-start | bytes 393220
  47.1 7.3 %copy-start.6 = (bf16[2,96,96]{2,1,0:T(8,128)(2,1)S(1)}, bf16[2,96,96]{2,1,0:T(8,128)(2,1)}, u32[]{:S(2)}) copy-start(bf16[2,96,96]{2,1,0:T(8,128)(2,1)} %constant.31.clone.refs_4_) | copy-start | bytes 110596
  47.1 7.3 %copy-start.7 = (bf16[2,48,48]{2,1,0:T(8,128)(2,1)S(1)}, bf16[2,48,48]{2,1,0:T(8,128)(2,1)}, u32[]{:S(2)}) copy-start(bf16[2,48,48]{2,1,0:T(8,128)(2,1)} %constant.32.clone.refs_5_) | copy-start | bytes 27652
  47.1 7.3 %copy-start.8 = (bf16[2,32,24]{2,1,0:T(8,128)(2,1)S(1)}, bf16[2,32,24]{2,1,0:T(8,128)(2,1)}, u32[]{:S(2)}) copy-start(bf16[2,32,24]{2,1,0:T(8,128)(2,1)} %constant.22.clone.table_ref) | copy-start | bytes 9220
  47.2 7.2 %collective-permute-start.2 = (f32[256,128]{1,0:T(8,128)S(1)}, f32[256,128]{1,0:T(8,128)S(1)}, u32[]{:S(2)}, u32[]{:S(2)}) collective-permute-start(f32[256,128]{1,0:T(8,128)S(1)} %upward.1), channel_id=1, source_target_pairs={{0,120},{8,0},{16,8},{24,16},{32,24},{40,32},{48,40},{56,48},{64,5... | collective-permute-start | bytes 393224 | tf_op jit(solution)/shard_map/ppermute | solution.py:720

commit v8 on v6

--- a/solution.py
+++ b/solution.py
@@ -80,6 +80,7 @@
 
 ABOVE_ROWS = ((0, 8), (184, 192), (192, 200), (376, 384))
 BELOW_ROWS = ((120, 136), (312, 328), (136, 168))
+SECOND_ROWS = ((0, 8), (120, 136), (136, 168), (184, 192))
 UP_MESSAGE = 5 * 16 + 5 * 16 + 3 * 32
 DOWN_MESSAGE = 5 * 16 + 8
 LEFT_MESSAGE = TILE_ROWS // 2 + 40
@@ -129,7 +130,9 @@
         assert not part[far].any()
     below = np.concatenate([below[start:stop] for start, stop in BELOW_ROWS], axis=0)
     above = np.concatenate([above[start:stop] for start, stop in ABOVE_ROWS], axis=0)
+    second = np.concatenate([rows[1][:, start:stop] for start, stop in SECOND_ROWS], axis=1)
     return {
+        "second": split(second),
         "inner": split(inner),
         "outer": split(outer),
         "own": split(first[:, :TILE_ROWS]),
@@ -596,28 +599,39 @@
     )(own, first, to_right, from_right, from_left, outer, below)
 
 
-def own_rows_kernel(own_ref, table_ref, out_ref):
+def second_columns(current, inner, rest):
+    main = mm3(current, inner)
+    rest = mm3(jnp.concatenate([current[:, 256:384], current[:, 0:128]], axis=1), rest)
+    return jnp.concatenate([main[:, 0:128], rest[:, 0:128], main[:, 128:256], rest[:, 128:256]], axis=1)
+
+
+def own_rows_kernel(own_ref, table_ref, inner_ref, rest_ref, rows_ref, out_ref, second_ref):
     for at in range(3):
         cols = slice(at * 256, (at + 1) * 256)
         out_ref[:, cols] = mm3_left(table_ref, own_ref[:, cols])
-
-
-def own_rows(own, table):
+    current = out_ref[0 : ROW_ROOM[0], 0 : COL_ROOM[0]]
+    second_ref[...] = mm3_left(rows_ref, second_columns(current, inner_ref, rest_ref))
+
+
+def own_rows(own, table, inner, rest, rows):
     return pl.pallas_call(
         own_rows_kernel,
-        out_shape=jax.ShapeDtypeStruct((2 * ROW_ROOM[0], 2 * COL_ROOM[0]), f32),
+        out_shape=(
+            jax.ShapeDtypeStruct((2 * ROW_ROOM[0], 2 * COL_ROOM[0]), f32),
+            jax.ShapeDtypeStruct((2 * ROW_ROOM[1], 2 * COL_ROOM[1]), f32),
+        ),
         compiler_params=pltpu.CompilerParams(vmem_limit_bytes=32 << 20),
-        cost_estimate=pl.CostEstimate(flops=480_000_000, bytes_accessed=2_000_000, transcendentals=0),
+        cost_estimate=pl.CostEstimate(flops=4_800_000_000, bytes_accessed=20_000_000, transcendentals=0),
         name="own_rows",
-    )(own, table)
-
-
-def levels_kernel(part_ref, below_ref, above_ref, table_ref, inner_ref, *refs):
+    )(own, table, inner, rest, rows)
+
+
+def levels_kernel(part_ref, second_ref, below_ref, above_ref, table_ref, inner_ref, added_ref, *refs):
     col_refs = (None,) + refs[0:3]
-    row_refs = (None,) + refs[3:6]
-    leader_refs = refs[6:10]
-    approx_ref = refs[10]
-    peak_ref = refs[11]
+    row_refs = (None, None) + refs[3:5]
+    leader_refs = refs[5:9]
+    approx_ref = refs[9]
+    peak_ref = refs[10]
     sub = iota((8, 128), 0)
     above = [
         jnp.concatenate(
@@ -652,10 +666,8 @@
         room_r = ROW_ROOM[level]
         room_c = COL_ROOM[level]
         if level == 1:
-            main = mm3(current, inner_ref)
-            rest = mm3(jnp.concatenate([current[:, 256:384], current[:, 0:128]], axis=1), col_refs[1])
-            parts = (main[:, 0:128], rest[:, 0:128], main[:, 128:256], rest[:, 128:256])
-            both = mm3_left(row_refs[1], jnp.concatenate(parts, axis=1))
+            halo = jnp.concatenate([added[start][:, :half] for start, _ in SECOND_ROWS], axis=0)
+            both = second_ref[...] + mm3_left(added_ref, second_columns(halo, inner_ref, col_refs[1]))
         elif level:
             both = mm3_left(row_refs[level], mm3(current, col_refs[level]))
         current = both[:room_r, :room_c]
@@ -691,7 +703,7 @@
     approx_ref[...] = current[: R_DEV >> 4, : C_DEV >> 4]
 
 
-def all_levels(part, below, above, near, inner, cols, rows):
+def all_levels(part, second, below, above, near, inner, added, cols, rows):
     shapes = [(R_DEV >> level, C_DEV >> level) for level in (1, 2, 3, 4, 4)]
     return pl.pallas_call(
         levels_kernel,
@@ -699,7 +711,7 @@
         scratch_shapes=[pltpu.VMEM((3 * ROW_ROOM[0], 128), f32)],
         compiler_params=pltpu.CompilerParams(vmem_limit_bytes=32 << 20),
         name="levels",
-    )(part, below, above, near, inner, *cols, *rows)
+    )(part, second, below, above, near, inner, added, *cols, *rows)
 
 
 def shifted(x, axis, by):
@@ -718,8 +730,10 @@
     )
     above = shifted(to_down, "rows", 1)
     below = shifted(to_up, "rows", -1)
-    part = own_rows(own, table["own"])
-    return all_levels(part, below, above, table["above"], table["inner"], table["cols"], table["rows"])
+    part, second = own_rows(own, table["own"], table["inner"], table["cols"][0], table["rows"][0])
+    return all_levels(
+        part, second, below, above, table["above"], table["inner"], table["second"], table["cols"], table["rows"][1:]
+    )
 
 
 def on_device(offsets, lens_weight, counts, owners, brick_slot):

time: 58.1 us -> 56.7 us (0.976)
  waiting for transfers between devices: 7.73 us -> 2.78 us
  starting transfers between devices: 2.61 us -> 5.88 us
    ppermute x4, waiting for transfers between devices: 7.73 us -> 2.78 us  [shifted(): return lax.ppermute(x, axis, [(i, (i + by) % size) for i in range(size)])]
    ppermute x4, starting transfers between devices: 2.61 us -> 5.88 us  [shifted(): return lax.ppermute(x, axis, [(i, (i + by) % size) for i in range(size)])]
    pallas_call x1, Pallas kernels: 1.08 us -> 1.73 us  [own_rows(): pl.pallas_call(own_rows_kernel, out_shape=(jax.ShapeDtypeStruct((2 * ROW_...]
  transfers between devices with their start and end apart: 4 -> 4, of which waited for: 2 -> 3; matrix products, arithmetic and copies ran while one was open for 0% -> 0% of each run, Pallas kernels for 5% -> 6%
where the time goes in v8:
time: 56.7 us; the launch traced here: 56.5 us
  blocking collectives  32.9 us (58%)
  Pallas kernels  14.1 us (25%)
  starting transfers between devices  5.88 us (10%)
  waiting for transfers between devices  2.78 us (5%)
  between operations  0.77 us (1%)
    all_to_all x1, blocking collectives, on_device(): lax.all_to_all(packed.reshape(N_DEST, MESSAGE // 4, 4, 128), ('rows', 'co...  32.9 us
    pallas_call x1, Pallas kernels, deposit_and_pack(): pl.pallas_call(deposit_kernel, out_shape=jax.ShapeDtypeStruct((N_DEST * M...  6.09 us
    ppermute x4, starting transfers between devices, shifted(): return lax.ppermute(x, axis, [(i, (i + by) % size) for i in range(size)])  5.88 us
    ppermute x4, waiting for transfers between devices, shifted(): return lax.ppermute(x, axis, [(i, (i + by) % size) for i in range(size)])  2.78 us
    pallas_call x1, Pallas kernels, all_levels(): pl.pallas_call(levels_kernel, out_shape=tuple((jax.ShapeDtypeStruct(shape...  2.32 us
    pallas_call x1, Pallas kernels, place_inner(): pl.pallas_call(place_inner_kernel, out_shape=jax.ShapeDtypeStruct((TILE_R...  1.8 us
    pallas_call x1, Pallas kernels, own_rows(): pl.pallas_call(own_rows_kernel, out_shape=(jax.ShapeDtypeStruct((2 * ROW_...  1.73 us
    pallas_call x1, Pallas kernels, place_edges(): pl.pallas_call(place_edges_kernel, out_shape=(tile, tile, jax.ShapeDtypeS...  1.39 us
  transfers between devices with their start and end apart: 4, of which 3 were waited for; matrix products, arithmetic and copies ran while one was open for 0% of the time, Pallas kernels for 6%

profile of v8, /device:TPU:0, one launch (start us, length us, event | category | flops | bytes accessed | tf_op | source)
XLA Modules:
  0.0 56.5 jit_solution(8623402098564647810)
XLA Ops:
  0.6 6.1 %deposit.1 = f32[2560,128]{1,0:T(8,128)S(1)} custom-call(f32[2048,128]{1,0:T(8,128)} %bitcast.13, f32[512,256]{1,0:T(8,128)} %w_hbm.1, s32[1,512]{1,0:T(1,128)} %bitcast.14, s32[1,512]{1,0:T(1,128)} %bitcast.15, s32[1,512]{1,0:T(1,128)} %bitcast.16), custom_call_target="tpu_custom_call" | custom-call | tf_op jit(solution)/shard_map/deposit/pallas_call | solution.py:313
  6.7 32.9 %all_to_all.5 = f32[128,5,4,128]{3,2,1,0:T(4,128)S(1)} all-to-all(f32[128,5,4,128]{3,2,1,0:T(4,128)S(1)} %bitcast.10), channel_id=1, replica_groups=mesh['rows'=16,'cols'=8] {'rows','cols'}, dimensions={0} | all-to-all | bytes 2621440 | tf_op jit(solution)/shard_map/all_to_all | solution.py:741
  39.7 0.0 copy-start.1
  39.7 1.4 %place_edges.1 = (f32[272,128]{1,0:T(8,128)S(1)}, f32[272,128]{1,0:T(8,128)S(1)}, f32[176,128]{1,0:T(8,128)S(1)}, f32[40,128]{1,0:T(8,128)S(1)}, f32[32,128]{1,0:T(8,128)S(1)}) custom-call(f32[2560,128]{1,0:T(8,128)S(1)} %bitcast.11), custom_call_target="tpu_custom_call" | custom-call | flops 600000000 | bytes 2000000 | tf_op jit(solution)/shard_map/place_edges/pallas_call | solution.py:476
  41.1 0.0 collective-permute-start
  41.1 0.5 collective-permute-start.1
  41.6 0.0 copy-done.1
  41.6 0.0 copy-start
  41.6 0.0 copy-start.7
  41.6 1.8 %place_inner.1.own_ref = f32[272,512]{1,0:T(8,128)S(1)} custom-call(f32[2560,128]{1,0:T(8,128)S(1)} %bitcast.12, f32[32,128]{1,0:T(8,128)S(1)} %get-tuple-element.15.carry_ref, f32[272,128]{1,0:T(8,128)S(1)} %get-tuple-element.16.first_ref, f32[272,128]{1,0:T(8,128)S(1)} %get-tuple-element.17.last_ref, bf16[2,384,256]{2,1,0:T(8,128)(2,1)S(1)} %copy-done.1), custom_call_target="tpu_custom_call" | custom-call | flops 800000000 | bytes 3000000 | tf_op jit(solution)/shard_map/place_inner/pallas_call | solution.py:513
  43.4 0.0 copy-start.2
  43.4 0.0 copy-start.10
  43.4 0.0 copy-start.11
  43.4 2.1 %collective-permute-done.1.from_left_ref = f32[40,128]{1,0:T(8,128)S(1)} collective-permute-done((f32[40,128]{1,0:T(8,128)S(1)}, f32[40,128]{1,0:T(8,128)S(1)}, u32[]{:S(2)}, u32[]{:S(2)}) %collective-permute-start.1) | collective-permute-done | bytes 20512 | tf_op jit(solution)/shard_map/ppermute | solution.py:719
  45.5 0.0 collective-permute-done.from_right_ref
  45.5 0.0 copy-done
  45.5 0.0 copy-done.7
  45.5 0.8 %columns.1 = (f32[272,768]{1,0:T(8,128)S(1)}, f32[256,128]{1,0:T(8,128)S(1)}, f32[88,128]{1,0:T(8,128)S(1)}) custom-call(f32[272,512]{1,0:T(8,128)S(1)} %place_inner.1.own_ref, f32[272,128]{1,0:T(8,128)S(1)} %get-tuple-element.16.first_ref, f32[40,128]{1,0:T(8,128)S(1)} %get-tuple-element.18.to_right_ref, ...), custom_call_target="tpu_custom_call" | custom-call | flops 220000000 | bytes 2000000 | tf_op jit(solution)/shard_map/columns/pallas_call | solution.py:589
  46.3 0.7 %collective-permute-start.3 = (f32[88,128]{1,0:T(8,128)S(1)}, f32[88,128]{1,0:T(8,128)S(1)}, u32[]{:S(2)}, u32[]{:S(2)}) collective-permute-start(f32[88,128]{1,0:T(8,128)S(1)} %get-tuple-element.24), channel_id=1, source_target_pairs={{0,8},{8,16},{16,24},{24,32},{32,40},{40,48},{48,56},{56,64},{64,7... | collective-permute-start | bytes 135176 | tf_op jit(solution)/shard_map/ppermute | solution.py:719
  47.0 4.6 %collective-permute-start.2 = (f32[256,128]{1,0:T(8,128)S(1)}, f32[256,128]{1,0:T(8,128)S(1)}, u32[]{:S(2)}, u32[]{:S(2)}) collective-permute-start(f32[256,128]{1,0:T(8,128)S(1)} %get-tuple-element.23), channel_id=1, source_target_pairs={{0,120},{8,0},{16,8},{24,16},{32,24},{40,32},{48,40},{56,48},{64,5... | collective-permute-start | bytes 393224 | tf_op jit(solution)/shard_map/ppermute | solution.py:719
  51.7 0.0 copy-done.2
  51.7 0.0 copy-done.10
  51.7 0.0 copy-done.11
  51.7 0.0 copy-start.3
  51.7 0.0 copy-start.4
  51.7 0.0 copy-start.5
  51.7 0.0 copy-start.6
  51.7 0.0 copy-start.8
  51.7 0.0 copy-start.9
  51.7 1.7 %own_rows.1 = (f32[384,768]{1,0:T(8,128)S(1)}, f32[192,512]{1,0:T(8,128)S(1)}) custom-call(f32[272,768]{1,0:T(8,128)S(1)} %get-tuple-element.20.own_ref, bf16[2,384,272]{2,1,0:T(8,128)(2,1)S(1)} %copy-done.10, bf16[2,384,256]{2,1,0:T(8,128)(2,1)S(1)} %copy-done.1, bf16[2,256,256]{2,1,0:T(8,128)(2,1)S(1)} %copy-done.2, bf16[2,192,192]{2,1,0:T(8,128)(2,1)S(1)} %copy-done.11), custom_call_target="tpu_custom_call" | custom-call | flops 4800000000 | bytes 20000000 | tf_op jit(solution)/shard_map/own_rows/pallas_call | solution.py:617
  53.5 0.2 collective-permute-done.3.above_ref
  53.7 0.5 collective-permute-done.2.below_ref
  54.2 0.0 copy-done.3
  54.2 0.0 copy-done.4
  54.2 0.0 copy-done.5
  54.2 0.0 copy-done.6
  54.2 0.0 copy-done.8
  54.2 0.0 copy-done.9
  54.2 2.3 %levels.1 = (f32[128,256]{1,0:T(8,128)}, f32[64,128]{1,0:T(8,128)}, f32[32,64]{1,0:T(8,128)}, f32[16,32]{1,0:T(8,128)}, f32[16,32]{1,0:T(8,128)}) custom-call(f32[384,768]{1,0:T(8,128)S(1)} %get-tuple-element.21.part_ref, f32[192,512]{1,0:T(8,128)S(1)} %get-tuple-element.22.second_ref, f32[256,128]{1,0:T(8,128)S(1)} %collective-permute-done.2.below_ref, ...), custom_call_target="tpu_custom_call" | custom-call | tf_op jit(solution)/shard_map/levels/pallas_call | solution.py:708
Async XLA Ops:
  39.7 1.9 %copy-start.1 = (bf16[2,384,256]{2,1,0:T(8,128)(2,1)S(1)}, bf16[2,384,256]{2,1,0:T(8,128)(2,1)}, u32[]{:S(2)}) copy-start(bf16[2,384,256]{2,1,0:T(8,128)(2,1)} %constant.29.clone.inner_ref) | copy-start | bytes 1179652
  41.1 4.5 %collective-permute-start = (f32[176,128]{1,0:T(8,128)S(1)}, f32[176,128]{1,0:T(8,128)S(1)}, u32[]{:S(2)}, u32[]{:S(2)}) collective-permute-start(f32[176,128]{1,0:T(8,128)S(1)} %get-tuple-element.19), channel_id=1, source_target_pairs={{0,7},{1,0},{2,1},{3,2},{4,3},{5,4},{6,5},{7,6},{8,15},{9,8},{10,9... | collective-permute-start | bytes 270344 | tf_op jit(solution)/shard_map/ppermute | solution.py:719
  41.1 4.4 %collective-permute-start.1 = (f32[40,128]{1,0:T(8,128)S(1)}, f32[40,128]{1,0:T(8,128)S(1)}, u32[]{:S(2)}, u32[]{:S(2)}) collective-permute-start(f32[40,128]{1,0:T(8,128)S(1)} %get-tuple-element.18.to_right_ref), channel_id=1, source_target_pairs={{0,1},{1,2},{2,3},{3,4},{4,5},{5,6},{6,7},{7,0},{8,9},{9,10},{10,1... | collective-permute-start | bytes 61448 | tf_op jit(solution)/shard_map/ppermute | solution.py:719
  41.6 3.9 %copy-start = (bf16[2,256,512]{2,1,0:T(8,128)(2,1)S(1)}, bf16[2,256,512]{2,1,0:T(8,128)(2,1)}, u32[]{:S(2)}) copy-start(bf16[2,256,512]{2,1,0:T(8,128)(2,1)} %constant.30.clone.outer_ref) | copy-start | bytes 1572868
  41.6 3.9 %copy-start.7 = (bf16[2,64,80]{2,1,0:T(8,128)(2,1)S(1)}, bf16[2,64,80]{2,1,0:T(8,128)(2,1)}, u32[]{:S(2)}) copy-start(bf16[2,64,80]{2,1,0:T(8,128)(2,1)} %constant.25.clone.below_ref) | copy-start | bytes 61444
  43.4 8.3 %copy-start.2 = (bf16[2,256,256]{2,1,0:T(8,128)(2,1)S(1)}, bf16[2,256,256]{2,1,0:T(8,128)(2,1)}, u32[]{:S(2)}) copy-start(bf16[2,256,256]{2,1,0:T(8,128)(2,1)} %constant.26.clone.rest_ref.refs_0_) | copy-start | bytes 786436
  43.4 8.3 %copy-start.10 = (bf16[2,384,272]{2,1,0:T(8,128)(2,1)S(1)}, bf16[2,384,272]{2,1,0:T(8,128)(2,1)}, u32[]{:S(2)}) copy-start(bf16[2,384,272]{2,1,0:T(8,128)(2,1)} %constant.31.clone.table_ref) | copy-start | bytes 1253380
  43.4 8.3 %copy-start.11 = (bf16[2,192,192]{2,1,0:T(8,128)(2,1)S(1)}, bf16[2,192,192]{2,1,0:T(8,128)(2,1)}, u32[]{:S(2)}) copy-start(bf16[2,192,192]{2,1,0:T(8,128)(2,1)} %constant.32.clone.rows_ref) | copy-start | bytes 442372
  46.3 7.4 %collective-permute-start.3 = (f32[88,128]{1,0:T(8,128)S(1)}, f32[88,128]{1,0:T(8,128)S(1)}, u32[]{:S(2)}, u32[]{:S(2)}) collective-permute-start(f32[88,128]{1,0:T(8,128)S(1)} %get-tuple-element.24), channel_id=1, source_target_pairs={{0,8},{8,16},{16,24},{24,32},{32,40},{40,48},{48,56},{56,64},{64,7... | collective-permute-start | bytes 135176 | tf_op jit(solution)/shard_map/ppermute | solution.py:719
  47.0 7.1 %collective-permute-start.2 = (f32[256,128]{1,0:T(8,128)S(1)}, f32[256,128]{1,0:T(8,128)S(1)}, u32[]{:S(2)}, u32[]{:S(2)}) collective-permute-start(f32[256,128]{1,0:T(8,128)S(1)} %get-tuple-element.23), channel_id=1, source_target_pairs={{0,120},{8,0},{16,8},{24,16},{32,24},{40,32},{48,40},{56,48},{64,5... | collective-permute-start | bytes 393224 | tf_op jit(solution)/shard_map/ppermute | solution.py:719
  51.7 2.5 %copy-start.3 = (bf16[2,256,256]{2,1,0:T(8,128)(2,1)S(1)}, bf16[2,256,256]{2,1,0:T(8,128)(2,1)}, u32[]{:S(2)}) copy-start(bf16[2,256,256]{2,1,0:T(8,128)(2,1)} %constant.27.clone.refs_1_) | copy-start | bytes 786436
  51.7 2.5 %copy-start.4 = (bf16[2,128,256]{2,1,0:T(8,128)(2,1)S(1)}, bf16[2,128,256]{2,1,0:T(8,128)(2,1)}, u32[]{:S(2)}) copy-start(bf16[2,128,256]{2,1,0:T(8,128)(2,1)} %constant.28.clone.refs_2_) | copy-start | bytes 393220
  51.7 2.5 %copy-start.5 = (bf16[2,192,64]{2,1,0:T(8,128)(2,1)S(1)}, bf16[2,192,64]{2,1,0:T(8,128)(2,1)}, u32[]{:S(2)}) copy-start(bf16[2,192,64]{2,1,0:T(8,128)(2,1)} %constant.35.clone.added_ref) | copy-start | bytes 147460
  51.7 2.5 %copy-start.6 = (bf16[2,96,96]{2,1,0:T(8,128)(2,1)S(1)}, bf16[2,96,96]{2,1,0:T(8,128)(2,1)}, u32[]{:S(2)}) copy-start(bf16[2,96,96]{2,1,0:T(8,128)(2,1)} %constant.33.clone.refs_3_) | copy-start | bytes 110596
  51.7 2.5 %copy-start.8 = (bf16[2,48,48]{2,1,0:T(8,128)(2,1)S(1)}, bf16[2,48,48]{2,1,0:T(8,128)(2,1)}, u32[]{:S(2)}) copy-start(bf16[2,48,48]{2,1,0:T(8,128)(2,1)} %constant.34.clone.refs_4_) | copy-start | bytes 27652
  51.7 2.5 %copy-start.9 = (bf16[2,32,24]{2,1,0:T(8,128)(2,1)S(1)}, bf16[2,32,24]{2,1,0:T(8,128)(2,1)}, u32[]{:S(2)}) copy-start(bf16[2,32,24]{2,1,0:T(8,128)(2,1)} %constant.24.clone.table_ref) | copy-start | bytes 9220

commit v9 on v8

--- a/solution.py
+++ b/solution.py
@@ -348,7 +348,17 @@
     return mm(table[0], high) + (mm(table[0], low) + mm(table[1], high))
 
 
-def place(x_ref, grid_ref, blocks):
+def block_slots(block):
+    row = iota((128, SLOTS), 0)
+    return (row // 16) * 64 + row % 16 + block * 16
+
+
+def edge_slots():
+    row = iota((128, SLOTS), 0)
+    return (row // 16) * 64 + row % 16 + jnp.where(row < 80, 0, 64 + 48)
+
+
+def place(x_ref, grid_ref, picks):
     lane8 = iota((8, 128), 1)
     upper = jnp.concatenate([x_ref[pl.ds(rank, N_DEST, stride=MESSAGE), :] for rank in range(8)], axis=0)
     lower = jnp.concatenate([x_ref[pl.ds(8 + rank, N_DEST, stride=MESSAGE), :] for rank in range(8)], axis=0)
@@ -361,10 +371,9 @@
     slot = mm_nt(weigh, ends_high)[0:1, :].astype(jnp.int32)
     high, low = hi_lo(jnp.concatenate([upper, lower], axis=1))
     ends = jnp.concatenate([ends_high, ends_low], axis=1)
-    row = iota((128, SLOTS), 0)
-    for at, block in enumerate(blocks):
+    for at, slots in enumerate(picks):
         rows = slice(at * 128, (at + 1) * 128)
-        pick = ((row // 16) * 64 + row % 16 + block * 16 == slot).astype(bf16)
+        pick = (slots == slot).astype(bf16)
         grid_ref[rows, 0:256] = mm(pick, high) + mm(pick, low)
         both = mm(pick, ends)
         grid_ref[rows, 256:384] = both[:, 0:128] + both[:, 128:256]
@@ -389,18 +398,17 @@
     return turned + [[pltpu.roll(corner[half], 16, 1) for half in range(2)]]
 
 
-def unpack_block(grid_ref, at):
+def unpack_block(grid_ref, starts):
     rows = [[None, None] for _ in range(17)]
     side, corner = [None, None], [None, None]
+    none = jnp.zeros((8, 128), f32)
     for half in range(2):
         parts = []
         for third in range(3):
+            lanes = slice(third * 128, (third + 1) * 128)
             parts.append(
                 swap_groups(
-                    [
-                        grid_ref[at * 128 + col * 16 + half * 8 : at * 128 + col * 16 + half * 8 + 8, third * 128 : (third + 1) * 128]
-                        for col in range(8)
-                    ]
+                    [none if at is None else grid_ref[at + half * 8 : at + half * 8 + 8, lanes] for at in starts]
                 )
             )
         for i in range(8):
@@ -439,18 +447,14 @@
     ref[264:TILE_ROWS, :] = jnp.zeros((8, 128), f32)
 
 
-def place_edges_kernel(x_ref, first_ref, last_ref, left_ref, right_ref, carry_ref, grid_ref, side_ref):
-    place(x_ref, grid_ref, (0, 3))
+def place_edges_kernel(x_ref, first_ref, left_ref, right_ref, grid_ref, side_ref):
+    place(x_ref, grid_ref, [edge_slots()])
     lane8 = iota((8, 128), 1)
-    rows, side, corner = unpack_block(grid_ref, 0)
+    rows, side, corner = unpack_block(grid_ref, [0, 16, 32, 48, 64, None, None, None])
     store_block(add_spills(rows, turn(side, corner), None), first_ref)
-    for half in range(2):
-        carry_ref[half * 8 : half * 8 + 8, :] = side[half]
-        carry_ref[16 + half * 8 : 24 + half * 8, :] = corner[half]
-    rows, side, corner = unpack_block(grid_ref, 1)
+    rows, side, corner = unpack_block(grid_ref, [None] * 6 + [80, 96])
     turned = turn(side, corner)
     rows = add_spills(rows, turned, None)
-    store_block(rows, last_ref)
     store_block(
         [[jnp.where(lane8 == 0, turned[i][half], rows[i][half]) for half in range(2)] for i in range(17)], side_ref
     )
@@ -477,47 +481,37 @@
         place_edges_kernel,
         out_shape=(
             tile,
-            tile,
             jax.ShapeDtypeStruct((LEFT_MESSAGE, 128), f32),
             jax.ShapeDtypeStruct((40, 128), f32),
-            jax.ShapeDtypeStruct((32, 128), f32),
         ),
-        scratch_shapes=[pltpu.VMEM((256, 384), f32), pltpu.VMEM((TILE_ROWS, 128), f32)],
+        scratch_shapes=[pltpu.VMEM((128, 384), f32), pltpu.VMEM((TILE_ROWS, 128), f32)],
         compiler_params=pltpu.CompilerParams(vmem_limit_bytes=32 << 20),
         cost_estimate=pl.CostEstimate(flops=600_000_000, bytes_accessed=2_000_000, transcendentals=0),
         name="place_edges",
     )(arrived)
 
 
-def place_inner_kernel(x_ref, carry_ref, first_ref, last_ref, inner_ref, own_ref, grid_ref, second_ref, third_ref, fix_ref):
-    place(x_ref, grid_ref, (1, 2))
-    lane8 = iota((8, 128), 1)
-    previous = turn(
-        [carry_ref[half * 8 : half * 8 + 8, :] for half in range(2)],
-        [carry_ref[16 + half * 8 : 24 + half * 8, :] for half in range(2)],
-    )
-    for at, ref in enumerate((second_ref, third_ref)):
-        rows, side, corner = unpack_block(grid_ref, at)
+def place_inner_kernel(x_ref, inner_ref, own_ref, grid_ref, *tile_refs):
+    place(x_ref, grid_ref, [block_slots(block) for block in range(4)])
+    previous = None
+    for block, ref in enumerate(tile_refs):
+        rows, side, corner = unpack_block(grid_ref, [block * 128 + col * 16 for col in range(8)])
         turned = turn(side, corner)
         store_block(add_spills(rows, turned, previous), ref)
         previous = turned
-    store_block([[jnp.where(lane8 == 0, previous[i][half], 0.0) for half in range(2)] for i in range(17)], fix_ref)
-    left = jnp.concatenate([first_ref[...], second_ref[...], third_ref[...]], axis=1)
-    right = jnp.concatenate([third_ref[...], last_ref[...] + fix_ref[...]], axis=1)
-    own_ref[:, 0:256] = mm3(left, inner_ref)
-    own_ref[:, 256:512] = mm3(right, inner_ref[:, 0:256, :])
-
-
-def place_inner(arrived, carry, first, last, inner):
-    tile = pltpu.VMEM((TILE_ROWS, 128), f32)
+    own_ref[:, 0:256] = mm3(jnp.concatenate([ref[...] for ref in tile_refs[0:3]], axis=1), inner_ref)
+    own_ref[:, 256:512] = mm3(jnp.concatenate([ref[...] for ref in tile_refs[2:4]], axis=1), inner_ref[:, 0:256, :])
+
+
+def place_inner(arrived, inner):
     return pl.pallas_call(
         place_inner_kernel,
         out_shape=jax.ShapeDtypeStruct((TILE_ROWS, 512), f32),
-        scratch_shapes=[pltpu.VMEM((256, 384), f32), tile, tile, tile],
+        scratch_shapes=[pltpu.VMEM((BRICKS, 384), f32)] + [pltpu.VMEM((TILE_ROWS, 128), f32)] * 4,
         compiler_params=pltpu.CompilerParams(vmem_limit_bytes=32 << 20),
-        cost_estimate=pl.CostEstimate(flops=800_000_000, bytes_accessed=3_000_000, transcendentals=0),
+        cost_estimate=pl.CostEstimate(flops=1_600_000_000, bytes_accessed=3_000_000, transcendentals=0),
         name="place_inner",
-    )(arrived, carry, first, last, inner)
+    )(arrived, inner)
 
 
 def pack_tiles(tiles):
@@ -721,10 +715,10 @@
 
 def transform(arrived):
     table = jax.tree.map(jnp.asarray, tables())
-    first, last, to_left, to_right, carry = place_edges(arrived)
+    first, to_left, to_right = place_edges(arrived)
     from_right = shifted(to_left, "cols", -1)
     from_left = shifted(to_right, "cols", 1)
-    inner = place_inner(arrived, carry, first, last, table["inner"])
+    inner = place_inner(arrived, table["inner"])
     own, to_up, to_down = outer_columns(
         inner, first, to_right, from_right, from_left, table["outer"], table["below"]
     )

time: 56.7 us -> 57.1 us (level)
  starting transfers between devices: 5.88 us -> 8.31 us
  waiting for transfers between devices: 2.78 us -> 0.72 us
    ppermute x4, starting transfers between devices: 5.88 us -> 8.31 us  [shifted(): return lax.ppermute(x, axis, [(i, (i + by) % size) for i in range(size)])]
    ppermute x4, waiting for transfers between devices: 2.78 us -> 0.72 us  [shifted(): return lax.ppermute(x, axis, [(i, (i + by) % size) for i in range(size)])]
  transfers between devices with their start and end apart: 4 -> 4, of which waited for: 3 -> 2; matrix products, arithmetic and copies ran while one was open for 0% -> 0% of each run, Pallas kernels for 6% -> 7%
where the time goes in v9:
time: 57.1 us; the launch traced here: 56.9 us
  blocking collectives  32.9 us (58%)
  Pallas kernels  14.1 us (25%)
  starting transfers between devices  8.31 us (15%)
  between operations  0.81 us (1%)
  waiting for transfers between devices  0.72 us (1%)
    all_to_all x1, blocking collectives, on_device(): lax.all_to_all(packed.reshape(N_DEST, MESSAGE // 4, 4, 128), ('rows', 'co...  32.9 us
    ppermute x4, starting transfers between devices, shifted(): return lax.ppermute(x, axis, [(i, (i + by) % size) for i in range(size)])  8.31 us
    pallas_call x1, Pallas kernels, deposit_and_pack(): pl.pallas_call(deposit_kernel, out_shape=jax.ShapeDtypeStruct((N_DEST * M...  6.09 us
    pallas_call x1, Pallas kernels, all_levels(): pl.pallas_call(levels_kernel, out_shape=tuple((jax.ShapeDtypeStruct(shape...  2.32 us
    pallas_call x1, Pallas kernels, place_inner(): pl.pallas_call(place_inner_kernel, out_shape=jax.ShapeDtypeStruct((TILE_R...  2.09 us
    pallas_call x1, Pallas kernels, own_rows(): pl.pallas_call(own_rows_kernel, out_shape=(jax.ShapeDtypeStruct((2 * ROW_...  1.72 us
  transfers between devices with their start and end apart: 4, of which 2 were waited for; matrix products, arithmetic and copies ran while one was open for 0% of the time, Pallas kernels for 7%

profile of v9, /device:TPU:0, one launch (start us, length us, event | category | flops | bytes accessed | tf_op | source)
XLA Modules:
  0.0 56.9 jit_solution(4488340570461744685)
XLA Ops:
  0.6 6.1 %deposit.1 = f32[2560,128]{1,0:T(8,128)S(1)} custom-call(f32[2048,128]{1,0:T(8,128)} %bitcast.13, f32[512,256]{1,0:T(8,128)} %w_hbm.1, s32[1,512]{1,0:T(1,128)} %bitcast.14, s32[1,512]{1,0:T(1,128)} %bitcast.15, s32[1,512]{1,0:T(1,128)} %bitcast.16), custom_call_target="tpu_custom_call" | custom-call | tf_op jit(solution)/shard_map/deposit/pallas_call | solution.py:313
  6.7 32.9 %all_to_all.5 = f32[128,5,4,128]{3,2,1,0:T(4,128)S(1)} all-to-all(f32[128,5,4,128]{3,2,1,0:T(4,128)S(1)} %bitcast.10), channel_id=1, replica_groups=mesh['rows'=16,'cols'=8] {'rows','cols'}, dimensions={0} | all-to-all | bytes 2621440 | tf_op jit(solution)/shard_map/all_to_all | solution.py:735
  39.7 0.0 copy-start.1
  39.7 1.1 %place_edges.1 = (f32[272,128]{1,0:T(8,128)S(1)}, f32[176,128]{1,0:T(8,128)S(1)}, f32[40,128]{1,0:T(8,128)S(1)}) custom-call(f32[2560,128]{1,0:T(8,128)S(1)} %bitcast.11), custom_call_target="tpu_custom_call" | custom-call | flops 600000000 | bytes 2000000 | tf_op jit(solution)/shard_map/place_edges/pallas_call | solution.py:480
  40.7 0.0 collective-permute-start.1
  40.8 0.0 copy-start
  40.8 0.0 copy-start.7
  40.8 2.9 %collective-permute-start = (f32[176,128]{1,0:T(8,128)S(1)}, f32[176,128]{1,0:T(8,128)S(1)}, u32[]{:S(2)}, u32[]{:S(2)}) collective-permute-start(f32[176,128]{1,0:T(8,128)S(1)} %get-tuple-element.15), channel_id=1, source_target_pairs={{0,7},{1,0},{2,1},{3,2},{4,3},{5,4},{6,5},{7,6},{8,15},{9,8},{10,9... | collective-permute-start | bytes 270344 | tf_op jit(solution)/shard_map/ppermute | solution.py:713
  43.7 0.0 copy-done.1
  43.7 2.1 %place_inner.1.own_ref = f32[272,512]{1,0:T(8,128)S(1)} custom-call(f32[2560,128]{1,0:T(8,128)S(1)} %bitcast.12, bf16[2,384,256]{2,1,0:T(8,128)(2,1)S(1)} %copy-done.1), custom_call_target="tpu_custom_call" | custom-call | flops 1600000000 | bytes 3000000 | tf_op jit(solution)/shard_map/place_inner/pallas_call | solution.py:507
  45.8 0.0 copy-start.2
  45.8 0.0 copy-start.10
  45.8 0.0 copy-start.11
  45.9 0.0 collective-permute-done.1.from_left_ref
  45.9 0.0 collective-permute-done.from_right_ref
  45.9 0.0 copy-done
  45.9 0.0 copy-done.7
  45.9 0.8 %columns.1 = (f32[272,768]{1,0:T(8,128)S(1)}, f32[256,128]{1,0:T(8,128)S(1)}, f32[88,128]{1,0:T(8,128)S(1)}) custom-call(f32[272,512]{1,0:T(8,128)S(1)} %place_inner.1.own_ref, f32[272,128]{1,0:T(8,128)S(1)} %get-tuple-element.13.first_ref, f32[40,128]{1,0:T(8,128)S(1)} %get-tuple-element.14.to_right_ref, ...), custom_call_target="tpu_custom_call" | custom-call | flops 220000000 | bytes 2000000 | tf_op jit(solution)/shard_map/columns/pallas_call | solution.py:583
  46.7 0.7 %collective-permute-start.3 = (f32[88,128]{1,0:T(8,128)S(1)}, f32[88,128]{1,0:T(8,128)S(1)}, u32[]{:S(2)}, u32[]{:S(2)}) collective-permute-start(f32[88,128]{1,0:T(8,128)S(1)} %get-tuple-element.20), channel_id=1, source_target_pairs={{0,8},{8,16},{16,24},{24,32},{32,40},{40,48},{48,56},{56,64},{64,7... | collective-permute-start | bytes 135176 | tf_op jit(solution)/shard_map/ppermute | solution.py:713
  47.4 4.6 %collective-permute-start.2 = (f32[256,128]{1,0:T(8,128)S(1)}, f32[256,128]{1,0:T(8,128)S(1)}, u32[]{:S(2)}, u32[]{:S(2)}) collective-permute-start(f32[256,128]{1,0:T(8,128)S(1)} %get-tuple-element.19), channel_id=1, source_target_pairs={{0,120},{8,0},{16,8},{24,16},{32,24},{40,32},{48,40},{56,48},{64,5... | collective-permute-start | bytes 393224 | tf_op jit(solution)/shard_map/ppermute | solution.py:713
  52.0 0.0 copy-done.2
  52.0 0.0 copy-done.10
  52.0 0.0 copy-done.11
  52.0 0.0 copy-start.3
  52.0 0.0 copy-start.4
  52.1 0.0 copy-start.5
  52.1 0.0 copy-start.6
  52.1 0.0 copy-start.8
  52.1 0.0 copy-start.9
  52.1 1.7 %own_rows.1 = (f32[384,768]{1,0:T(8,128)S(1)}, f32[192,512]{1,0:T(8,128)S(1)}) custom-call(f32[272,768]{1,0:T(8,128)S(1)} %get-tuple-element.16.own_ref, bf16[2,384,272]{2,1,0:T(8,128)(2,1)S(1)} %copy-done.10, bf16[2,384,256]{2,1,0:T(8,128)(2,1)S(1)} %copy-done.1, bf16[2,256,256]{2,1,0:T(8,128)(2,1)S(1)} %copy-done.2, bf16[2,192,192]{2,1,0:T(8,128)(2,1)S(1)} %copy-done.11), custom_call_target="tpu_custom_call" | custom-call | flops 4800000000 | bytes 20000000 | tf_op jit(solution)/shard_map/own_rows/pallas_call | solution.py:611
  53.8 0.2 collective-permute-done.3.above_ref
  54.1 0.5 collective-permute-done.2.below_ref
  54.6 0.0 copy-done.3
  54.6 0.0 copy-done.4
  54.6 0.0 copy-done.5
  54.6 0.0 copy-done.6
  54.6 0.0 copy-done.8
  54.6 0.0 copy-done.9
  54.6 2.3 %levels.1 = (f32[128,256]{1,0:T(8,128)}, f32[64,128]{1,0:T(8,128)}, f32[32,64]{1,0:T(8,128)}, f32[16,32]{1,0:T(8,128)}, f32[16,32]{1,0:T(8,128)}) custom-call(f32[384,768]{1,0:T(8,128)S(1)} %get-tuple-element.17.part_ref, f32[192,512]{1,0:T(8,128)S(1)} %get-tuple-element.18.second_ref, f32[256,128]{1,0:T(8,128)S(1)} %collective-permute-done.2.below_ref, ...), custom_call_target="tpu_custom_call" | custom-call | tf_op jit(solution)/shard_map/levels/pallas_call | solution.py:702
Async XLA Ops:
  39.7 4.1 %copy-start.1 = (bf16[2,384,256]{2,1,0:T(8,128)(2,1)S(1)}, bf16[2,384,256]{2,1,0:T(8,128)(2,1)}, u32[]{:S(2)}) copy-start(bf16[2,384,256]{2,1,0:T(8,128)(2,1)} %constant.29.clone.inner_ref) | copy-start | bytes 1179652
  40.7 5.1 %collective-permute-start.1 = (f32[40,128]{1,0:T(8,128)S(1)}, f32[40,128]{1,0:T(8,128)S(1)}, u32[]{:S(2)}, u32[]{:S(2)}) collective-permute-start(f32[40,128]{1,0:T(8,128)S(1)} %get-tuple-element.14.to_right_ref), channel_id=1, source_target_pairs={{0,1},{1,2},{2,3},{3,4},{4,5},{5,6},{6,7},{7,0},{8,9},{9,10},{10,1... | collective-permute-start | bytes 61448 | tf_op jit(solution)/shard_map/ppermute | solution.py:713
  40.8 5.1 %copy-start = (bf16[2,256,512]{2,1,0:T(8,128)(2,1)S(1)}, bf16[2,256,512]{2,1,0:T(8,128)(2,1)}, u32[]{:S(2)}) copy-start(bf16[2,256,512]{2,1,0:T(8,128)(2,1)} %constant.30.clone.outer_ref) | copy-start | bytes 1572868
  40.8 5.1 %copy-start.7 = (bf16[2,64,80]{2,1,0:T(8,128)(2,1)S(1)}, bf16[2,64,80]{2,1,0:T(8,128)(2,1)}, u32[]{:S(2)}) copy-start(bf16[2,64,80]{2,1,0:T(8,128)(2,1)} %constant.25.clone.below_ref) | copy-start | bytes 61444
  40.8 5.1 %collective-permute-start = (f32[176,128]{1,0:T(8,128)S(1)}, f32[176,128]{1,0:T(8,128)S(1)}, u32[]{:S(2)}, u32[]{:S(2)}) collective-permute-start(f32[176,128]{1,0:T(8,128)S(1)} %get-tuple-element.15), channel_id=1, source_target_pairs={{0,7},{1,0},{2,1},{3,2},{4,3},{5,4},{6,5},{7,6},{8,15},{9,8},{10,9... | collective-permute-start | bytes 270344 | tf_op jit(solution)/shard_map/ppermute | solution.py:713
  45.8 6.2 %copy-start.2 = (bf16[2,256,256]{2,1,0:T(8,128)(2,1)S(1)}, bf16[2,256,256]{2,1,0:T(8,128)(2,1)}, u32[]{:S(2)}) copy-start(bf16[2,256,256]{2,1,0:T(8,128)(2,1)} %constant.26.clone.rest_ref.refs_0_) | copy-start | bytes 786436
  45.8 6.2 %copy-start.10 = (bf16[2,384,272]{2,1,0:T(8,128)(2,1)S(1)}, bf16[2,384,272]{2,1,0:T(8,128)(2,1)}, u32[]{:S(2)}) copy-start(bf16[2,384,272]{2,1,0:T(8,128)(2,1)} %constant.31.clone.table_ref) | copy-start | bytes 1253380
  45.8 6.2 %copy-start.11 = (bf16[2,192,192]{2,1,0:T(8,128)(2,1)S(1)}, bf16[2,192,192]{2,1,0:T(8,128)(2,1)}, u32[]{:S(2)}) copy-start(bf16[2,192,192]{2,1,0:T(8,128)(2,1)} %constant.32.clone.rows_ref) | copy-start | bytes 442372
  46.7 7.4 %collective-permute-start.3 = (f32[88,128]{1,0:T(8,128)S(1)}, f32[88,128]{1,0:T(8,128)S(1)}, u32[]{:S(2)}, u32[]{:S(2)}) collective-permute-start(f32[88,128]{1,0:T(8,128)S(1)} %get-tuple-element.20), channel_id=1, source_target_pairs={{0,8},{8,16},{16,24},{24,32},{32,40},{40,48},{48,56},{56,64},{64,7... | collective-permute-start | bytes 135176 | tf_op jit(solution)/shard_map/ppermute | solution.py:713
  47.4 7.2 %collective-permute-start.2 = (f32[256,128]{1,0:T(8,128)S(1)}, f32[256,128]{1,0:T(8,128)S(1)}, u32[]{:S(2)}, u32[]{:S(2)}) collective-permute-start(f32[256,128]{1,0:T(8,128)S(1)} %get-tuple-element.19), channel_id=1, source_target_pairs={{0,120},{8,0},{16,8},{24,16},{32,24},{40,32},{48,40},{56,48},{64,5... | collective-permute-start | bytes 393224 | tf_op jit(solution)/shard_map/ppermute | solution.py:713
  52.0 2.5 %copy-start.3 = (bf16[2,256,256]{2,1,0:T(8,128)(2,1)S(1)}, bf16[2,256,256]{2,1,0:T(8,128)(2,1)}, u32[]{:S(2)}) copy-start(bf16[2,256,256]{2,1,0:T(8,128)(2,1)} %constant.27.clone.refs_1_) | copy-start | bytes 786436
  52.0 2.5 %copy-start.4 = (bf16[2,128,256]{2,1,0:T(8,128)(2,1)S(1)}, bf16[2,128,256]{2,1,0:T(8,128)(2,1)}, u32[]{:S(2)}) copy-start(bf16[2,128,256]{2,1,0:T(8,128)(2,1)} %constant.28.clone.refs_2_) | copy-start | bytes 393220
  52.1 2.5 %copy-start.5 = (bf16[2,192,64]{2,1,0:T(8,128)(2,1)S(1)}, bf16[2,192,64]{2,1,0:T(8,128)(2,1)}, u32[]{:S(2)}) copy-start(bf16[2,192,64]{2,1,0:T(8,128)(2,1)} %constant.35.clone.added_ref) | copy-start | bytes 147460
  52.1 2.5 %copy-start.6 = (bf16[2,96,96]{2,1,0:T(8,128)(2,1)S(1)}, bf16[2,96,96]{2,1,0:T(8,128)(2,1)}, u32[]{:S(2)}) copy-start(bf16[2,96,96]{2,1,0:T(8,128)(2,1)} %constant.33.clone.refs_3_) | copy-start | bytes 110596
  52.1 2.5 %copy-start.8 = (bf16[2,48,48]{2,1,0:T(8,128)(2,1)S(1)}, bf16[2,48,48]{2,1,0:T(8,128)(2,1)}, u32[]{:S(2)}) copy-start(bf16[2,48,48]{2,1,0:T(8,128)(2,1)} %constant.34.clone.refs_4_) | copy-start | bytes 27652
  52.1 2.5 %copy-start.9 = (bf16[2,32,24]{2,1,0:T(8,128)(2,1)S(1)}, bf16[2,32,24]{2,1,0:T(8,128)(2,1)}, u32[]{:S(2)}) copy-start(bf16[2,32,24]{2,1,0:T(8,128)(2,1)} %constant.24.clone.table_ref) | copy-start | bytes 9220

commit v10 on v9

--- a/solution.py
+++ b/solution.py
@@ -509,7 +509,7 @@
         out_shape=jax.ShapeDtypeStruct((TILE_ROWS, 512), f32),
         scratch_shapes=[pltpu.VMEM((BRICKS, 384), f32)] + [pltpu.VMEM((TILE_ROWS, 128), f32)] * 4,
         compiler_params=pltpu.CompilerParams(vmem_limit_bytes=32 << 20),
-        cost_estimate=pl.CostEstimate(flops=1_600_000_000, bytes_accessed=3_000_000, transcendentals=0),
+        cost_estimate=pl.CostEstimate(flops=800_000_000, bytes_accessed=3_000_000, transcendentals=0),
         name="place_inner",
     )(arrived, inner)
 

time: 57.1 us -> 56.4 us (0.988)
  starting transfers between devices: 8.31 us -> 5.86 us
  waiting for transfers between devices: 0.72 us -> 2.56 us
    ppermute x4, starting transfers between devices: 8.31 us -> 5.86 us  [shifted(): return lax.ppermute(x, axis, [(i, (i + by) % size) for i in range(size)])]
    ppermute x4, waiting for transfers between devices: 0.72 us -> 2.56 us  [shifted(): return lax.ppermute(x, axis, [(i, (i + by) % size) for i in range(size)])]
  transfers between devices with their start and end apart: 4 -> 4, of which waited for: 2 -> 3; matrix products, arithmetic and copies ran while one was open for 0% -> 0% of each run, Pallas kernels for 7% -> 7%
where the time goes in v10:
time: 56.4 us; the launch traced here: 56.3 us
  blocking collectives  32.9 us (58%)
  Pallas kernels  14.1 us (25%)
  starting transfers between devices  5.86 us (10%)
  waiting for transfers between devices  2.56 us (5%)
  between operations  0.78 us (1%)
    all_to_all x1, blocking collectives, on_device(): lax.all_to_all(packed.reshape(N_DEST, MESSAGE // 4, 4, 128), ('rows', 'co...  32.9 us
    pallas_call x1, Pallas kernels, deposit_and_pack(): pl.pallas_call(deposit_kernel, out_shape=jax.ShapeDtypeStruct((N_DEST * M...  6.09 us
    ppermute x4, starting transfers between devices, shifted(): return lax.ppermute(x, axis, [(i, (i + by) % size) for i in range(size)])  5.86 us
    ppermute x4, waiting for transfers between devices, shifted(): return lax.ppermute(x, axis, [(i, (i + by) % size) for i in range(size)])  2.56 us
    pallas_call x1, Pallas kernels, all_levels(): pl.pallas_call(levels_kernel, out_shape=tuple((jax.ShapeDtypeStruct(shape...  2.32 us
    pallas_call x1, Pallas kernels, place_inner(): pl.pallas_call(place_inner_kernel, out_shape=jax.ShapeDtypeStruct((TILE_R...  2.07 us
    pallas_call x1, Pallas kernels, own_rows(): pl.pallas_call(own_rows_kernel, out_shape=(jax.ShapeDtypeStruct((2 * ROW_...  1.71 us
  transfers between devices with their start and end apart: 4, of which 3 were waited for; matrix products, arithmetic and copies ran while one was open for 0% of the time, Pallas kernels for 7%

profile of v10, /device:TPU:0, one launch (start us, length us, event | category | flops | bytes accessed | tf_op | source)
XLA Modules:
  0.0 56.3 jit_solution(13625367194309999504)
XLA Ops:
  0.6 6.1 %deposit.1 = f32[2560,128]{1,0:T(8,128)S(1)} custom-call(f32[2048,128]{1,0:T(8,128)} %bitcast.13, f32[512,256]{1,0:T(8,128)} %w_hbm.1, s32[1,512]{1,0:T(1,128)} %bitcast.14, s32[1,512]{1,0:T(1,128)} %bitcast.15, s32[1,512]{1,0:T(1,128)} %bitcast.16), custom_call_target="tpu_custom_call" | custom-call | tf_op jit(solution)/shard_map/deposit/pallas_call | solution.py:313
  6.7 32.9 %all_to_all.5 = f32[128,5,4,128]{3,2,1,0:T(4,128)S(1)} all-to-all(f32[128,5,4,128]{3,2,1,0:T(4,128)S(1)} %bitcast.10), channel_id=1, replica_groups=mesh['rows'=16,'cols'=8] {'rows','cols'}, dimensions={0} | all-to-all | bytes 2621440 | tf_op jit(solution)/shard_map/all_to_all | solution.py:735
  39.7 0.0 copy-start.1
  39.7 1.1 %place_edges.1 = (f32[272,128]{1,0:T(8,128)S(1)}, f32[176,128]{1,0:T(8,128)S(1)}, f32[40,128]{1,0:T(8,128)S(1)}) custom-call(f32[2560,128]{1,0:T(8,128)S(1)} %bitcast.11), custom_call_target="tpu_custom_call" | custom-call | flops 600000000 | bytes 2000000 | tf_op jit(solution)/shard_map/place_edges/pallas_call | solution.py:480
  40.7 0.0 collective-permute-start
  40.8 0.0 copy-start
  40.8 0.0 copy-start.7
  40.8 0.5 collective-permute-start.1
  41.3 0.0 copy-done.1
  41.3 2.1 %place_inner.1.own_ref = f32[272,512]{1,0:T(8,128)S(1)} custom-call(f32[2560,128]{1,0:T(8,128)S(1)} %bitcast.12, bf16[2,384,256]{2,1,0:T(8,128)(2,1)S(1)} %copy-done.1), custom_call_target="tpu_custom_call" | custom-call | flops 800000000 | bytes 3000000 | tf_op jit(solution)/shard_map/place_inner/pallas_call | solution.py:507
  43.4 0.0 copy-start.2
  43.4 0.0 copy-start.10
  43.4 0.0 copy-start.11
  43.4 1.8 %collective-permute-done.1.from_left_ref = f32[40,128]{1,0:T(8,128)S(1)} collective-permute-done((f32[40,128]{1,0:T(8,128)S(1)}, f32[40,128]{1,0:T(8,128)S(1)}, u32[]{:S(2)}, u32[]{:S(2)}) %collective-permute-start.1) | collective-permute-done | bytes 20512 | tf_op jit(solution)/shard_map/ppermute | solution.py:713
  45.2 0.0 collective-permute-done.from_right_ref
  45.2 0.0 copy-done
  45.2 0.0 copy-done.7
  45.2 0.8 %columns.1 = (f32[272,768]{1,0:T(8,128)S(1)}, f32[256,128]{1,0:T(8,128)S(1)}, f32[88,128]{1,0:T(8,128)S(1)}) custom-call(f32[272,512]{1,0:T(8,128)S(1)} %place_inner.1.own_ref, f32[272,128]{1,0:T(8,128)S(1)} %get-tuple-element.13.first_ref, f32[40,128]{1,0:T(8,128)S(1)} %get-tuple-element.14.to_right_ref, ...), custom_call_target="tpu_custom_call" | custom-call | flops 220000000 | bytes 2000000 | tf_op jit(solution)/shard_map/columns/pallas_call | solution.py:583
  46.0 0.7 %collective-permute-start.3 = (f32[88,128]{1,0:T(8,128)S(1)}, f32[88,128]{1,0:T(8,128)S(1)}, u32[]{:S(2)}, u32[]{:S(2)}) collective-permute-start(f32[88,128]{1,0:T(8,128)S(1)} %get-tuple-element.20), channel_id=1, source_target_pairs={{0,8},{8,16},{16,24},{24,32},{32,40},{40,48},{48,56},{56,64},{64,7... | collective-permute-start | bytes 135176 | tf_op jit(solution)/shard_map/ppermute | solution.py:713
  46.8 4.6 %collective-permute-start.2 = (f32[256,128]{1,0:T(8,128)S(1)}, f32[256,128]{1,0:T(8,128)S(1)}, u32[]{:S(2)}, u32[]{:S(2)}) collective-permute-start(f32[256,128]{1,0:T(8,128)S(1)} %get-tuple-element.19), channel_id=1, source_target_pairs={{0,120},{8,0},{16,8},{24,16},{32,24},{40,32},{48,40},{56,48},{64,5... | collective-permute-start | bytes 393224 | tf_op jit(solution)/shard_map/ppermute | solution.py:713
  51.4 0.0 copy-done.2
  51.4 0.0 copy-done.10
  51.4 0.0 copy-done.11
  51.4 0.0 copy-start.3
  51.4 0.0 copy-start.4
  51.4 0.0 copy-start.5
  51.4 0.0 copy-start.6
  51.4 0.0 copy-start.8
  51.4 0.0 copy-start.9
  51.5 1.7 %own_rows.1 = (f32[384,768]{1,0:T(8,128)S(1)}, f32[192,512]{1,0:T(8,128)S(1)}) custom-call(f32[272,768]{1,0:T(8,128)S(1)} %get-tuple-element.16.own_ref, bf16[2,384,272]{2,1,0:T(8,128)(2,1)S(1)} %copy-done.10, bf16[2,384,256]{2,1,0:T(8,128)(2,1)S(1)} %copy-done.1, bf16[2,256,256]{2,1,0:T(8,128)(2,1)S(1)} %copy-done.2, bf16[2,192,192]{2,1,0:T(8,128)(2,1)S(1)} %copy-done.11), custom_call_target="tpu_custom_call" | custom-call | flops 4800000000 | bytes 20000000 | tf_op jit(solution)/shard_map/own_rows/pallas_call | solution.py:611
  53.2 0.2 collective-permute-done.3.above_ref
  53.4 0.5 collective-permute-done.2.below_ref
  53.9 0.0 copy-done.3
  53.9 0.0 copy-done.4
  53.9 0.0 copy-done.5
  53.9 0.0 copy-done.6
  53.9 0.0 copy-done.8
  53.9 0.0 copy-done.9
  53.9 2.3 %levels.1 = (f32[128,256]{1,0:T(8,128)}, f32[64,128]{1,0:T(8,128)}, f32[32,64]{1,0:T(8,128)}, f32[16,32]{1,0:T(8,128)}, f32[16,32]{1,0:T(8,128)}) custom-call(f32[384,768]{1,0:T(8,128)S(1)} %get-tuple-element.17.part_ref, f32[192,512]{1,0:T(8,128)S(1)} %get-tuple-element.18.second_ref, f32[256,128]{1,0:T(8,128)S(1)} %collective-permute-done.2.below_ref, ...), custom_call_target="tpu_custom_call" | custom-call | tf_op jit(solution)/shard_map/levels/pallas_call | solution.py:702
Async XLA Ops:
  39.7 1.6 %copy-start.1 = (bf16[2,384,256]{2,1,0:T(8,128)(2,1)S(1)}, bf16[2,384,256]{2,1,0:T(8,128)(2,1)}, u32[]{:S(2)}) copy-start(bf16[2,384,256]{2,1,0:T(8,128)(2,1)} %constant.29.clone.inner_ref) | copy-start | bytes 1179652
  40.7 4.5 %collective-permute-start = (f32[176,128]{1,0:T(8,128)S(1)}, f32[176,128]{1,0:T(8,128)S(1)}, u32[]{:S(2)}, u32[]{:S(2)}) collective-permute-start(f32[176,128]{1,0:T(8,128)S(1)} %get-tuple-element.15), channel_id=1, source_target_pairs={{0,7},{1,0},{2,1},{3,2},{4,3},{5,4},{6,5},{7,6},{8,15},{9,8},{10,9... | collective-permute-start | bytes 270344 | tf_op jit(solution)/shard_map/ppermute | solution.py:713
  40.8 4.5 %copy-start = (bf16[2,256,512]{2,1,0:T(8,128)(2,1)S(1)}, bf16[2,256,512]{2,1,0:T(8,128)(2,1)}, u32[]{:S(2)}) copy-start(bf16[2,256,512]{2,1,0:T(8,128)(2,1)} %constant.30.clone.outer_ref) | copy-start | bytes 1572868
  40.8 4.5 %copy-start.7 = (bf16[2,64,80]{2,1,0:T(8,128)(2,1)S(1)}, bf16[2,64,80]{2,1,0:T(8,128)(2,1)}, u32[]{:S(2)}) copy-start(bf16[2,64,80]{2,1,0:T(8,128)(2,1)} %constant.25.clone.below_ref) | copy-start | bytes 61444
  40.8 4.4 %collective-permute-start.1 = (f32[40,128]{1,0:T(8,128)S(1)}, f32[40,128]{1,0:T(8,128)S(1)}, u32[]{:S(2)}, u32[]{:S(2)}) collective-permute-start(f32[40,128]{1,0:T(8,128)S(1)} %get-tuple-element.14.to_right_ref), channel_id=1, source_target_pairs={{0,1},{1,2},{2,3},{3,4},{4,5},{5,6},{6,7},{7,0},{8,9},{9,10},{10,1... | collective-permute-start | bytes 61448 | tf_op jit(solution)/shard_map/ppermute | solution.py:713
  43.4 8.0 %copy-start.2 = (bf16[2,256,256]{2,1,0:T(8,128)(2,1)S(1)}, bf16[2,256,256]{2,1,0:T(8,128)(2,1)}, u32[]{:S(2)}) copy-start(bf16[2,256,256]{2,1,0:T(8,128)(2,1)} %constant.26.clone.rest_ref.refs_0_) | copy-start | bytes 786436
  43.4 8.0 %copy-start.10 = (bf16[2,384,272]{2,1,0:T(8,128)(2,1)S(1)}, bf16[2,384,272]{2,1,0:T(8,128)(2,1)}, u32[]{:S(2)}) copy-start(bf16[2,384,272]{2,1,0:T(8,128)(2,1)} %constant.31.clone.table_ref) | copy-start | bytes 1253380
  43.4 8.0 %copy-start.11 = (bf16[2,192,192]{2,1,0:T(8,128)(2,1)S(1)}, bf16[2,192,192]{2,1,0:T(8,128)(2,1)}, u32[]{:S(2)}) copy-start(bf16[2,192,192]{2,1,0:T(8,128)(2,1)} %constant.32.clone.rows_ref) | copy-start | bytes 442372
  46.0 7.4 %collective-permute-start.3 = (f32[88,128]{1,0:T(8,128)S(1)}, f32[88,128]{1,0:T(8,128)S(1)}, u32[]{:S(2)}, u32[]{:S(2)}) collective-permute-start(f32[88,128]{1,0:T(8,128)S(1)} %get-tuple-element.20), channel_id=1, source_target_pairs={{0,8},{8,16},{16,24},{24,32},{32,40},{40,48},{48,56},{56,64},{64,7... | collective-permute-start | bytes 135176 | tf_op jit(solution)/shard_map/ppermute | solution.py:713
  46.8 7.1 %collective-permute-start.2 = (f32[256,128]{1,0:T(8,128)S(1)}, f32[256,128]{1,0:T(8,128)S(1)}, u32[]{:S(2)}, u32[]{:S(2)}) collective-permute-start(f32[256,128]{1,0:T(8,128)S(1)} %get-tuple-element.19), channel_id=1, source_target_pairs={{0,120},{8,0},{16,8},{24,16},{32,24},{40,32},{48,40},{56,48},{64,5... | collective-permute-start | bytes 393224 | tf_op jit(solution)/shard_map/ppermute | solution.py:713
  51.4 2.5 %copy-start.3 = (bf16[2,256,256]{2,1,0:T(8,128)(2,1)S(1)}, bf16[2,256,256]{2,1,0:T(8,128)(2,1)}, u32[]{:S(2)}) copy-start(bf16[2,256,256]{2,1,0:T(8,128)(2,1)} %constant.27.clone.refs_1_) | copy-start | bytes 786436
  51.4 2.5 %copy-start.4 = (bf16[2,128,256]{2,1,0:T(8,128)(2,1)S(1)}, bf16[2,128,256]{2,1,0:T(8,128)(2,1)}, u32[]{:S(2)}) copy-start(bf16[2,128,256]{2,1,0:T(8,128)(2,1)} %constant.28.clone.refs_2_) | copy-start | bytes 393220
  51.4 2.5 %copy-start.5 = (bf16[2,192,64]{2,1,0:T(8,128)(2,1)S(1)}, bf16[2,192,64]{2,1,0:T(8,128)(2,1)}, u32[]{:S(2)}) copy-start(bf16[2,192,64]{2,1,0:T(8,128)(2,1)} %constant.35.clone.added_ref) | copy-start | bytes 147460
  51.4 2.5 %copy-start.6 = (bf16[2,96,96]{2,1,0:T(8,128)(2,1)S(1)}, bf16[2,96,96]{2,1,0:T(8,128)(2,1)}, u32[]{:S(2)}) copy-start(bf16[2,96,96]{2,1,0:T(8,128)(2,1)} %constant.33.clone.refs_3_) | copy-start | bytes 110596
  51.4 2.5 %copy-start.8 = (bf16[2,48,48]{2,1,0:T(8,128)(2,1)S(1)}, bf16[2,48,48]{2,1,0:T(8,128)(2,1)}, u32[]{:S(2)}) copy-start(bf16[2,48,48]{2,1,0:T(8,128)(2,1)} %constant.34.clone.refs_4_) | copy-start | bytes 27652
  51.4 2.5 %copy-start.9 = (bf16[2,32,24]{2,1,0:T(8,128)(2,1)S(1)}, bf16[2,32,24]{2,1,0:T(8,128)(2,1)}, u32[]{:S(2)}) copy-start(bf16[2,32,24]{2,1,0:T(8,128)(2,1)} %constant.24.clone.table_ref) | copy-start | bytes 9220

commit v11 on v10

--- a/solution.py
+++ b/solution.py
@@ -525,7 +525,7 @@
 
 
 def columns_kernel(
-    own_ref, first_ref, to_right_ref, from_right_ref, from_left_ref, outer_ref, below_ref, out_ref, up_ref, down_ref
+    own_ref, first_ref, to_right_ref, from_right_ref, from_left_ref, outer_ref, out_ref, down_ref
 ):
     lane8 = iota((8, 128), 1)
     none = jnp.zeros((8, 128), f32)
@@ -561,15 +561,6 @@
         own_ref[:, 384:512] + outer[:, 384:512],
         outer[:, 128:256],
     ]
-    low = mm3_left(below_ref, jnp.concatenate([piece[0:UP_ROWS] for piece in pieces[0:3]], axis=1))
-    high = mm3_left(below_ref[:, 0:32, :], jnp.concatenate([piece[0:UP_ROWS] for piece in pieces[3:6]], axis=1))
-    for part in range(2):
-        rows16 = slice(part * 16, part * 16 + 16)
-        fives = pack_tiles([half[rows16, at * 128 : (at + 1) * 128] for half in (low, high) for at in range(3)])
-        for at, tile in enumerate(fives):
-            up_ref[part * 80 + at * 16 : part * 80 + at * 16 + 16, :] = tile
-    for at in range(3):
-        up_ref[160 + at * 32 : 192 + at * 32, :] = low[32:64, at * 128 : (at + 1) * 128]
     for at, tile in enumerate(pack_tiles([piece[DOWN_FROM : DOWN_FROM + 24] for piece in pieces])):
         down_ref[at * 16 : at * 16 + 16, :] = tile[0:16]
         down_ref[80 + at : 81 + at, :] = tile[16:17]
@@ -578,19 +569,41 @@
         out_ref[:, at * 128 : (at + 1) * 128] = piece
 
 
-def outer_columns(own, first, to_right, from_right, from_left, outer, below):
+def outer_columns(own, first, to_right, from_right, from_left, outer):
     width = 2 * COL_ROOM[0]
     return pl.pallas_call(
         columns_kernel,
         out_shape=(
             jax.ShapeDtypeStruct((TILE_ROWS, width), f32),
-            jax.ShapeDtypeStruct((UP_MESSAGE, 128), f32),
             jax.ShapeDtypeStruct((DOWN_MESSAGE, 128), f32),
         ),
         compiler_params=pltpu.CompilerParams(vmem_limit_bytes=32 << 20),
         cost_estimate=pl.CostEstimate(flops=220_000_000, bytes_accessed=2_000_000, transcendentals=0),
         name="columns",
-    )(own, first, to_right, from_right, from_left, outer, below)
+    )(own, first, to_right, from_right, from_left, outer)
+
+
+def upward_kernel(own_ref, below_ref, up_ref):
+    half = COL_ROOM[0]
+    low = mm3_left(below_ref, own_ref[0:UP_ROWS, 0:half])
+    high = mm3_left(below_ref[:, 0:32, :], own_ref[0:UP_ROWS, half : 2 * half])
+    for part in range(2):
+        rows16 = slice(part * 16, part * 16 + 16)
+        fives = pack_tiles([side[rows16, at * 128 : (at + 1) * 128] for side in (low, high) for at in range(3)])
+        for at, tile in enumerate(fives):
+            up_ref[part * 80 + at * 16 : part * 80 + at * 16 + 16, :] = tile
+    for at in range(3):
+        up_ref[160 + at * 32 : 192 + at * 32, :] = low[32:64, at * 128 : (at + 1) * 128]
+
+
+def upward(own, below):
+    return pl.pallas_call(
+        upward_kernel,
+        out_shape=jax.ShapeDtypeStruct((UP_MESSAGE, 128), f32),
+        compiler_params=pltpu.CompilerParams(vmem_limit_bytes=32 << 20),
+        cost_estimate=pl.CostEstimate(flops=2_000_000_000, bytes_accessed=6_000_000, transcendentals=0),
+        name="upward",
+    )(own, below)
 
 
 def second_columns(current, inner, rest):
@@ -719,11 +732,9 @@
     from_right = shifted(to_left, "cols", -1)
     from_left = shifted(to_right, "cols", 1)
     inner = place_inner(arrived, table["inner"])
-    own, to_up, to_down = outer_columns(
-        inner, first, to_right, from_right, from_left, table["outer"], table["below"]
-    )
+    own, to_down = outer_columns(inner, first, to_right, from_right, from_left, table["outer"])
     above = shifted(to_down, "rows", 1)
-    below = shifted(to_up, "rows", -1)
+    below = shifted(upward(own, table["below"]), "rows", -1)
     part, second = own_rows(own, table["own"], table["inner"], table["cols"][0], table["rows"][0])
     return all_levels(
         part, second, below, above, table["above"], table["inner"], table["second"], table["cols"], table["rows"][1:]

time: 56.4 us -> 56.6 us (level)
  transfers between devices with their start and end apart: 4 -> 4, of which waited for: 3 -> 2; matrix products, arithmetic and copies ran while one was open for 0% -> 0% of each run, Pallas kernels for 7% -> 7%
where the time goes in v11:
time: 56.6 us; the launch traced here: 56.4 us
  blocking collectives  32.9 us (58%)
  Pallas kernels  14.1 us (25%)
  starting transfers between devices  5.93 us (10%)
  waiting for transfers between devices  2.61 us (5%)
  between operations  0.76 us (1%)
    all_to_all x1, blocking collectives, on_device(): lax.all_to_all(packed.reshape(N_DEST, MESSAGE // 4, 4, 128), ('rows', 'co...  32.9 us
    pallas_call x1, Pallas kernels, deposit_and_pack(): pl.pallas_call(deposit_kernel, out_shape=jax.ShapeDtypeStruct((N_DEST * M...  6.09 us
    ppermute x4, starting transfers between devices, shifted(): return lax.ppermute(x, axis, [(i, (i + by) % size) for i in range(size)])  5.93 us
    ppermute x4, waiting for transfers between devices, shifted(): return lax.ppermute(x, axis, [(i, (i + by) % size) for i in range(size)])  2.61 us
    pallas_call x1, Pallas kernels, all_levels(): pl.pallas_call(levels_kernel, out_shape=tuple((jax.ShapeDtypeStruct(shape...  2.32 us
    pallas_call x1, Pallas kernels, place_inner(): pl.pallas_call(place_inner_kernel, out_shape=jax.ShapeDtypeStruct((TILE_R...  2.09 us
    pallas_call x1, Pallas kernels, own_rows(): pl.pallas_call(own_rows_kernel, out_shape=(jax.ShapeDtypeStruct((2 * ROW_...  1.73 us
  transfers between devices with their start and end apart: 4, of which 2 were waited for; matrix products, arithmetic and copies ran while one was open for 0% of the time, Pallas kernels for 7%

profile of v11, /device:TPU:0, one launch (start us, length us, event | category | flops | bytes accessed | tf_op | source)
XLA Modules:
  0.0 56.4 jit_solution(3949123659867663386)
XLA Ops:
  0.6 6.1 %deposit.1 = f32[2560,128]{1,0:T(8,128)S(1)} custom-call(f32[2048,128]{1,0:T(8,128)} %bitcast.13, f32[512,256]{1,0:T(8,128)} %w_hbm.1, s32[1,512]{1,0:T(1,128)} %bitcast.14, s32[1,512]{1,0:T(1,128)} %bitcast.15, s32[1,512]{1,0:T(1,128)} %bitcast.16), custom_call_target="tpu_custom_call" | custom-call | tf_op jit(solution)/shard_map/deposit/pallas_call | solution.py:313
  6.7 32.9 %all_to_all.5 = f32[128,5,4,128]{3,2,1,0:T(4,128)S(1)} all-to-all(f32[128,5,4,128]{3,2,1,0:T(4,128)S(1)} %bitcast.10), channel_id=1, replica_groups=mesh['rows'=16,'cols'=8] {'rows','cols'}, dimensions={0} | all-to-all | bytes 2621440 | tf_op jit(solution)/shard_map/all_to_all | solution.py:746
  39.7 0.0 copy-start.1
  39.7 1.1 %place_edges.1 = (f32[272,128]{1,0:T(8,128)S(1)}, f32[176,128]{1,0:T(8,128)S(1)}, f32[40,128]{1,0:T(8,128)S(1)}) custom-call(f32[2560,128]{1,0:T(8,128)S(1)} %bitcast.11), custom_call_target="tpu_custom_call" | custom-call | flops 600000000 | bytes 2000000 | tf_op jit(solution)/shard_map/place_edges/pallas_call | solution.py:480
  40.7 0.0 collective-permute-start
  40.8 0.0 copy-start
  40.8 0.5 collective-permute-start.1
  41.3 0.0 copy-done.1
  41.3 2.1 %place_inner.1.own_ref = f32[272,512]{1,0:T(8,128)S(1)} custom-call(f32[2560,128]{1,0:T(8,128)S(1)} %bitcast.12, bf16[2,384,256]{2,1,0:T(8,128)(2,1)S(1)} %copy-done.1), custom_call_target="tpu_custom_call" | custom-call | flops 800000000 | bytes 3000000 | tf_op jit(solution)/shard_map/place_inner/pallas_call | solution.py:507
  43.4 0.0 copy-start.11
  43.4 1.8 %collective-permute-done.1.from_left_ref = f32[40,128]{1,0:T(8,128)S(1)} collective-permute-done((f32[40,128]{1,0:T(8,128)S(1)}, f32[40,128]{1,0:T(8,128)S(1)}, u32[]{:S(2)}, u32[]{:S(2)}) %collective-permute-start.1) | collective-permute-done | bytes 20512 | tf_op jit(solution)/shard_map/ppermute | solution.py:726
  45.2 0.0 collective-permute-done.from_right_ref
  45.2 0.0 copy-done
  45.2 0.6 columns.1
  45.8 0.7 %collective-permute-start.3 = (f32[88,128]{1,0:T(8,128)S(1)}, f32[88,128]{1,0:T(8,128)S(1)}, u32[]{:S(2)}, u32[]{:S(2)}) collective-permute-start(f32[88,128]{1,0:T(8,128)S(1)} %get-tuple-element.18), channel_id=1, source_target_pairs={{0,8},{8,16},{16,24},{24,32},{32,40},{40,48},{48,56},{56,64},{64,7... | collective-permute-start | bytes 135176 | tf_op jit(solution)/shard_map/ppermute | solution.py:726
  46.5 0.0 copy-done.11
  46.5 0.0 copy-start.2
  46.5 0.0 copy-start.9
  46.5 0.0 copy-start.10
  46.5 0.3 upward.1
  46.8 0.0 copy-start.3
  46.8 0.0 copy-start.4
  46.8 0.0 copy-start.5
  46.8 0.0 copy-start.6
  46.8 0.0 copy-start.7
  46.9 0.0 copy-start.8
  46.9 4.7 %collective-permute-start.2 = (f32[256,128]{1,0:T(8,128)S(1)}, f32[256,128]{1,0:T(8,128)S(1)}, u32[]{:S(2)}, u32[]{:S(2)}) collective-permute-start(f32[256,128]{1,0:T(8,128)S(1)} %upward.1), channel_id=1, source_target_pairs={{0,120},{8,0},{16,8},{24,16},{32,24},{40,32},{48,40},{56,48},{64,5... | collective-permute-start | bytes 393224 | tf_op jit(solution)/shard_map/ppermute | solution.py:726
  51.6 0.0 copy-done.2
  51.6 0.0 copy-done.9
  51.6 0.0 copy-done.10
  51.6 1.7 %own_rows.1 = (f32[384,768]{1,0:T(8,128)S(1)}, f32[192,512]{1,0:T(8,128)S(1)}) custom-call(f32[272,768]{1,0:T(8,128)S(1)} %get-tuple-element.15.own_ref, bf16[2,384,272]{2,1,0:T(8,128)(2,1)S(1)} %copy-done.9, bf16[2,384,256]{2,1,0:T(8,128)(2,1)S(1)} %copy-done.1, bf16[2,256,256]{2,1,0:T(8,128)(2,1)S(1)} %copy-done.2, bf16[2,192,192]{2,1,0:T(8,128)(2,1)S(1)} %copy-done.10), custom_call_target="tpu_custom_call" | custom-call | flops 4800000000 | bytes 20000000 | tf_op jit(solution)/shard_map/own_rows/pallas_call | solution.py:624
  53.3 0.0 collective-permute-done.3.above_ref
  53.3 0.8 %collective-permute-done.2.below_ref = f32[256,128]{1,0:T(8,128)S(1)} collective-permute-done((f32[256,128]{1,0:T(8,128)S(1)}, f32[256,128]{1,0:T(8,128)S(1)}, u32[]{:S(2)}, u32[]{:S(2)}) %collective-permute-start.2) | collective-permute-done | bytes 131104 | tf_op jit(solution)/shard_map/ppermute | solution.py:726
  54.1 0.0 copy-done.3
  54.1 0.0 copy-done.4
  54.1 0.0 copy-done.5
  54.1 0.0 copy-done.6
  54.1 0.0 copy-done.7
  54.1 0.0 copy-done.8
  54.1 2.3 %levels.1 = (f32[128,256]{1,0:T(8,128)}, f32[64,128]{1,0:T(8,128)}, f32[32,64]{1,0:T(8,128)}, f32[16,32]{1,0:T(8,128)}, f32[16,32]{1,0:T(8,128)}) custom-call(f32[384,768]{1,0:T(8,128)S(1)} %get-tuple-element.16.part_ref, f32[192,512]{1,0:T(8,128)S(1)} %get-tuple-element.17.second_ref, f32[256,128]{1,0:T(8,128)S(1)} %collective-permute-done.2.below_ref, ...), custom_call_target="tpu_custom_call" | custom-call | tf_op jit(solution)/shard_map/levels/pallas_call | solution.py:715
Async XLA Ops:
  39.7 1.6 %copy-start.1 = (bf16[2,384,256]{2,1,0:T(8,128)(2,1)S(1)}, bf16[2,384,256]{2,1,0:T(8,128)(2,1)}, u32[]{:S(2)}) copy-start(bf16[2,384,256]{2,1,0:T(8,128)(2,1)} %constant.29.clone.inner_ref) | copy-start | bytes 1179652
  40.7 4.5 %collective-permute-start = (f32[176,128]{1,0:T(8,128)S(1)}, f32[176,128]{1,0:T(8,128)S(1)}, u32[]{:S(2)}, u32[]{:S(2)}) collective-permute-start(f32[176,128]{1,0:T(8,128)S(1)} %get-tuple-element.14), channel_id=1, source_target_pairs={{0,7},{1,0},{2,1},{3,2},{4,3},{5,4},{6,5},{7,6},{8,15},{9,8},{10,9... | collective-permute-start | bytes 270344 | tf_op jit(solution)/shard_map/ppermute | solution.py:726
  40.8 4.4 %copy-start = (bf16[2,256,512]{2,1,0:T(8,128)(2,1)S(1)}, bf16[2,256,512]{2,1,0:T(8,128)(2,1)}, u32[]{:S(2)}) copy-start(bf16[2,256,512]{2,1,0:T(8,128)(2,1)} %constant.30.clone.outer_ref) | copy-start | bytes 1572868
  40.8 4.4 %collective-permute-start.1 = (f32[40,128]{1,0:T(8,128)S(1)}, f32[40,128]{1,0:T(8,128)S(1)}, u32[]{:S(2)}, u32[]{:S(2)}) collective-permute-start(f32[40,128]{1,0:T(8,128)S(1)} %get-tuple-element.13.to_right_ref), channel_id=1, source_target_pairs={{0,1},{1,2},{2,3},{3,4},{4,5},{5,6},{6,7},{7,0},{8,9},{9,10},{10,1... | collective-permute-start | bytes 61448 | tf_op jit(solution)/shard_map/ppermute | solution.py:726
  43.4 3.2 %copy-start.11 = (bf16[2,64,80]{2,1,0:T(8,128)(2,1)S(1)}, bf16[2,64,80]{2,1,0:T(8,128)(2,1)}, u32[]{:S(2)}) copy-start(bf16[2,64,80]{2,1,0:T(8,128)(2,1)} %constant.25.clone.below_ref) | copy-start | bytes 61444
  45.8 7.5 %collective-permute-start.3 = (f32[88,128]{1,0:T(8,128)S(1)}, f32[88,128]{1,0:T(8,128)S(1)}, u32[]{:S(2)}, u32[]{:S(2)}) collective-permute-start(f32[88,128]{1,0:T(8,128)S(1)} %get-tuple-element.18), channel_id=1, source_target_pairs={{0,8},{8,16},{16,24},{24,32},{32,40},{40,48},{48,56},{56,64},{64,7... | collective-permute-start | bytes 135176 | tf_op jit(solution)/shard_map/ppermute | solution.py:726
  46.5 5.0 %copy-start.2 = (bf16[2,256,256]{2,1,0:T(8,128)(2,1)S(1)}, bf16[2,256,256]{2,1,0:T(8,128)(2,1)}, u32[]{:S(2)}) copy-start(bf16[2,256,256]{2,1,0:T(8,128)(2,1)} %constant.26.clone.rest_ref.refs_0_) | copy-start | bytes 786436
  46.5 5.0 %copy-start.9 = (bf16[2,384,272]{2,1,0:T(8,128)(2,1)S(1)}, bf16[2,384,272]{2,1,0:T(8,128)(2,1)}, u32[]{:S(2)}) copy-start(bf16[2,384,272]{2,1,0:T(8,128)(2,1)} %constant.31.clone.table_ref) | copy-start | bytes 1253380
  46.5 5.0 %copy-start.10 = (bf16[2,192,192]{2,1,0:T(8,128)(2,1)S(1)}, bf16[2,192,192]{2,1,0:T(8,128)(2,1)}, u32[]{:S(2)}) copy-start(bf16[2,192,192]{2,1,0:T(8,128)(2,1)} %constant.32.clone.rows_ref) | copy-start | bytes 442372
  46.8 7.3 %copy-start.3 = (bf16[2,256,256]{2,1,0:T(8,128)(2,1)S(1)}, bf16[2,256,256]{2,1,0:T(8,128)(2,1)}, u32[]{:S(2)}) copy-start(bf16[2,256,256]{2,1,0:T(8,128)(2,1)} %constant.27.clone.refs_1_) | copy-start | bytes 786436
  46.8 7.3 %copy-start.4 = (bf16[2,128,256]{2,1,0:T(8,128)(2,1)S(1)}, bf16[2,128,256]{2,1,0:T(8,128)(2,1)}, u32[]{:S(2)}) copy-start(bf16[2,128,256]{2,1,0:T(8,128)(2,1)} %constant.28.clone.refs_2_) | copy-start | bytes 393220
  46.8 7.3 %copy-start.5 = (bf16[2,192,64]{2,1,0:T(8,128)(2,1)S(1)}, bf16[2,192,64]{2,1,0:T(8,128)(2,1)}, u32[]{:S(2)}) copy-start(bf16[2,192,64]{2,1,0:T(8,128)(2,1)} %constant.35.clone.added_ref) | copy-start | bytes 147460
  46.8 7.3 %copy-start.6 = (bf16[2,96,96]{2,1,0:T(8,128)(2,1)S(1)}, bf16[2,96,96]{2,1,0:T(8,128)(2,1)}, u32[]{:S(2)}) copy-start(bf16[2,96,96]{2,1,0:T(8,128)(2,1)} %constant.33.clone.refs_3_) | copy-start | bytes 110596
  46.8 7.3 %copy-start.7 = (bf16[2,48,48]{2,1,0:T(8,128)(2,1)S(1)}, bf16[2,48,48]{2,1,0:T(8,128)(2,1)}, u32[]{:S(2)}) copy-start(bf16[2,48,48]{2,1,0:T(8,128)(2,1)} %constant.34.clone.refs_4_) | copy-start | bytes 27652
  46.9 7.3 %copy-start.8 = (bf16[2,32,24]{2,1,0:T(8,128)(2,1)S(1)}, bf16[2,32,24]{2,1,0:T(8,128)(2,1)}, u32[]{:S(2)}) copy-start(bf16[2,32,24]{2,1,0:T(8,128)(2,1)} %constant.24.clone.table_ref) | copy-start | bytes 9220
  46.9 7.2 %collective-permute-start.2 = (f32[256,128]{1,0:T(8,128)S(1)}, f32[256,128]{1,0:T(8,128)S(1)}, u32[]{:S(2)}, u32[]{:S(2)}) collective-permute-start(f32[256,128]{1,0:T(8,128)S(1)} %upward.1), channel_id=1, source_target_pairs={{0,120},{8,0},{16,8},{24,16},{32,24},{40,32},{48,40},{56,48},{64,5... | collective-permute-start | bytes 393224 | tf_op jit(solution)/shard_map/ppermute | solution.py:726

commit v12 on v10

--- a/solution.py
+++ b/solution.py
@@ -671,11 +671,13 @@
         now = jnp.maximum(jnp.maximum(jnp.abs(detail_a), jnp.abs(detail_b)), jnp.abs(detail_c))
         if peak is not None:
             now = jnp.maximum(now, peak)
-        wide = jnp.maximum(now, jnp.maximum(pltpu.roll(now, 1, 1), pltpu.roll(now, room_c - 1, 1)))
-        wide = jnp.maximum(wide, jnp.maximum(pltpu.roll(wide, 1, 0), pltpu.roll(wide, room_r - 1, 0)))
         n_r = R_DEV >> (level + 1)
         n_c = C_DEV >> (level + 1)
-        leader_refs[level][...] = wide[:n_r, :n_c]
+        after = pltpu.roll(now[: n_r + 8], n_r + 7, 0)[:n_r]
+        before = pltpu.roll(jnp.concatenate([now[room_r - 8 :], now[:n_r]], axis=0), 1, 0)[8:]
+        tall = jnp.maximum(now[:n_r], jnp.maximum(after, before))
+        wide = jnp.maximum(tall, jnp.maximum(pltpu.roll(tall, 1, 1), pltpu.roll(tall, room_c - 1, 1)))
+        leader_refs[level][...] = wide[:, :n_c]
         if level < 3:
             pairs = jnp.maximum(now, pltpu.roll(now, room_c - 1, 1))
             pooled = []

time: 56.4 us -> 56.4 us (level)
  no operation moved by 1% of the time
where the time goes in v12:
time: 56.4 us; the launch traced here: 56.3 us
  blocking collectives  32.9 us (58%)
  Pallas kernels  14.1 us (25%)
  starting transfers between devices  5.86 us (10%)
  waiting for transfers between devices  2.56 us (5%)
  between operations  0.78 us (1%)
    all_to_all x1, blocking collectives, on_device(): lax.all_to_all(packed.reshape(N_DEST, MESSAGE // 4, 4, 128), ('rows', 'co...  32.9 us
    pallas_call x1, Pallas kernels, deposit_and_pack(): pl.pallas_call(deposit_kernel, out_shape=jax.ShapeDtypeStruct((N_DEST * M...  6.09 us
    ppermute x4, starting transfers between devices, shifted(): return lax.ppermute(x, axis, [(i, (i + by) % size) for i in range(size)])  5.86 us
    ppermute x4, waiting for transfers between devices, shifted(): return lax.ppermute(x, axis, [(i, (i + by) % size) for i in range(size)])  2.56 us
    pallas_call x1, Pallas kernels, all_levels(): pl.pallas_call(levels_kernel, out_shape=tuple((jax.ShapeDtypeStruct(shape...  2.32 us
    pallas_call x1, Pallas kernels, place_inner(): pl.pallas_call(place_inner_kernel, out_shape=jax.ShapeDtypeStruct((TILE_R...  2.07 us
    pallas_call x1, Pallas kernels, own_rows(): pl.pallas_call(own_rows_kernel, out_shape=(jax.ShapeDtypeStruct((2 * ROW_...  1.71 us
  transfers between devices with their start and end apart: 4, of which 3 were waited for; matrix products, arithmetic and copies ran while one was open for 0% of the time, Pallas kernels for 7%

profile of v12, /device:TPU:0, one launch (start us, length us, event | category | flops | bytes accessed | tf_op | source)
XLA Modules:
  0.0 56.3 jit_solution(13009370379123036983)
XLA Ops:
  0.6 6.1 %deposit.1 = f32[2560,128]{1,0:T(8,128)S(1)} custom-call(f32[2048,128]{1,0:T(8,128)} %bitcast.13, f32[512,256]{1,0:T(8,128)} %w_hbm.1, s32[1,512]{1,0:T(1,128)} %bitcast.14, s32[1,512]{1,0:T(1,128)} %bitcast.15, s32[1,512]{1,0:T(1,128)} %bitcast.16), custom_call_target="tpu_custom_call" | custom-call | tf_op jit(solution)/shard_map/deposit/pallas_call | solution.py:313
  6.7 32.9 %all_to_all.5 = f32[128,5,4,128]{3,2,1,0:T(4,128)S(1)} all-to-all(f32[128,5,4,128]{3,2,1,0:T(4,128)S(1)} %bitcast.10), channel_id=1, replica_groups=mesh['rows'=16,'cols'=8] {'rows','cols'}, dimensions={0} | all-to-all | bytes 2621440 | tf_op jit(solution)/shard_map/all_to_all | solution.py:737
  39.7 0.0 copy-start.1
  39.7 1.1 %place_edges.1 = (f32[272,128]{1,0:T(8,128)S(1)}, f32[176,128]{1,0:T(8,128)S(1)}, f32[40,128]{1,0:T(8,128)S(1)}) custom-call(f32[2560,128]{1,0:T(8,128)S(1)} %bitcast.11), custom_call_target="tpu_custom_call" | custom-call | flops 600000000 | bytes 2000000 | tf_op jit(solution)/shard_map/place_edges/pallas_call | solution.py:480
  40.7 0.0 collective-permute-start
  40.8 0.0 copy-start
  40.8 0.0 copy-start.7
  40.8 0.5 collective-permute-start.1
  41.3 0.0 copy-done.1
  41.3 2.1 %place_inner.1.own_ref = f32[272,512]{1,0:T(8,128)S(1)} custom-call(f32[2560,128]{1,0:T(8,128)S(1)} %bitcast.12, bf16[2,384,256]{2,1,0:T(8,128)(2,1)S(1)} %copy-done.1), custom_call_target="tpu_custom_call" | custom-call | flops 800000000 | bytes 3000000 | tf_op jit(solution)/shard_map/place_inner/pallas_call | solution.py:507
  43.4 0.0 copy-start.2
  43.4 0.0 copy-start.10
  43.4 0.0 copy-start.11
  43.4 1.8 %collective-permute-done.1.from_left_ref = f32[40,128]{1,0:T(8,128)S(1)} collective-permute-done((f32[40,128]{1,0:T(8,128)S(1)}, f32[40,128]{1,0:T(8,128)S(1)}, u32[]{:S(2)}, u32[]{:S(2)}) %collective-permute-start.1) | collective-permute-done | bytes 20512 | tf_op jit(solution)/shard_map/ppermute | solution.py:715
  45.2 0.0 collective-permute-done.from_right_ref
  45.2 0.0 copy-done
  45.2 0.0 copy-done.7
  45.2 0.8 %columns.1 = (f32[272,768]{1,0:T(8,128)S(1)}, f32[256,128]{1,0:T(8,128)S(1)}, f32[88,128]{1,0:T(8,128)S(1)}) custom-call(f32[272,512]{1,0:T(8,128)S(1)} %place_inner.1.own_ref, f32[272,128]{1,0:T(8,128)S(1)} %get-tuple-element.13.first_ref, f32[40,128]{1,0:T(8,128)S(1)} %get-tuple-element.14.to_right_ref, ...), custom_call_target="tpu_custom_call" | custom-call | flops 220000000 | bytes 2000000 | tf_op jit(solution)/shard_map/columns/pallas_call | solution.py:583
  46.0 0.7 %collective-permute-start.3 = (f32[88,128]{1,0:T(8,128)S(1)}, f32[88,128]{1,0:T(8,128)S(1)}, u32[]{:S(2)}, u32[]{:S(2)}) collective-permute-start(f32[88,128]{1,0:T(8,128)S(1)} %get-tuple-element.20), channel_id=1, source_target_pairs={{0,8},{8,16},{16,24},{24,32},{32,40},{40,48},{48,56},{56,64},{64,7... | collective-permute-start | bytes 135176 | tf_op jit(solution)/shard_map/ppermute | solution.py:715
  46.8 4.6 %collective-permute-start.2 = (f32[256,128]{1,0:T(8,128)S(1)}, f32[256,128]{1,0:T(8,128)S(1)}, u32[]{:S(2)}, u32[]{:S(2)}) collective-permute-start(f32[256,128]{1,0:T(8,128)S(1)} %get-tuple-element.19), channel_id=1, source_target_pairs={{0,120},{8,0},{16,8},{24,16},{32,24},{40,32},{48,40},{56,48},{64,5... | collective-permute-start | bytes 393224 | tf_op jit(solution)/shard_map/ppermute | solution.py:715
  51.4 0.0 copy-done.2
  51.4 0.0 copy-done.10
  51.4 0.0 copy-done.11
  51.4 0.0 copy-start.3
  51.4 0.0 copy-start.4
  51.4 0.0 copy-start.5
  51.4 0.0 copy-start.6
  51.4 0.0 copy-start.8
  51.4 0.0 copy-start.9
  51.5 1.7 %own_rows.1 = (f32[384,768]{1,0:T(8,128)S(1)}, f32[192,512]{1,0:T(8,128)S(1)}) custom-call(f32[272,768]{1,0:T(8,128)S(1)} %get-tuple-element.16.own_ref, bf16[2,384,272]{2,1,0:T(8,128)(2,1)S(1)} %copy-done.10, bf16[2,384,256]{2,1,0:T(8,128)(2,1)S(1)} %copy-done.1, bf16[2,256,256]{2,1,0:T(8,128)(2,1)S(1)} %copy-done.2, bf16[2,192,192]{2,1,0:T(8,128)(2,1)S(1)} %copy-done.11), custom_call_target="tpu_custom_call" | custom-call | flops 4800000000 | bytes 20000000 | tf_op jit(solution)/shard_map/own_rows/pallas_call | solution.py:611
  53.2 0.2 collective-permute-done.3.above_ref
  53.4 0.5 collective-permute-done.2.below_ref
  53.9 0.0 copy-done.3
  53.9 0.0 copy-done.4
  53.9 0.0 copy-done.5
  53.9 0.0 copy-done.6
  53.9 0.0 copy-done.8
  53.9 0.0 copy-done.9
  53.9 2.3 %levels.1 = (f32[128,256]{1,0:T(8,128)}, f32[64,128]{1,0:T(8,128)}, f32[32,64]{1,0:T(8,128)}, f32[16,32]{1,0:T(8,128)}, f32[16,32]{1,0:T(8,128)}) custom-call(f32[384,768]{1,0:T(8,128)S(1)} %get-tuple-element.17.part_ref, f32[192,512]{1,0:T(8,128)S(1)} %get-tuple-element.18.second_ref, f32[256,128]{1,0:T(8,128)S(1)} %collective-permute-done.2.below_ref, ...), custom_call_target="tpu_custom_call" | custom-call | tf_op jit(solution)/shard_map/levels/pallas_call | solution.py:704
Async XLA Ops:
  39.7 1.6 %copy-start.1 = (bf16[2,384,256]{2,1,0:T(8,128)(2,1)S(1)}, bf16[2,384,256]{2,1,0:T(8,128)(2,1)}, u32[]{:S(2)}) copy-start(bf16[2,384,256]{2,1,0:T(8,128)(2,1)} %constant.29.clone.inner_ref) | copy-start | bytes 1179652
  40.7 4.5 %collective-permute-start = (f32[176,128]{1,0:T(8,128)S(1)}, f32[176,128]{1,0:T(8,128)S(1)}, u32[]{:S(2)}, u32[]{:S(2)}) collective-permute-start(f32[176,128]{1,0:T(8,128)S(1)} %get-tuple-element.15), channel_id=1, source_target_pairs={{0,7},{1,0},{2,1},{3,2},{4,3},{5,4},{6,5},{7,6},{8,15},{9,8},{10,9... | collective-permute-start | bytes 270344 | tf_op jit(solution)/shard_map/ppermute | solution.py:715
  40.8 4.5 %copy-start = (bf16[2,256,512]{2,1,0:T(8,128)(2,1)S(1)}, bf16[2,256,512]{2,1,0:T(8,128)(2,1)}, u32[]{:S(2)}) copy-start(bf16[2,256,512]{2,1,0:T(8,128)(2,1)} %constant.30.clone.outer_ref) | copy-start | bytes 1572868
  40.8 4.5 %copy-start.7 = (bf16[2,64,80]{2,1,0:T(8,128)(2,1)S(1)}, bf16[2,64,80]{2,1,0:T(8,128)(2,1)}, u32[]{:S(2)}) copy-start(bf16[2,64,80]{2,1,0:T(8,128)(2,1)} %constant.25.clone.below_ref) | copy-start | bytes 61444
  40.8 4.4 %collective-permute-start.1 = (f32[40,128]{1,0:T(8,128)S(1)}, f32[40,128]{1,0:T(8,128)S(1)}, u32[]{:S(2)}, u32[]{:S(2)}) collective-permute-start(f32[40,128]{1,0:T(8,128)S(1)} %get-tuple-element.14.to_right_ref), channel_id=1, source_target_pairs={{0,1},{1,2},{2,3},{3,4},{4,5},{5,6},{6,7},{7,0},{8,9},{9,10},{10,1... | collective-permute-start | bytes 61448 | tf_op jit(solution)/shard_map/ppermute | solution.py:715
  43.4 8.0 %copy-start.2 = (bf16[2,256,256]{2,1,0:T(8,128)(2,1)S(1)}, bf16[2,256,256]{2,1,0:T(8,128)(2,1)}, u32[]{:S(2)}) copy-start(bf16[2,256,256]{2,1,0:T(8,128)(2,1)} %constant.26.clone.rest_ref.refs_0_) | copy-start | bytes 786436
  43.4 8.0 %copy-start.10 = (bf16[2,384,272]{2,1,0:T(8,128)(2,1)S(1)}, bf16[2,384,272]{2,1,0:T(8,128)(2,1)}, u32[]{:S(2)}) copy-start(bf16[2,384,272]{2,1,0:T(8,128)(2,1)} %constant.31.clone.table_ref) | copy-start | bytes 1253380
  43.4 8.0 %copy-start.11 = (bf16[2,192,192]{2,1,0:T(8,128)(2,1)S(1)}, bf16[2,192,192]{2,1,0:T(8,128)(2,1)}, u32[]{:S(2)}) copy-start(bf16[2,192,192]{2,1,0:T(8,128)(2,1)} %constant.32.clone.rows_ref) | copy-start | bytes 442372
  46.0 7.4 %collective-permute-start.3 = (f32[88,128]{1,0:T(8,128)S(1)}, f32[88,128]{1,0:T(8,128)S(1)}, u32[]{:S(2)}, u32[]{:S(2)}) collective-permute-start(f32[88,128]{1,0:T(8,128)S(1)} %get-tuple-element.20), channel_id=1, source_target_pairs={{0,8},{8,16},{16,24},{24,32},{32,40},{40,48},{48,56},{56,64},{64,7... | collective-permute-start | bytes 135176 | tf_op jit(solution)/shard_map/ppermute | solution.py:715
  46.8 7.1 %collective-permute-start.2 = (f32[256,128]{1,0:T(8,128)S(1)}, f32[256,128]{1,0:T(8,128)S(1)}, u32[]{:S(2)}, u32[]{:S(2)}) collective-permute-start(f32[256,128]{1,0:T(8,128)S(1)} %get-tuple-element.19), channel_id=1, source_target_pairs={{0,120},{8,0},{16,8},{24,16},{32,24},{40,32},{48,40},{56,48},{64,5... | collective-permute-start | bytes 393224 | tf_op jit(solution)/shard_map/ppermute | solution.py:715
  51.4 2.5 %copy-start.3 = (bf16[2,256,256]{2,1,0:T(8,128)(2,1)S(1)}, bf16[2,256,256]{2,1,0:T(8,128)(2,1)}, u32[]{:S(2)}) copy-start(bf16[2,256,256]{2,1,0:T(8,128)(2,1)} %constant.27.clone.refs_1_) | copy-start | bytes 786436
  51.4 2.5 %copy-start.4 = (bf16[2,128,256]{2,1,0:T(8,128)(2,1)S(1)}, bf16[2,128,256]{2,1,0:T(8,128)(2,1)}, u32[]{:S(2)}) copy-start(bf16[2,128,256]{2,1,0:T(8,128)(2,1)} %constant.28.clone.refs_2_) | copy-start | bytes 393220
  51.4 2.5 %copy-start.5 = (bf16[2,192,64]{2,1,0:T(8,128)(2,1)S(1)}, bf16[2,192,64]{2,1,0:T(8,128)(2,1)}, u32[]{:S(2)}) copy-start(bf16[2,192,64]{2,1,0:T(8,128)(2,1)} %constant.35.clone.added_ref) | copy-start | bytes 147460
  51.4 2.5 %copy-start.6 = (bf16[2,96,96]{2,1,0:T(8,128)(2,1)S(1)}, bf16[2,96,96]{2,1,0:T(8,128)(2,1)}, u32[]{:S(2)}) copy-start(bf16[2,96,96]{2,1,0:T(8,128)(2,1)} %constant.33.clone.refs_3_) | copy-start | bytes 110596
  51.4 2.5 %copy-start.8 = (bf16[2,48,48]{2,1,0:T(8,128)(2,1)S(1)}, bf16[2,48,48]{2,1,0:T(8,128)(2,1)}, u32[]{:S(2)}) copy-start(bf16[2,48,48]{2,1,0:T(8,128)(2,1)} %constant.34.clone.refs_4_) | copy-start | bytes 27652
  51.4 2.5 %copy-start.9 = (bf16[2,32,24]{2,1,0:T(8,128)(2,1)S(1)}, bf16[2,32,24]{2,1,0:T(8,128)(2,1)}, u32[]{:S(2)}) copy-start(bf16[2,32,24]{2,1,0:T(8,128)(2,1)} %constant.24.clone.table_ref) | copy-start | bytes 9220
